TPU v7x, 256 devices: a whole 4x4x8 slice. The times are simulated.
256 devices in a mesh: dom: 16 (over x, y_lo, core), space: 16 (over y_hi, z).
Axes of the slice: x: 4, y: 4 (y_hi: 2, y_lo: 2; y = y_hi * 2 + y_lo), z: 8, core: 2. Of those that a mesh axis runs over, the one named last changes fastest.
Arguments:
- ancestor: int32 [64], replicated, may hold values from 0 to 63, as said below
- state: float32 [64, 3, 256, 2048], P('dom', None, 'space'), may hold values from -6 to 6
- jitter: float32 [64, 3, 256, 2048], P('dom', None, 'space'), may hold values from -4 to 4
- depth: float32 [256, 2048], P('space'), may hold values from 0.5 to 2
- coriolis: float32 [256, 2048], P('space'), may hold values from -1 to 1
- drag: float32 [256, 2048], P('space'), may hold values from 0.1 to 1
Outputs:
- forecast: float32 [64, 3, 256, 2048], P('dom', None, 'space')
Inputs may be any that keep to these rules, and one draw needn't show every extreme that they name: In-place replacement: every particle either keeps its slot (ancestor[j] = j) or is replaced by a survivor p with ancestor[p] = p and p != j; a survivor is the ancestor of at most two new particles. Among the particles k*4 to k*4 + 3, at most 2 are ancestors of a particle other than themselves, and in every draw some such block has exactly 2.
All inputs are finite; a program needn't handle non-finite values.
Results may differ from a plain program's by a relative error of at most 0.00007.
Values sent between devices are 32-bit elements; how exact they have to be, the bound alone decides.
No kernel may reach another device: no remote copies, remote signals or barrier semaphores. Data moves between devices by JAX's collectives and lax.ppermute only.
A program may use at most 128 MiB of HBM per device.

v0:
```python
import jax
import jax.numpy as jnp
from jax import lax
from jax.sharding import PartitionSpec as P

STEPS = 4


time_step = 0.3


def extended(cells, sides, width):
    for axis, dim in sides:
        count = lax.axis_size(axis)
        head = lax.slice_in_dim(cells, 0, width, axis=dim)
        tail = lax.slice_in_dim(cells, cells.shape[dim] - width, cells.shape[dim], axis=dim)
        cells = jnp.concatenate(
            [
                lax.ppermute(tail, axis, [(i, (i + 1) % count) for i in range(count)]),
                cells,
                lax.ppermute(head, axis, [((i + 1) % count, i) for i in range(count)]),
            ],
            axis=dim,
        )
    return cells


def diff_zero(values):
    padded = jnp.pad(values, [(0, 0)] * (values.ndim - 1) + [(1, 1)])
    return 0.5 * (padded[..., 2:] - padded[..., :-2])


def diff_edge(values):
    padded = jnp.pad(values, [(0, 0)] * (values.ndim - 1) + [(1, 1)], mode="edge")
    return 0.5 * (padded[..., 2:] - padded[..., :-2])


def local(ancestor, state, jitter, depth, coriolis, drag):
    members = state.shape[0]
    myself = lax.axis_index("dom")
    wanted = lax.dynamic_slice_in_dim(ancestor, myself * members, members)
    piece = lax.all_gather(state, "dom", axis=0, tiled=True)
    take_count = piece.shape[0]
    select = (wanted[:, None] == jnp.arange(take_count, dtype=jnp.int32)[None, :]).astype(
        jnp.float32
    )
    copied = jnp.einsum("jk,kfrc->jfrc", select, piece, precision=lax.Precision.HIGHEST)
    fields = copied + jitter
    height, across, along = (fields[:, 0], fields[:, 1], fields[:, 2])
    for count in range(STEPS):
        flux = depth * along
        padded = extended(flux, (("space", 1),), 1)
        height_new = height - time_step * (
            diff_zero(depth * across) + 0.5 * (padded[:, 2:] - padded[:, :-2])
        )
        rimmed = extended(height_new, (("space", 1),), 1)
        across_new = (across + time_step * (coriolis * along - diff_edge(height_new))) / (
            1.0 + time_step * drag
        )
        along_new = (
            along + time_step * (-coriolis * across - 0.5 * (rimmed[:, 2:] - rimmed[:, :-2]))
        ) / (1.0 + time_step * drag)
        height, across, along = (height_new, across_new, along_new)
    return jnp.stack([height, across, along], axis=1)


def solution(mesh):
    placed = (
        P(),
        P("dom", None, "space", None),
        P("dom", None, "space", None),
        P("space", None),
        P("space", None),
        P("space", None),
    )
    return jax.shard_map(
        local, mesh=mesh, in_specs=placed, out_specs=P("dom", None, "space", None), check_vma=False
    )
```

profile of v0, /device:TPU:2, one launch (start us, length us, event | category | flops | bytes accessed | tf_op | source)
XLA Modules:
  0.0 258.6 jit_solution(7539135098943396371)
XLA Ops:
  6.5 0.7 all-gather.2.cloned.1.call-update
  7.4 138.2 %all-gather.2.cloned.1.call-done = f32[64,3,16,2048]{3,2,1,0:T(8,128)} async-done(((f32[4,3,16,2048]{3,2,1,0:T(8,128)}), f32[64,3,16,2048]{3,2,1,0:T(8,128)}) %all-gather.2.cloned.1.call-update) | async-done | bytes 25165840 | tf_op jit(solution)/shard_map/all_gather | solution.py:42
  145.6 29.7 %fusion.2 = f32[4,3,16,2048]{3,0,2,1:T(4,128)S(1)} fusion(f32[64,3,16,2048]{3,2,1,0:T(8,128)} %all-gather.2.cloned.1.call-done, f32[4,3,16,2048]{3,2,1,0:T(8,128)S(1)} %copy-done.2, s32[4]{0:T(128)S(1)} %dynamic_slice.3), kind=kOutput, calls=%fused_computation.2 | convolution fusion | flops 302383360 | bytes 28311568 | tf_op jit(solution)/shard_map/jk,kfrc->jfrc/dot_general | solution.py:47
  175.5 5.8 %collective-permute-start = (f32[4,1,2048]{2,0,1:T(4,128)S(1)}, f32[4,1,2048]{2,0,1:T(4,128)S(1)}, u32[]{:S(2)}, u32[]{:S(2)}) collective-permute-start(f32[4,1,2048]{2,0,1:T(4,128)S(1)} %get-tuple-element.49), channel_id=1, source_target_pairs={{1,0},{2,1},{3,2},{4,3},{5,4},{6,5},{7,6},{8,7},{9,8},{10,9},{11,1... | collective-permute-start | bytes 98312 | tf_op jit(solution)/shard_map/ppermute | solution.py:21
  181.4 1.5 collective-permute-done
  183.0 5.9 %collective-permute-done.1 = f32[4,1,2048]{2,0,1:T(4,128)S(1)} collective-permute-done((f32[4,1,2048]{2,0,1:T(4,128)S(1)}, f32[4,1,2048]{2,0,1:T(4,128)S(1)}, u32[]{:S(2)}, u32[]{:S(2)}) %collective-permute-start.1) | collective-permute-done | bytes 32800 | tf_op jit(solution)/shard_map/ppermute | solution.py:19
  189.6 2.0 collective-permute-start.3
  191.7 1.8 collective-permute-done.2
  193.5 3.7 %collective-permute-done.3 = f32[4,1,2048]{2,0,1:T(4,128)S(1)} collective-permute-done((f32[4,1,2048]{2,0,1:T(4,128)S(1)}, f32[4,1,2048]{2,0,1:T(4,128)S(1)}, u32[]{:S(2)}, u32[]{:S(2)}) %collective-permute-start.3) | collective-permute-done | bytes 32800 | tf_op jit(solution)/shard_map/ppermute | solution.py:19
  197.2 1.0 broadcast_multiply_fusion.5
  198.3 2.0 collective-permute-start.5
  200.3 1.9 collective-permute-done.4
  202.2 3.7 %collective-permute-done.5 = f32[4,1,2048]{2,0,1:T(4,128)S(1)} collective-permute-done((f32[4,1,2048]{2,0,1:T(4,128)S(1)}, f32[4,1,2048]{2,0,1:T(4,128)S(1)}, u32[]{:S(2)}, u32[]{:S(2)}) %collective-permute-start.5) | collective-permute-done | bytes 32800 | tf_op jit(solution)/shard_map/ppermute | solution.py:19
  206.6 2.0 collective-permute-start.7
  208.7 1.8 collective-permute-done.6
  210.5 3.7 %collective-permute-done.7 = f32[4,1,2048]{2,0,1:T(4,128)S(1)} collective-permute-done((f32[4,1,2048]{2,0,1:T(4,128)S(1)}, f32[4,1,2048]{2,0,1:T(4,128)S(1)}, u32[]{:S(2)}, u32[]{:S(2)}) %collective-permute-start.7) | collective-permute-done | bytes 32800 | tf_op jit(solution)/shard_map/ppermute | solution.py:19
  214.2 1.0 broadcast_multiply_fusion.3
  215.3 2.0 collective-permute-start.9
  217.3 1.9 collective-permute-done.8
  219.2 3.7 %collective-permute-done.9 = f32[4,1,2048]{2,0,1:T(4,128)S(1)} collective-permute-done((f32[4,1,2048]{2,0,1:T(4,128)S(1)}, f32[4,1,2048]{2,0,1:T(4,128)S(1)}, u32[]{:S(2)}, u32[]{:S(2)}) %collective-permute-start.9) | collective-permute-done | bytes 32800 | tf_op jit(solution)/shard_map/ppermute | solution.py:19
  223.9 2.0 collective-permute-start.11
  225.9 1.8 collective-permute-done.10
  227.8 3.7 %collective-permute-done.11 = f32[4,1,2048]{2,0,1:T(4,128)S(1)} collective-permute-done((f32[4,1,2048]{2,0,1:T(4,128)S(1)}, f32[4,1,2048]{2,0,1:T(4,128)S(1)}, u32[]{:S(2)}, u32[]{:S(2)}) %collective-permute-start.11) | collective-permute-done | bytes 32800 | tf_op jit(solution)/shard_map/ppermute | solution.py:19
  231.5 1.0 broadcast_multiply_fusion.1
  232.5 2.0 collective-permute-start.13
  234.5 1.9 collective-permute-done.12
  236.4 3.7 %collective-permute-done.13 = f32[4,1,2048]{2,0,1:T(4,128)S(1)} collective-permute-done((f32[4,1,2048]{2,0,1:T(4,128)S(1)}, f32[4,1,2048]{2,0,1:T(4,128)S(1)}, u32[]{:S(2)}, u32[]{:S(2)}) %collective-permute-start.13) | collective-permute-done | bytes 32800 | tf_op jit(solution)/shard_map/ppermute | solution.py:19
  240.9 2.0 collective-permute-start.15
  243.0 1.8 collective-permute-done.14
  244.8 3.7 %collective-permute-done.15 = f32[4,1,2048]{2,0,1:T(4,128)S(1)} collective-permute-done((f32[4,1,2048]{2,0,1:T(4,128)S(1)}, f32[4,1,2048]{2,0,1:T(4,128)S(1)}, u32[]{:S(2)}, u32[]{:S(2)}) %collective-permute-start.15) | collective-permute-done | bytes 32800 | tf_op jit(solution)/shard_map/ppermute | solution.py:19
  248.5 0.8 fusion.69
  249.7 2.1 copy.12
  (40 shorter events, 4.4 us)
Async XLA Ops:
  6.5 0.7 copy-start.4
  6.5 139.0 %copy-start.2 = (f32[4,3,16,2048]{3,2,1,0:T(8,128)S(1)}, f32[4,3,16,2048]{3,2,1,0:T(8,128)}, u32[]{:S(2)}) copy-start(f32[4,3,16,2048]{3,2,1,0:T(8,128)} %param.8) | copy-start | bytes 4718596
  6.5 139.0 %all-gather.2.cloned.1.call-start = ((), (), s32[]{:S(2)}) async-start(), calls=%async_computation | async-start | bytes 26738688 | tf_op jit(solution)/shard_map/all_gather | solution.py:42
  7.4 167.9 %copy-start.1 = (f32[16,2048]{1,0:T(8,128)S(1)}, f32[16,2048]{1,0:T(8,128)}, u32[]{:S(2)}) copy-start(f32[16,2048]{1,0:T(8,128)} %param.9) | copy-start | bytes 393220
  175.3 6.1 %copy-start.3 = (f32[16,2048]{1,0:T(8,128)S(1)}, f32[16,2048]{1,0:T(8,128)}, u32[]{:S(2)}) copy-start(f32[16,2048]{1,0:T(8,128)} %param.11) | copy-start | bytes 393220
  175.3 6.1 %copy-start = (f32[16,2048]{1,0:T(8,128)S(1)}, f32[16,2048]{1,0:T(8,128)}, u32[]{:S(2)}) copy-start(f32[16,2048]{1,0:T(8,128)} %param.10) | copy-start | bytes 393220
  175.5 7.4 %collective-permute-start = (f32[4,1,2048]{2,0,1:T(4,128)S(1)}, f32[4,1,2048]{2,0,1:T(4,128)S(1)}, u32[]{:S(2)}, u32[]{:S(2)}) collective-permute-start(f32[4,1,2048]{2,0,1:T(4,128)S(1)} %get-tuple-element.49), channel_id=1, source_target_pairs={{1,0},{2,1},{3,2},{4,3},{5,4},{6,5},{7,6},{8,7},{9,8},{10,9},{11,1... | collective-permute-start | bytes 98312 | tf_op jit(solution)/shard_map/ppermute | solution.py:21
  181.4 7.5 %collective-permute-start.1 = (f32[4,1,2048]{2,0,1:T(4,128)S(1)}, f32[4,1,2048]{2,0,1:T(4,128)S(1)}, u32[]{:S(2)}, u32[]{:S(2)}) collective-permute-start(f32[4,1,2048]{2,0,1:T(4,128)S(1)} %get-tuple-element.50), channel_id=1, source_target_pairs={{0,1},{1,2},{2,3},{3,4},{4,5},{5,6},{6,7},{7,8},{8,9},{9,10},{10,1... | collective-permute-start | bytes 98312 | tf_op jit(solution)/shard_map/ppermute | solution.py:19
  189.5 4.0 %collective-permute-start.2 = (f32[4,1,2048]{2,0,1:T(4,128)S(1)}, f32[4,1,2048]{2,0,1:T(4,128)S(1)}, u32[]{:S(2)}, u32[]{:S(2)}) collective-permute-start(f32[4,1,2048]{2,0,1:T(4,128)S(1)} %get-tuple-element.47), channel_id=1, source_target_pairs={{1,0},{2,1},{3,2},{4,3},{5,4},{6,5},{7,6},{8,7},{9,8},{10,9},{11,1... | collective-permute-start | bytes 98312 | tf_op jit(solution)/shard_map/ppermute | solution.py:21
  189.6 7.6 %collective-permute-start.3 = (f32[4,1,2048]{2,0,1:T(4,128)S(1)}, f32[4,1,2048]{2,0,1:T(4,128)S(1)}, u32[]{:S(2)}, u32[]{:S(2)}) collective-permute-start(f32[4,1,2048]{2,0,1:T(4,128)S(1)} %get-tuple-element.48), channel_id=1, source_target_pairs={{0,1},{1,2},{2,3},{3,4},{4,5},{5,6},{6,7},{7,8},{8,9},{9,10},{10,1... | collective-permute-start | bytes 98312 | tf_op jit(solution)/shard_map/ppermute | solution.py:19
  198.2 4.0 %collective-permute-start.4 = (f32[4,1,2048]{2,0,1:T(4,128)S(1)}, f32[4,1,2048]{2,0,1:T(4,128)S(1)}, u32[]{:S(2)}, u32[]{:S(2)}) collective-permute-start(f32[4,1,2048]{2,0,1:T(4,128)S(1)} %get-tuple-element.45), channel_id=1, source_target_pairs={{1,0},{2,1},{3,2},{4,3},{5,4},{6,5},{7,6},{8,7},{9,8},{10,9},{11,1... | collective-permute-start | bytes 98312 | tf_op jit(solution)/shard_map/ppermute | solution.py:21
  198.3 7.6 %collective-permute-start.5 = (f32[4,1,2048]{2,0,1:T(4,128)S(1)}, f32[4,1,2048]{2,0,1:T(4,128)S(1)}, u32[]{:S(2)}, u32[]{:S(2)}) collective-permute-start(f32[4,1,2048]{2,0,1:T(4,128)S(1)} %get-tuple-element.46), channel_id=1, source_target_pairs={{0,1},{1,2},{2,3},{3,4},{4,5},{5,6},{6,7},{7,8},{8,9},{9,10},{10,1... | collective-permute-start | bytes 98312 | tf_op jit(solution)/shard_map/ppermute | solution.py:19
  206.5 4.0 %collective-permute-start.6 = (f32[4,1,2048]{2,0,1:T(4,128)S(1)}, f32[4,1,2048]{2,0,1:T(4,128)S(1)}, u32[]{:S(2)}, u32[]{:S(2)}) collective-permute-start(f32[4,1,2048]{2,0,1:T(4,128)S(1)} %get-tuple-element.41), channel_id=1, source_target_pairs={{1,0},{2,1},{3,2},{4,3},{5,4},{6,5},{7,6},{8,7},{9,8},{10,9},{11,1... | collective-permute-start | bytes 98312 | tf_op jit(solution)/shard_map/ppermute | solution.py:21
  206.6 7.6 %collective-permute-start.7 = (f32[4,1,2048]{2,0,1:T(4,128)S(1)}, f32[4,1,2048]{2,0,1:T(4,128)S(1)}, u32[]{:S(2)}, u32[]{:S(2)}) collective-permute-start(f32[4,1,2048]{2,0,1:T(4,128)S(1)} %get-tuple-element.42), channel_id=1, source_target_pairs={{0,1},{1,2},{2,3},{3,4},{4,5},{5,6},{6,7},{7,8},{8,9},{9,10},{10,1... | collective-permute-start | bytes 98312 | tf_op jit(solution)/shard_map/ppermute | solution.py:19
  215.2 4.0 %collective-permute-start.8 = (f32[4,1,2048]{2,0,1:T(4,128)S(1)}, f32[4,1,2048]{2,0,1:T(4,128)S(1)}, u32[]{:S(2)}, u32[]{:S(2)}) collective-permute-start(f32[4,1,2048]{2,0,1:T(4,128)S(1)} %get-tuple-element.39), channel_id=1, source_target_pairs={{1,0},{2,1},{3,2},{4,3},{5,4},{6,5},{7,6},{8,7},{9,8},{10,9},{11,1... | collective-permute-start | bytes 98312 | tf_op jit(solution)/shard_map/ppermute | solution.py:21
  215.3 7.6 %collective-permute-start.9 = (f32[4,1,2048]{2,0,1:T(4,128)S(1)}, f32[4,1,2048]{2,0,1:T(4,128)S(1)}, u32[]{:S(2)}, u32[]{:S(2)}) collective-permute-start(f32[4,1,2048]{2,0,1:T(4,128)S(1)} %get-tuple-element.40), channel_id=1, source_target_pairs={{0,1},{1,2},{2,3},{3,4},{4,5},{5,6},{6,7},{7,8},{8,9},{9,10},{10,1... | collective-permute-start | bytes 98312 | tf_op jit(solution)/shard_map/ppermute | solution.py:19
  223.5 4.2 %collective-permute-start.10 = (f32[4,1,2048]{2,0,1:T(4,128)S(1)}, f32[4,1,2048]{2,0,1:T(4,128)S(1)}, u32[]{:S(2)}, u32[]{:S(2)}) collective-permute-start(f32[4,1,2048]{2,0,1:T(4,128)S(1)} %get-tuple-element.35), channel_id=1, source_target_pairs={{1,0},{2,1},{3,2},{4,3},{5,4},{6,5},{7,6},{8,7},{9,8},{10,9},{11,1... | collective-permute-start | bytes 98312 | tf_op jit(solution)/shard_map/ppermute | solution.py:21
  223.9 7.6 %collective-permute-start.11 = (f32[4,1,2048]{2,0,1:T(4,128)S(1)}, f32[4,1,2048]{2,0,1:T(4,128)S(1)}, u32[]{:S(2)}, u32[]{:S(2)}) collective-permute-start(f32[4,1,2048]{2,0,1:T(4,128)S(1)} %get-tuple-element.36), channel_id=1, source_target_pairs={{0,1},{1,2},{2,3},{3,4},{4,5},{5,6},{6,7},{7,8},{8,9},{9,10},{10,1... | collective-permute-start | bytes 98312 | tf_op jit(solution)/shard_map/ppermute | solution.py:19
  232.4 4.0 %collective-permute-start.12 = (f32[4,1,2048]{2,0,1:T(4,128)S(1)}, f32[4,1,2048]{2,0,1:T(4,128)S(1)}, u32[]{:S(2)}, u32[]{:S(2)}) collective-permute-start(f32[4,1,2048]{2,0,1:T(4,128)S(1)} %get-tuple-element.33), channel_id=1, source_target_pairs={{1,0},{2,1},{3,2},{4,3},{5,4},{6,5},{7,6},{8,7},{9,8},{10,9},{11,1... | collective-permute-start | bytes 98312 | tf_op jit(solution)/shard_map/ppermute | solution.py:21
  232.5 7.6 %collective-permute-start.13 = (f32[4,1,2048]{2,0,1:T(4,128)S(1)}, f32[4,1,2048]{2,0,1:T(4,128)S(1)}, u32[]{:S(2)}, u32[]{:S(2)}) collective-permute-start(f32[4,1,2048]{2,0,1:T(4,128)S(1)} %get-tuple-element.34), channel_id=1, source_target_pairs={{0,1},{1,2},{2,3},{3,4},{4,5},{5,6},{6,7},{7,8},{8,9},{9,10},{10,1... | collective-permute-start | bytes 98312 | tf_op jit(solution)/shard_map/ppermute | solution.py:19
  240.8 4.0 %collective-permute-start.14 = (f32[4,1,2048]{2,0,1:T(4,128)S(1)}, f32[4,1,2048]{2,0,1:T(4,128)S(1)}, u32[]{:S(2)}, u32[]{:S(2)}) collective-permute-start(f32[4,1,2048]{2,0,1:T(4,128)S(1)} %get-tuple-element.29), channel_id=1, source_target_pairs={{1,0},{2,1},{3,2},{4,3},{5,4},{6,5},{7,6},{8,7},{9,8},{10,9},{11,1... | collective-permute-start | bytes 98312 | tf_op jit(solution)/shard_map/ppermute | solution.py:21
  240.9 7.6 %collective-permute-start.15 = (f32[4,1,2048]{2,0,1:T(4,128)S(1)}, f32[4,1,2048]{2,0,1:T(4,128)S(1)}, u32[]{:S(2)}, u32[]{:S(2)}) collective-permute-start(f32[4,1,2048]{2,0,1:T(4,128)S(1)} %get-tuple-element.30), channel_id=1, source_target_pairs={{0,1},{1,2},{2,3},{3,4},{4,5},{5,6},{6,7},{7,8},{8,9},{9,10},{10,1... | collective-permute-start | bytes 98312 | tf_op jit(solution)/shard_map/ppermute | solution.py:19
Sparse Core Ops, SparseCore 0:
  9.2 136.3 all-gather.1
where the time goes:
time: 259 us
  waiting for transfers between devices  185 us (71%)
  matrix products  29.7 us (11%)
  starting transfers between devices  20.7 us (8%)
  between operations  13.6 us (5%)
  other arithmetic  6.78 us (3%)
    all_gather x1, waiting for transfers between devices, local(): piece = lax.all_gather(state, 'dom', axis=0, tiled=True)  138 us
    ppermute x8, waiting for transfers between devices, extended(): lax.ppermute(tail, axis, [(i, (i + 1) % count) for i in range(count)])  31.9 us
    dot_general x1, matrix products, local(): jnp.einsum('jk,kfrc->jfrc', select, piece, precision=lax.Precision.HIGHEST)  29.7 us
    ppermute x8, waiting for transfers between devices, extended(): lax.ppermute(head, axis, [((i + 1) % count, i) for i in range(count)])  14.4 us
    ppermute x8, starting transfers between devices, extended(): lax.ppermute(tail, axis, [(i, (i + 1) % count) for i in range(count)])  14.1 us
    ppermute x8, starting transfers between devices, extended(): lax.ppermute(head, axis, [((i + 1) % count, i) for i in range(count)])  6.64 us
  transfers between devices with their start and end apart: 17, of which 17 were waited for; matrix products, arithmetic and copies ran while one was open for 0% of the time, Pallas kernels for 0%

commit v1 on v0

v1 whole, which is shorter than its diff:
```python
import functools

import jax
import jax.numpy as jnp
from jax import lax
from jax.experimental import pallas as pl
from jax.experimental.pallas import tpu as pltpu
from jax.sharding import PartitionSpec as P

STEPS = 4
CAP = 2
DT = 0.3
LANES = 128
HALO = 8
CHUNKS = ((0, 2), (2, 4))

VM = pl.BlockSpec(memory_space=pltpu.VMEM)
SM = pl.BlockSpec(memory_space=pltpu.SMEM)
ANY = pl.BlockSpec(memory_space=pl.ANY)
PARAMS = pltpu.CompilerParams(vmem_limit_bytes=24 << 20)


def pack_kernel(members, tiles, anc, state, out, sem):
    me = lax.axis_index("dom")
    bits = jnp.int32(0)
    for j in range(anc.shape[0]):
        a = anc[j]
        hit = (a != j) & (a // members == me)
        bits = bits | jnp.where(hit, jnp.left_shift(1, a % members), 0)
    first = jnp.int32(members - 1)
    for k in reversed(range(members)):
        first = jnp.where((bits >> k) & 1 == 1, k, first)
    second = jnp.int32(members - 1)
    for k in reversed(range(members)):
        second = jnp.where(((bits >> k) & 1 == 1) & (k != first), k, second)
    copies = []
    for q, p in enumerate((first, second)):
        for i in range(tiles):
            copies.append(
                pltpu.make_async_copy(
                    state.at[p, :, :, pl.ds(i * LANES, LANES)], out.at[i, q], sem.at[q * tiles + i]
                )
            )
    for c in copies:
        c.start()
    for c in copies:
        c.wait()


def pick_kernel(members, low, high, table, got, out):
    for d in range(out.shape[0]):
        for k in range(low, high):
            at = table[d * members + k]
            out[d, k - low] = got[at]


def prep_kernel(low, high, kept, routed, state, jitter, fields, top, bottom):
    tiles = routed.shape[0]
    for k in range(high - low):
        mine = kept[low + k] == 1
        for i in range(tiles):
            cols = slice(i * LANES, (i + 1) * LANES)
            value = jnp.where(mine, state[low + k, :, :, cols], routed[i, k]) + jitter[low + k, :, :, cols]
            fields[k, :, :, cols] = value
            top[k, :, :, cols] = value[:, :HALO]
            bottom[k, :, :, cols] = value[:, HALO:]


def step_kernel(low, high, fields, above, below, coef, *rest):
    out, eta, u, v = rest[-4:]
    rows, width = eta.shape
    own = fields.shape[2]
    tiles = width // LANES
    lane = lax.broadcasted_iota(jnp.int32, (rows, LANES), 1)
    first = lane == 0
    last = lane == LANES - 1
    half = 0.5 * DT

    def cols(i):
        return slice(i * LANES, (i + 1) * LANES)

    def left(x):
        return pltpu.roll(x, 1, 1)

    def right(x):
        return pltpu.roll(x, LANES - 1, 1)

    def row_diff(x):
        return pltpu.roll(x, rows - 1, 0) - pltpu.roll(x, 1, 0)

    def particle(k, carry):
        for f, ref in enumerate((eta, u, v)):
            ref[0:HALO, :] = above[k, f]
            ref[HALO : HALO + own, :] = fields[k, f]
            ref[HALO + own :, :] = below[k, f]

        def step(n, carry):
            zero = jnp.zeros((rows, LANES), jnp.float32)

            def load(i):
                uu = u[:, cols(i)]
                vv = v[:, cols(i)]
                d = coef[0, :, cols(i)]
                du = d * uu
                return uu, vv, d * vv, left(du), right(du)

            def finish(i, held, eta_new, eta_left, eta_right):
                uu, vv = held
                c = coef[1, :, cols(i)]
                r = coef[2, :, cols(i)]
                rh = half * r
                u[:, cols(i)] = r * (uu + c * vv) - rh * (eta_right - eta_left)
                v[:, cols(i)] = r * (vv - c * uu) - rh * row_diff(eta_new)

            ahead = load(0)
            shifted_before = zero
            before = None
            for i in range(tiles):
                uu, vv, dv, du_l, du_r = ahead
                if i + 1 < tiles:
                    ahead = load(i + 1)
                    du_next = ahead[4]
                else:
                    du_next = zero
                du_right = jnp.where(last, du_next, du_r)
                du_left = jnp.where(first, shifted_before, du_l)
                shifted_before = du_l
                eta_new = eta[:, cols(i)] - ((du_right - du_left) + row_diff(dv))
                eta[:, cols(i)] = eta_new
                e_l, e_r = left(eta_new), right(eta_new)
                if before is None:
                    e_left = jnp.where(first, eta_new, e_l)
                else:
                    b_i, b_held, b_new, b_left, b_l, b_r = before
                    finish(b_i, b_held, b_new, b_left, jnp.where(last, e_r, b_r))
                    e_left = jnp.where(first, b_l, e_l)
                before = (i, (uu, vv), eta_new, e_left, e_l, e_r)
            b_i, b_held, b_new, b_left, b_l, b_r = before
            finish(b_i, b_held, b_new, b_left, jnp.where(last, b_new, b_r))
            return carry

        lax.fori_loop(0, STEPS, step, 0)
        for f, ref in enumerate((eta, u, v)):
            out[k, f] = ref[HALO : HALO + own, :]
        return carry

    lax.fori_loop(0, high - low, particle, 0)


def local(ancestor, state, jitter, depth, coriolis, drag):
    members, kinds, rows, width = state.shape
    tiles = width // LANES
    blocks = lax.axis_size("dom")
    count = lax.axis_size("space")
    down = [(i, (i + 1) % count) for i in range(count)]
    up = [((i + 1) % count, i) for i in range(count)]
    me = lax.axis_index("dom")

    packed = pl.pallas_call(
        functools.partial(pack_kernel, members, tiles),
        in_specs=[SM, ANY],
        out_specs=ANY,
        out_shape=jax.ShapeDtypeStruct((tiles, CAP, kinds, rows, LANES), jnp.float32),
        scratch_shapes=[pltpu.SemaphoreType.DMA((CAP * tiles,))],
        compiler_params=PARAMS,
        name="pack",
    )(ancestor, state)
    pieces = lax.all_to_all(packed, "dom", 0, 0, tiled=True)
    pieces = pieces.reshape(blocks * CAP, kinds, rows, LANES)

    slot = jnp.arange(ancestor.shape[0], dtype=jnp.int32)
    moved = ancestor != slot
    donor = jnp.any((ancestor[:, None] == slot[None, :]) & moved[:, None], axis=0)
    same = (slot[:, None] // members == slot[None, :] // members) & (slot[:, None] < slot[None, :])
    rank = jnp.any(same & donor[:, None], axis=0).astype(jnp.int32)
    place = slot // members * CAP + rank
    table = jnp.sum(jnp.where(ancestor[:, None] == slot[None, :], place[None, :], 0), axis=1)
    kept = lax.dynamic_slice_in_dim(jnp.where(moved, 0, 1).astype(jnp.int32), me * members, members)

    coef = jnp.stack([(0.5 * DT) * depth, DT * coriolis, 1.0 / (1.0 + DT * drag)])
    coef = jnp.concatenate(
        [
            lax.ppermute(coef[:, rows - HALO :], "space", down),
            coef,
            lax.ppermute(coef[:, :HALO], "space", up),
        ],
        axis=1,
    )

    routed = []
    for low, high in CHUNKS:
        chosen = pl.pallas_call(
            functools.partial(pick_kernel, members, low, high),
            in_specs=[SM, VM],
            out_specs=VM,
            out_shape=jax.ShapeDtypeStruct((blocks, high - low, kinds, rows, LANES), jnp.float32),
            compiler_params=PARAMS,
            name="pick",
        )(table, pieces)
        routed.append(lax.all_to_all(chosen, "dom", 0, 0, tiled=True))

    out = None
    for (low, high), arrived in zip(CHUNKS, routed):
        size = high - low
        rim = jax.ShapeDtypeStruct((size, kinds, HALO, width), jnp.float32)
        fields, top, bottom = pl.pallas_call(
            functools.partial(prep_kernel, low, high),
            in_specs=[SM, VM, VM, VM],
            out_specs=(VM, VM, VM),
            out_shape=(jax.ShapeDtypeStruct((size, kinds, rows, width), jnp.float32), rim, rim),
            compiler_params=PARAMS,
            name="prep",
        )(kept, arrived, state, jitter)
        above = lax.ppermute(bottom, "space", down)
        below = lax.ppermute(top, "space", up)
        done = pl.BlockSpec((size, kinds, rows, width), lambda i, at=low // size: (at, 0, 0, 0))
        whole = [pl.BlockSpec(memory_space=pltpu.VMEM)] * 4
        out = pl.pallas_call(
            functools.partial(step_kernel, low, high),
            grid=(1,),
            in_specs=whole + ([] if out is None else [ANY]),
            out_specs=done,
            out_shape=jax.ShapeDtypeStruct(state.shape, jnp.float32),
            scratch_shapes=[pltpu.VMEM((rows + 2 * HALO, width), jnp.float32)] * 3,
            input_output_aliases={} if out is None else {4: 0},
            compiler_params=PARAMS,
            name="steps",
        )(fields, above, below, coef, *([] if out is None else [out]))
    return out


def solution(mesh):
    placed = (
        P(),
        P("dom", None, "space", None),
        P("dom", None, "space", None),
        P("space", None),
        P("space", None),
        P("space", None),
    )
    return jax.shard_map(
        local, mesh=mesh, in_specs=placed, out_specs=P("dom", None, "space", None), check_vma=False
    )
```

time: 259 us -> 108 us (0.42)
  the two profiles are of different devices: /device:TPU:2 before, /device:TPU:7 now
where the time goes in v1:
time: 108 us
  starting transfers between devices  56.2 us (52%)
  Pallas kernels  25.4 us (24%)
  waiting for transfers between devices  19.9 us (18%)
  local copies, waits for them, and re-layouts  4.71 us (4%)
  other arithmetic  1.56 us (1%)
    ppermute x2, starting transfers between devices, local(): below = lax.ppermute(top, 'space', up)  28.2 us
    pallas_call x2, Pallas kernels, local(): pl.pallas_call(functools.partial(step_kernel, low, high), grid=(1,), in_s...  17.6 us
    all_to_all x2, starting transfers between devices, local(): routed.append(lax.all_to_all(chosen, 'dom', 0, 0, tiled=True))  13.9 us
    all_to_all x1, waiting for transfers between devices, local(): pieces = lax.all_to_all(packed, 'dom', 0, 0, tiled=True)  10.5 us
    all_to_all x2, waiting for transfers between devices, local(): routed.append(lax.all_to_all(chosen, 'dom', 0, 0, tiled=True))  9.4 us
    ppermute x1, starting transfers between devices, local(): lax.ppermute(coef[:, :HALO], 'space', up)  6.28 us
    all_to_all x1, starting transfers between devices, local(): pieces = lax.all_to_all(packed, 'dom', 0, 0, tiled=True)  6.13 us
    unnamed x34, local copies, waits for them, and re-layouts  3.87 us
  transfers between devices with their start and end apart: 9, of which 2 were waited for; matrix products, arithmetic and copies ran while one was open for 2% of the time, Pallas kernels for 12%

profile of v1, /device:TPU:7, one launch (start us, length us, event | category | flops | bytes accessed | tf_op | source)
XLA Modules:
  0.0 108.0 jit_solution(13656677449729329098)
XLA Ops:
  0.0 1.4 %copy-done = f32[4,3,16,2048]{3,2,1,0:T(8,128)S(1)} copy-done((f32[4,3,16,2048]{3,2,1,0:T(8,128)S(1)}, f32[4,3,16,2048]{3,2,1,0:T(8,128)}, u32[]{:S(2)}) %copy-start) | copy-done | bytes 1572888
  1.4 0.7 copy-done.6
  2.1 2.1 %pack.1 = f32[16,2,3,16,128]{4,3,2,1,0:T(8,128)} custom-call(s32[64]{0:T(128)S(1)} %copy-done.6, f32[4,3,16,2048]{3,2,1,0:T(8,128)S(1)} %copy-done), custom_call_target="tpu_custom_call" | custom-call | tf_op jit(solution)/shard_map/pack/pallas_call | solution.py:159
  4.2 6.1 %all-to-all-start = ((f32[16,2,3,16,128]{4,3,2,1,0:T(8,128)}), f32[16,2,3,16,128]{4,3,2,1,0:T(8,128)S(1)}, u32[]{:S(2)}, u32[]{:S(2)}) async-start(f32[16,2,3,16,128]{4,3,2,1,0:T(8,128)} %pack.1), calls=%async_computation | async-start | bytes 1572864 | tf_op jit(solution)/shard_map/all_to_all | solution.py:168
  10.4 0.1 fusion.1
  10.5 0.1 fusion.4
  10.6 0.2 select_reduce_fusion.table
  10.8 10.5 %all-to-all-done = f32[16,2,3,16,128]{4,3,2,1,0:T(8,128)S(1)} async-done(((f32[16,2,3,16,128]{4,3,2,1,0:T(8,128)}), f32[16,2,3,16,128]{4,3,2,1,0:T(8,128)S(1)}, u32[]{:S(2)}, u32[]{:S(2)}) %all-to-all-start) | async-done | bytes 786464 | tf_op jit(solution)/shard_map/all_to_all | solution.py:168
  21.3 1.5 %pick.3 = f32[16,2,3,16,128]{4,3,2,1,0:T(8,128)} custom-call(s32[64]{0:T(128)S(1)} %select_reduce_fusion.table, f32[32,3,16,128]{3,2,1,0:T(8,128)S(1)} %bitcast.7), custom_call_target="tpu_custom_call" | custom-call | tf_op jit(solution)/shard_map/pick/pallas_call | solution.py:192
  22.8 6.9 %all-to-all-start.2 = ((f32[16,2,3,16,128]{4,3,2,1,0:T(8,128)}), f32[16,2,3,16,128]{4,3,2,1,0:T(8,128)}, u32[]{:S(2)}, u32[]{:S(2)}) async-start(f32[16,2,3,16,128]{4,3,2,1,0:T(8,128)} %pick.3), calls=%async_computation.2 | async-start | bytes 1572864 | tf_op jit(solution)/shard_map/all_to_all | solution.py:200
  29.8 0.6 pick.2
  30.4 0.0 copy-start.3
  30.5 0.9 copy-done.3
  31.3 9.4 %all-to-all-done.2.routed = f32[16,2,3,16,128]{4,3,2,1,0:T(8,128)} async-done(((f32[16,2,3,16,128]{4,3,2,1,0:T(8,128)}), f32[16,2,3,16,128]{4,3,2,1,0:T(8,128)}, u32[]{:S(2)}, u32[]{:S(2)}) %all-to-all-start.2) | async-done | bytes 786464 | tf_op jit(solution)/shard_map/all_to_all | solution.py:200
  40.7 7.0 %all-to-all-start.1 = ((f32[16,2,3,16,128]{4,3,2,1,0:T(8,128)}), f32[16,2,3,16,128]{4,3,2,1,0:T(8,128)}, u32[]{:S(2)}, u32[]{:S(2)}) async-start(f32[16,2,3,16,128]{4,3,2,1,0:T(8,128)} %copy-done.3), calls=%async_computation.1 | async-start | bytes 1572864 | tf_op jit(solution)/shard_map/all_to_all | solution.py:200
  47.8 0.8 fusion.5
  48.5 1.6 %collective-permute-start.2 = (f32[3,8,2048]{2,1,0:T(8,128)}, f32[3,8,2048]{2,1,0:T(8,128)}, u32[]{:S(2)}, u32[]{:S(2)}) collective-permute-start(f32[3,8,2048]{2,1,0:T(8,128)} %get-tuple-element.17), channel_id=1, source_target_pairs={{0,1},{1,2},{2,3},{3,4},{4,5},{5,6},{6,7},{7,8},{8,9},{9,10},{10,1... | collective-permute-start | bytes 589832 | tf_op jit(solution)/shard_map/ppermute | solution.py:183
  50.2 6.3 %collective-permute-start.3 = (f32[3,8,2048]{2,1,0:T(8,128)}, f32[3,8,2048]{2,1,0:T(8,128)}, u32[]{:S(2)}, u32[]{:S(2)}) collective-permute-start(f32[3,8,2048]{2,1,0:T(8,128)} %get-tuple-element.18), channel_id=1, source_target_pairs={{1,0},{2,1},{3,2},{4,3},{5,4},{6,5},{7,6},{8,7},{9,8},{10,9},{11,1... | collective-permute-start | bytes 589832 | tf_op jit(solution)/shard_map/ppermute | solution.py:185
  56.5 0.1 dynamic_slice.3.kept
  56.5 2.2 %prep.3 = (f32[2,3,16,2048]{3,2,1,0:T(8,128)S(1)}, f32[2,3,8,2048]{3,2,1,0:T(8,128)}, f32[2,3,8,2048]{3,2,1,0:T(8,128)}) custom-call(s32[4]{0:T(128)S(1)} %dynamic_slice.3.kept, f32[16,2,3,16,128]{4,3,2,1,0:T(8,128)} %all-to-all-done.2.routed, f32[4,3,16,2048]{3,2,1,0:T(8,128)S(1)} %copy-done.1, f32[4,3,16,2048]{3,2,1,0:T(8,128)S(1)} %copy-done.2), custom_call_target="tpu_custom_call" | custom-call | tf_op jit(solution)/shard_map/prep/pallas_call | solution.py:206
  58.7 0.9 copy-done.4
  59.6 0.0 collective-permute-start.4
  59.6 5.1 %collective-permute-start.5 = (f32[2,3,8,2048]{3,2,1,0:T(8,128)}, f32[2,3,8,2048]{3,2,1,0:T(8,128)}, u32[]{:S(2)}, u32[]{:S(2)}) collective-permute-start(f32[2,3,8,2048]{3,2,1,0:T(8,128)} %get-tuple-element.16), channel_id=1, source_target_pairs={{1,0},{2,1},{3,2},{4,3},{5,4},{6,5},{7,6},{8,7},{9,8},{10,9},{11,1... | collective-permute-start | bytes 1179656 | tf_op jit(solution)/shard_map/ppermute | solution.py:215
  64.7 1.3 %prep.2 = (f32[2,3,16,2048]{3,2,1,0:T(8,128)S(1)}, f32[2,3,8,2048]{3,2,1,0:T(8,128)S(1)}, f32[2,3,8,2048]{3,2,1,0:T(8,128)S(1)}) custom-call(s32[4]{0:T(128)S(1)} %dynamic_slice.3.kept, f32[16,2,3,16,128]{4,3,2,1,0:T(8,128)} %all-to-all-done.1.routed, f32[4,3,16,2048]{3,2,1,0:T(8,128)S(1)} %copy-done.1, f32[4,3,16,2048]{3,2,1,0:T(8,128)S(1)} %copy-done.2), custom_call_target="tpu_custom_call" | custom-call | tf_op jit(solution)/shard_map/prep/pallas_call | solution.py:206
  66.0 0.1 collective-permute-start
  66.1 0.0 collective-permute-done.2
  66.1 23.1 %collective-permute-start.1 = (f32[2,3,8,2048]{3,2,1,0:T(8,128)S(1)}, f32[2,3,8,2048]{3,2,1,0:T(8,128)S(1)}, u32[]{:S(2)}, u32[]{:S(2)}) collective-permute-start(f32[2,3,8,2048]{3,2,1,0:T(8,128)S(1)} %get-tuple-element.13), channel_id=1, source_target_pairs={{1,0},{2,1},{3,2},{4,3},{5,4},{6,5},{7,6},{8,7},{9,8},{10,9},{11,1... | collective-permute-start | bytes 1179656 | tf_op jit(solution)/shard_map/ppermute | solution.py:215
  89.3 1.1 pad_maximum_fusion.coef
  90.4 0.0 collective-permute-done.4.above
  90.4 9.3 %steps.2.rest_0_ = f32[4,3,16,2048]{3,2,1,0:T(8,128)} custom-call(f32[2,3,16,2048]{3,2,1,0:T(8,128)S(1)} %copy-done.5, f32[2,3,8,2048]{3,2,1,0:T(8,128)S(1)} %collective-permute-done.4.above, f32[2,3,8,2048]{3,2,1,0:T(8,128)} %collective-permute-done.5.below, f32[3,32,2048]{2,1,0:T(8,128)S(1)} %pad_maximum_fusion.coef), custom_call_target="tpu_custom_call" | custom-call | tf_op jit(solution)/shard_map/steps/pallas_call | solution.py:218
  99.7 0.0 collective-permute-done.above
  99.7 8.3 %steps.3 = f32[4,3,16,2048]{3,2,1,0:T(8,128)} custom-call(f32[2,3,16,2048]{3,2,1,0:T(8,128)S(1)} %get-tuple-element.11.fields, f32[2,3,8,2048]{3,2,1,0:T(8,128)S(1)} %collective-permute-done.above, f32[2,3,8,2048]{3,2,1,0:T(8,128)S(1)} %collective-permute-done.1.below, f32[3,32,2048]{2,1,0:T(8,128)S(1)} %pad_maximum_fusion.coef, ...), custom_call_target="tpu_custom_call", output_to_operand_aliasing={{}: (4, {})} | custom-call | tf_op jit(solution)/shard_map/steps/pallas_call | solution.py:218
  (40 shorter events, 0.2 us)
Async XLA Ops:
  0.0 1.4 %copy-start = (f32[4,3,16,2048]{3,2,1,0:T(8,128)S(1)}, f32[4,3,16,2048]{3,2,1,0:T(8,128)}, u32[]{:S(2)}) copy-start(f32[4,3,16,2048]{3,2,1,0:T(8,128)} %state.5) | copy-start | bytes 4718596
  1.4 0.7 copy-start.6
  2.1 8.3 %copy-start.7 = (s32[64]{0:T(128)S(1)}, s32[64]{0:T(128)}, u32[]{:S(2)}) copy-start(s32[64]{0:T(128)} %anc.1) | copy-start | bytes 772
  4.2 17.1 %all-to-all-start = ((f32[16,2,3,16,128]{4,3,2,1,0:T(8,128)}), f32[16,2,3,16,128]{4,3,2,1,0:T(8,128)S(1)}, u32[]{:S(2)}, u32[]{:S(2)}) async-start(f32[16,2,3,16,128]{4,3,2,1,0:T(8,128)} %pack.1), calls=%async_computation | async-start | bytes 1572864 | tf_op jit(solution)/shard_map/all_to_all | solution.py:168
  21.3 8.5 %copy-start.14 = (f32[16,2048]{1,0:T(8,128)S(1)}, f32[16,2048]{1,0:T(8,128)}, u32[]{:S(2)}) copy-start(f32[16,2048]{1,0:T(8,128)} %param.9) | copy-start | bytes 393220
  21.3 8.5 %copy-start.15 = (f32[16,2048]{1,0:T(8,128)S(1)}, f32[16,2048]{1,0:T(8,128)}, u32[]{:S(2)}) copy-start(f32[16,2048]{1,0:T(8,128)} %param.11) | copy-start | bytes 393220
  21.3 8.5 %copy-start.16 = (f32[16,2048]{1,0:T(8,128)S(1)}, f32[16,2048]{1,0:T(8,128)}, u32[]{:S(2)}) copy-start(f32[16,2048]{1,0:T(8,128)} %param.10) | copy-start | bytes 393220
  22.8 18.0 %all-to-all-start.2 = ((f32[16,2,3,16,128]{4,3,2,1,0:T(8,128)}), f32[16,2,3,16,128]{4,3,2,1,0:T(8,128)}, u32[]{:S(2)}, u32[]{:S(2)}) async-start(f32[16,2,3,16,128]{4,3,2,1,0:T(8,128)} %pick.3), calls=%async_computation.2 | async-start | bytes 1572864 | tf_op jit(solution)/shard_map/all_to_all | solution.py:200
  29.8 17.9 %copy-start.8 = (f32[1,16,2048]{2,1,0:T(8,128)}, f32[1,16,2048]{2,1,0:T(8,128)S(1)}, u32[]{:S(2)}) copy-start(f32[1,16,2048]{2,1,0:T(8,128)S(1)} %multiply_bitcast_fusion.1) | copy-start | bytes 393220
  29.8 17.9 %copy-start.10 = (f32[1,16,2048]{2,1,0:T(8,128)}, f32[1,16,2048]{2,1,0:T(8,128)S(1)}, u32[]{:S(2)}) copy-start(f32[1,16,2048]{2,1,0:T(8,128)S(1)} %get-tuple-element.19) | copy-start | bytes 393220
  29.8 17.9 %copy-start.12 = (f32[1,16,2048]{2,1,0:T(8,128)}, f32[1,16,2048]{2,1,0:T(8,128)S(1)}, u32[]{:S(2)}) copy-start(f32[1,16,2048]{2,1,0:T(8,128)S(1)} %get-tuple-element.20) | copy-start | bytes 393220
  30.4 0.9 copy-start.3
  31.3 25.2 %copy-start.1 = (f32[4,3,16,2048]{3,2,1,0:T(8,128)S(1)}, f32[4,3,16,2048]{3,2,1,0:T(8,128)}, u32[]{:S(2)}) copy-start(f32[4,3,16,2048]{3,2,1,0:T(8,128)} %state.5) | copy-start | bytes 4718596
  31.3 25.2 %copy-start.2 = (f32[4,3,16,2048]{3,2,1,0:T(8,128)S(1)}, f32[4,3,16,2048]{3,2,1,0:T(8,128)}, u32[]{:S(2)}) copy-start(f32[4,3,16,2048]{3,2,1,0:T(8,128)} %jitter.3) | copy-start | bytes 4718596
  40.7 23.9 %all-to-all-start.1 = ((f32[16,2,3,16,128]{4,3,2,1,0:T(8,128)}), f32[16,2,3,16,128]{4,3,2,1,0:T(8,128)}, u32[]{:S(2)}, u32[]{:S(2)}) async-start(f32[16,2,3,16,128]{4,3,2,1,0:T(8,128)} %copy-done.3), calls=%async_computation.1 | async-start | bytes 1572864 | tf_op jit(solution)/shard_map/all_to_all | solution.py:200
  48.5 17.6 %collective-permute-start.2 = (f32[3,8,2048]{2,1,0:T(8,128)}, f32[3,8,2048]{2,1,0:T(8,128)}, u32[]{:S(2)}, u32[]{:S(2)}) collective-permute-start(f32[3,8,2048]{2,1,0:T(8,128)} %get-tuple-element.17), channel_id=1, source_target_pairs={{0,1},{1,2},{2,3},{3,4},{4,5},{5,6},{6,7},{7,8},{8,9},{9,10},{10,1... | collective-permute-start | bytes 589832 | tf_op jit(solution)/shard_map/ppermute | solution.py:183
  50.2 39.1 %collective-permute-start.3 = (f32[3,8,2048]{2,1,0:T(8,128)}, f32[3,8,2048]{2,1,0:T(8,128)}, u32[]{:S(2)}, u32[]{:S(2)}) collective-permute-start(f32[3,8,2048]{2,1,0:T(8,128)} %get-tuple-element.18), channel_id=1, source_target_pairs={{1,0},{2,1},{3,2},{4,3},{5,4},{6,5},{7,6},{8,7},{9,8},{10,9},{11,1... | collective-permute-start | bytes 589832 | tf_op jit(solution)/shard_map/ppermute | solution.py:185
  58.7 0.9 copy-start.4
  59.6 30.8 %collective-permute-start.4 = (f32[2,3,8,2048]{3,2,1,0:T(8,128)}, f32[2,3,8,2048]{3,2,1,0:T(8,128)S(1)}, u32[]{:S(2)}, u32[]{:S(2)}) collective-permute-start(f32[2,3,8,2048]{3,2,1,0:T(8,128)} %get-tuple-element.15), channel_id=1, source_target_pairs={{0,1},{1,2},{2,3},{3,4},{4,5},{5,6},{6,7},{7,8},{8,9},{9,10},{10,1... | collective-permute-start | bytes 1179656 | tf_op jit(solution)/shard_map/ppermute | solution.py:214
  59.6 30.8 %collective-permute-start.5 = (f32[2,3,8,2048]{3,2,1,0:T(8,128)}, f32[2,3,8,2048]{3,2,1,0:T(8,128)}, u32[]{:S(2)}, u32[]{:S(2)}) collective-permute-start(f32[2,3,8,2048]{3,2,1,0:T(8,128)} %get-tuple-element.16), channel_id=1, source_target_pairs={{1,0},{2,1},{3,2},{4,3},{5,4},{6,5},{7,6},{8,7},{9,8},{10,9},{11,1... | collective-permute-start | bytes 1179656 | tf_op jit(solution)/shard_map/ppermute | solution.py:215
  64.7 24.6 %copy-start.9 = (f32[1,16,2048]{2,1,0:T(8,128)S(1)}, f32[1,16,2048]{2,1,0:T(8,128)}, u32[]{:S(2)}) copy-start(f32[1,16,2048]{2,1,0:T(8,128)} %copy-done.8) | copy-start | bytes 393220
  64.7 24.6 %copy-start.11 = (f32[1,16,2048]{2,1,0:T(8,128)S(1)}, f32[1,16,2048]{2,1,0:T(8,128)}, u32[]{:S(2)}) copy-start(f32[1,16,2048]{2,1,0:T(8,128)} %copy-done.10) | copy-start | bytes 393220
  64.7 24.6 %copy-start.13 = (f32[1,16,2048]{2,1,0:T(8,128)S(1)}, f32[1,16,2048]{2,1,0:T(8,128)}, u32[]{:S(2)}) copy-start(f32[1,16,2048]{2,1,0:T(8,128)} %copy-done.12) | copy-start | bytes 393220
  66.0 24.3 %copy-start.5 = (f32[2,3,16,2048]{3,2,1,0:T(8,128)S(1)}, f32[2,3,16,2048]{3,2,1,0:T(8,128)}, u32[]{:S(2)}) copy-start(f32[2,3,16,2048]{3,2,1,0:T(8,128)} %copy-done.4) | copy-start | bytes 2359300
  66.0 33.6 %collective-permute-start = (f32[2,3,8,2048]{3,2,1,0:T(8,128)S(1)}, f32[2,3,8,2048]{3,2,1,0:T(8,128)S(1)}, u32[]{:S(2)}, u32[]{:S(2)}) collective-permute-start(f32[2,3,8,2048]{3,2,1,0:T(8,128)S(1)} %get-tuple-element.12), channel_id=1, source_target_pairs={{0,1},{1,2},{2,3},{3,4},{4,5},{5,6},{6,7},{7,8},{8,9},{9,10},{10,1... | collective-permute-start | bytes 1179656 | tf_op jit(solution)/shard_map/ppermute | solution.py:214
  66.1 33.5 %collective-permute-start.1 = (f32[2,3,8,2048]{3,2,1,0:T(8,128)S(1)}, f32[2,3,8,2048]{3,2,1,0:T(8,128)S(1)}, u32[]{:S(2)}, u32[]{:S(2)}) collective-permute-start(f32[2,3,8,2048]{3,2,1,0:T(8,128)S(1)} %get-tuple-element.13), channel_id=1, source_target_pairs={{1,0},{2,1},{3,2},{4,3},{5,4},{6,5},{7,6},{8,7},{9,8},{10,9},{11,1... | collective-permute-start | bytes 1179656 | tf_op jit(solution)/shard_map/ppermute | solution.py:215

commit v2 on v0

v2 whole, which is shorter than its diff:
```python
import functools

import jax
import jax.numpy as jnp
from jax import lax
from jax.experimental import pallas as pl
from jax.experimental.pallas import tpu as pltpu
from jax.sharding import PartitionSpec as P

STEPS = 4
CAP = 2
DT = 0.3
LANES = 128
SUB = 8
DEEP = 8
RIM = (7, 7, 8)
RIMS = sum(RIM)
FROM = (0, 7, 14)
CHUNKS = ((0, 2), (2, 4))

VM = pl.BlockSpec(memory_space=pltpu.VMEM)
SM = pl.BlockSpec(memory_space=pltpu.SMEM)
HB = pl.BlockSpec(memory_space=pltpu.HBM)
PARAMS = pltpu.CompilerParams(vmem_limit_bytes=24 << 20)


def pack_kernel(members, anc, state, out, sem):
    me = lax.axis_index("dom")
    bits = jnp.int32(0)
    for j in range(anc.shape[0]):
        a = anc[j]
        hit = (a != j) & (a // members == me)
        bits = bits | jnp.where(hit, jnp.left_shift(1, a % members), 0)
    first = jnp.int32(members - 1)
    for k in reversed(range(members)):
        first = jnp.where((bits >> k) & 1 == 1, k, first)
    second = jnp.int32(members - 1)
    for k in reversed(range(members)):
        second = jnp.where(((bits >> k) & 1 == 1) & (k != first), k, second)
    copies = []
    for q, p in enumerate((first, second)):
        for f in range(state.shape[1]):
            for t in range(state.shape[2]):
                copies.append(
                    pltpu.make_async_copy(state.at[p, f, t], out.at[:, q, f, t], sem.at[len(copies)])
                )
    for c in copies:
        c.start()
    for c in copies:
        c.wait()


def coef_kernel(depth, coriolis, drag, own, top, bottom):
    rows, tiles = own.shape[1:3]
    for r in range(rows):
        at = pl.ds(r // SUB * tiles * SUB + r % SUB, tiles, stride=SUB)
        values = ((0.5 * DT) * depth[at, :], DT * coriolis[at, :], 1.0 / (1.0 + DT * drag[at, :]))
        for n, value in enumerate(values):
            own[n, r] = value
            if r < DEEP:
                top[n, r] = value
            if r >= rows - DEEP:
                bottom[n, r - (rows - DEEP)] = value


def pick_kernel(members, low, high, table, got, out):
    for d in range(out.shape[0]):
        for k in range(low, high):
            at = table[d * members + k]
            out[d, k - low] = got[at]


def prep_kernel(members, low, high, kept, routed, state, jitter, fields, top, bottom):
    kinds, rows, tiles = fields.shape[1:4]
    slab = kinds * rows
    for k in range(low, high):
        mine = kept[k] == 1
        for f in range(kinds):
            for r in range(rows):
                far = pl.ds(k * slab + f * rows + r, tiles, stride=members * slab)
                t = (k * kinds + f) * (rows // SUB) + r // SUB
                near = pl.ds(t * tiles * SUB + r % SUB, tiles, stride=SUB)
                value = jnp.where(mine, state[near, :], routed[far, :]) + jitter[near, :]
                fields[k - low, f, r] = value
                if r < RIM[f]:
                    top[k - low, FROM[f] + r] = value
                if r >= rows - RIM[f]:
                    bottom[k - low, FROM[f] + r - (rows - RIM[f])] = value


def step_kernel(low, high, fields, above, below, coef, coef_above, coef_below, *rest):
    out, eta, u, v = rest[-4:]
    kinds, rows, tiles = fields.shape[1:4]
    lane = lax.broadcasted_iota(jnp.int32, (tiles, LANES), 1)
    tile = lax.broadcasted_iota(jnp.int32, (tiles, LANES), 0)
    lane_first, lane_last = lane == 0, lane == LANES - 1
    wall_first = lane_first & (tile == 0)
    wall_last = lane_last & (tile == tiles - 1)
    half = 0.5 * DT

    def difference(x, before, after):
        x_before = pltpu.roll(jnp.where(lane_last, pltpu.roll(x, 1, 0), x), 1, 1)
        x_after = pltpu.roll(jnp.where(lane_first, pltpu.roll(x, tiles - 1, 0), x), LANES - 1, 1)
        return jnp.where(wall_last, after, x_after) - jnp.where(wall_first, before, x_before)

    def const(n, r):
        if r < 0:
            return coef_above[n, r + DEEP]
        if r >= rows:
            return coef_below[n, r - rows]
        return coef[n, r]

    def particle(k, carry):
        def start(f, r):
            if r < 0:
                return above[k, FROM[f] + r + RIM[f]]
            if r >= rows:
                return below[k, FROM[f] + r - rows]
            return fields[k, f, r]

        held = (eta, u, v)

        def store(n, f, r, value):
            if n + 1 < STEPS:
                held[f][r + DEEP] = value
            else:
                out[k, f, pl.ds(r // SUB * tiles * SUB + r % SUB, tiles, stride=SUB), :] = value

        for n in range(STEPS):
            left = STEPS - 1 - n
            get = start if n == 0 else (lambda f, r: held[f][r + DEEP])
            low_e, high_e = -(2 * left + 1), rows + 2 * left + 1
            low_v, high_v = -2 * left, rows + 2 * left
            low_u, high_u = (-(2 * left - 1), rows + 2 * left - 1) if left else (0, rows)
            zero = jnp.zeros((tiles, LANES), jnp.float32)

            def flux(r):
                return const(0, r) * get(2, r)

            flux_b, flux_m = flux(low_e - 1), flux(low_e)
            eta_b = eta_m = None
            for r in range(low_e, high_e):
                flux_a = flux(r + 1)
                across = difference(const(0, r) * get(1, r), zero, zero)
                eta_a = get(0, r) - (across + (flux_a - flux_b))
                flux_b, flux_m = flux_m, flux_a
                if low_u <= r < high_u:
                    store(n, 0, r, eta_a)
                m = r - 1
                if low_v <= m < high_v:
                    uu, vv, c, s = get(1, m), get(2, m), const(1, m), const(2, m)
                    if low_u <= m < high_u:
                        store(n, 1, m, s * (uu + c * vv - half * difference(eta_m, eta_m, eta_m)))
                    store(n, 2, m, s * (vv - c * uu - half * (eta_a - eta_b)))
                eta_b, eta_m = eta_m, eta_a
        return carry

    lax.fori_loop(0, high - low, particle, 0)


def local(ancestor, state, jitter, depth, coriolis, drag):
    members, kinds, rows, width = state.shape
    tiles, bands = width // LANES, rows // SUB
    blocks = lax.axis_size("dom")
    count = lax.axis_size("space")
    down = [(i, (i + 1) % count) for i in range(count)]
    up = [((i + 1) % count, i) for i in range(count)]
    me = lax.axis_index("dom")
    f32 = jnp.float32

    def tiled(x):
        x = x.reshape(x.shape[:-2] + (bands, SUB, tiles, LANES))
        return jnp.swapaxes(x, -3, -2)

    state_t, jitter_t = tiled(state), tiled(jitter)

    packed = pl.pallas_call(
        functools.partial(pack_kernel, members),
        in_specs=[SM, HB],
        out_specs=HB,
        out_shape=jax.ShapeDtypeStruct((tiles, CAP, kinds, bands, SUB, LANES), f32),
        scratch_shapes=[pltpu.SemaphoreType.DMA((CAP * kinds * bands,))],
        compiler_params=PARAMS,
        name="pack",
    )(ancestor, state_t)
    pieces = lax.all_to_all(packed, "dom", 0, 0, tiled=True)
    pieces = pieces.reshape(blocks * CAP, kinds * rows, LANES)

    slot = jnp.arange(ancestor.shape[0], dtype=jnp.int32)
    moved = ancestor != slot
    donor = jnp.any((ancestor[:, None] == slot[None, :]) & moved[:, None], axis=0)
    same = (slot[:, None] // members == slot[None, :] // members) & (slot[:, None] < slot[None, :])
    rank = jnp.any(same & donor[:, None], axis=0).astype(jnp.int32)
    place = slot // members * CAP + rank
    table = jnp.sum(jnp.where(ancestor[:, None] == slot[None, :], place[None, :], 0), axis=1)
    kept = lax.dynamic_slice_in_dim(jnp.where(moved, 0, 1).astype(jnp.int32), me * members, members)

    rim = jax.ShapeDtypeStruct((3, DEEP, tiles, LANES), f32)
    coef, coef_top, coef_bottom = pl.pallas_call(
        coef_kernel,
        in_specs=[VM] * 3,
        out_specs=(VM, VM, VM),
        out_shape=(jax.ShapeDtypeStruct((3, rows, tiles, LANES), f32), rim, rim),
        compiler_params=PARAMS,
        name="coef",
    )(*(tiled(x).reshape(rows * tiles, LANES) for x in (depth, coriolis, drag)))
    coef_above = lax.ppermute(coef_bottom, "space", down)
    coef_below = lax.ppermute(coef_top, "space", up)
    pieces, coef_above, coef_below, table, kept = lax.optimization_barrier(
        (pieces, coef_above, coef_below, table, kept)
    )

    chosen = pl.pallas_call(
        functools.partial(pick_kernel, members, 0, members),
        in_specs=[SM, VM],
        out_specs=VM,
        out_shape=jax.ShapeDtypeStruct((blocks, members, kinds * rows, LANES), f32),
        compiler_params=PARAMS,
        name="pick",
    )(table, pieces)
    routed = lax.all_to_all(chosen, "dom", 0, 0, tiled=True).reshape(-1, LANES)

    out = None
    chunks = []
    for low, high in CHUNKS:
        size = high - low
        rim = jax.ShapeDtypeStruct((size, RIMS, tiles, LANES), f32)
        fields, top, bottom = pl.pallas_call(
            functools.partial(prep_kernel, members, low, high),
            in_specs=[SM, VM, VM, VM],
            out_specs=(VM, VM, VM),
            out_shape=(jax.ShapeDtypeStruct((size, kinds, rows, tiles, LANES), f32), rim, rim),
            compiler_params=PARAMS,
            name="prep",
        )(kept, routed, state_t.reshape(-1, LANES), jitter_t.reshape(-1, LANES))
        above = lax.ppermute(bottom, "space", down)
        below = lax.ppermute(top, "space", up)
        chunks.append((fields, above, below))

    for (low, high), (fields, above, below) in zip(CHUNKS, chunks):
        size = high - low
        done = pl.BlockSpec((size, kinds, rows * tiles, LANES), lambda i, at=low // size: (at, 0, 0, 0))
        out = pl.pallas_call(
            functools.partial(step_kernel, low, high),
            grid=(1,),
            in_specs=[VM] * 6 + ([] if out is None else [HB]),
            out_specs=done,
            out_shape=jax.ShapeDtypeStruct((members, kinds, rows * tiles, LANES), f32),
            scratch_shapes=[pltpu.VMEM((rows + 2 * DEEP, tiles, LANES), f32)] * 3,
            input_output_aliases={} if out is None else {6: 0},
            compiler_params=PARAMS,
            name="steps",
        )(fields, above, below, coef, coef_above, coef_below, *([] if out is None else [out]))
    out = out.reshape(members, kinds, bands, tiles, SUB, LANES)
    return jnp.swapaxes(out, -3, -2).reshape(state.shape)


def solution(mesh):
    placed = (
        P(),
        P("dom", None, "space", None),
        P("dom", None, "space", None),
        P("space", None),
        P("space", None),
        P("space", None),
    )
    return jax.shard_map(
        local, mesh=mesh, in_specs=placed, out_specs=P("dom", None, "space", None), check_vma=False
    )
```

time: 259 us -> 84.5 us (0.33)
  the two profiles are of different devices: /device:TPU:2 before, /device:TPU:1 now
where the time goes in v2:
time: 84.5 us; the launch traced here: 84.3 us
  starting transfers between devices  26.5 us (31%)
  blocking collectives  25.9 us (31%)
  Pallas kernels  19 us (22%)
  waiting for transfers between devices  10.2 us (12%)
  local copies, waits for them, and re-layouts  2.17 us (3%)
    all_to_all x1, blocking collectives, local(): routed = lax.all_to_all(chosen, 'dom', 0, 0, tiled=True).reshape(-1, LANES)  25.9 us
    pallas_call x2, Pallas kernels, local(): pl.pallas_call(functools.partial(step_kernel, low, high), grid=(1,), in_s...  13.9 us
    ppermute x2, starting transfers between devices, local(): below = lax.ppermute(top, 'space', up)  11.4 us
    ppermute x1, waiting for transfers between devices, local(): coef_above = lax.ppermute(coef_bottom, 'space', down)  8.08 us
    all_to_all x1, starting transfers between devices, local(): pieces = lax.all_to_all(packed, 'dom', 0, 0, tiled=True)  6.84 us
    ppermute x1, starting transfers between devices, local(): coef_below = lax.ppermute(coef_top, 'space', up)  6.36 us
    pallas_call x2, Pallas kernels, local(): pl.pallas_call(functools.partial(prep_kernel, members, low, high), in_spe...  2.41 us
    unnamed x16, local copies, waits for them, and re-layouts  2.09 us
  transfers between devices with their start and end apart: 7, of which 3 were waited for; matrix products, arithmetic and copies ran while one was open for 1% of the time, Pallas kernels for 10%

profile of v2, /device:TPU:1, one launch (start us, length us, event | category | flops | bytes accessed | tf_op | source)
XLA Modules:
  0.0 84.3 jit_solution(7942090964493993391)
XLA Ops:
  0.0 1.4 %copy-done = f32[4,3,16,2048]{3,2,1,0:T(8,128)S(1)} copy-done((f32[4,3,16,2048]{3,2,1,0:T(8,128)S(1)}, f32[4,3,16,2048]{3,2,1,0:T(8,128)}, u32[]{:S(2)}) %copy-start) | copy-done | bytes 1572888
  1.4 0.7 copy-done.6
  2.1 2.0 %pack.1 = f32[16,2,3,2,8,128]{5,4,3,2,1,0:T(8,128)} custom-call(s32[64]{0:T(128)S(1)} %copy-done.6, f32[4,3,2,16,8,128]{5,4,3,2,1,0:T(8,128)S(1)} %bitcast.32), custom_call_target="tpu_custom_call" | custom-call | tf_op jit(solution)/shard_map/pack/pallas_call | solution.py:177
  4.0 0.0 copy-start.7
  4.1 6.8 %all-to-all-start = ((f32[16,2,3,2,8,128]{5,4,3,2,1,0:T(8,128)}), f32[16,2,3,2,8,128]{5,4,3,2,1,0:T(8,128)S(1)}, u32[]{:S(2)}, u32[]{:S(2)}) async-start(f32[16,2,3,2,8,128]{5,4,3,2,1,0:T(8,128)} %pack.1), calls=%async_computation | async-start | bytes 1572864 | tf_op jit(solution)/shard_map/all_to_all | solution.py:186
  10.9 0.0 copy-done.3
  10.9 0.1 coef.1
  11.0 1.7 %collective-permute-start = (f32[3,8,16,128]{3,2,1,0:T(8,128)S(1)}, f32[3,8,16,128]{3,2,1,0:T(8,128)S(1)}, u32[]{:S(2)}, u32[]{:S(2)}) collective-permute-start(f32[3,8,16,128]{3,2,1,0:T(8,128)S(1)} %get-tuple-element.19), channel_id=1, source_target_pairs={{0,1},{1,2},{2,3},{3,4},{4,5},{5,6},{6,7},{7,8},{8,9},{9,10},{10,1... | collective-permute-start | bytes 589832 | tf_op jit(solution)/shard_map/ppermute | solution.py:207
  12.8 6.4 %collective-permute-start.1 = (f32[3,8,16,128]{3,2,1,0:T(8,128)S(1)}, f32[3,8,16,128]{3,2,1,0:T(8,128)S(1)}, u32[]{:S(2)}, u32[]{:S(2)}) collective-permute-start(f32[3,8,16,128]{3,2,1,0:T(8,128)S(1)} %get-tuple-element.20), channel_id=1, source_target_pairs={{1,0},{2,1},{3,2},{4,3},{5,4},{6,5},{7,6},{8,7},{9,8},{10,9},{11,1... | collective-permute-start | bytes 589832 | tf_op jit(solution)/shard_map/ppermute | solution.py:208
  19.1 0.1 fusion.1
  19.3 0.1 fusion.4
  19.4 0.1 dynamic_slice.3.kept
  19.5 0.2 select_reduce_fusion.table
  19.6 8.1 %collective-permute-done.coef_above = f32[3,8,16,128]{3,2,1,0:T(8,128)S(1)} collective-permute-done((f32[3,8,16,128]{3,2,1,0:T(8,128)S(1)}, f32[3,8,16,128]{3,2,1,0:T(8,128)S(1)}, u32[]{:S(2)}, u32[]{:S(2)}) %collective-permute-start) | collective-permute-done | bytes 196640 | tf_op jit(solution)/shard_map/ppermute | solution.py:207
  27.7 0.0 collective-permute-done.1.coef_below
  27.7 0.0 all-to-all-done
  27.7 0.6 pick.1
  28.4 0.0 copy-start.1
  28.4 0.0 copy-start.2
  28.4 25.9 %all_to_all.10 = f32[16,4,48,128]{3,2,1,0:T(8,128)S(1)} all-to-all(f32[16,4,48,128]{3,2,1,0:T(8,128)S(1)} %pick.1), channel_id=1, replica_groups=mesh['dom'=16,'space'=16] {'dom'}, dimensions={0} | all-to-all | bytes 3145728 | tf_op jit(solution)/shard_map/all_to_all | solution.py:221
  54.3 1.2 %prep.3 = (f32[2,3,16,16,128]{4,3,2,1,0:T(8,128)S(1)}, f32[2,22,16,128]{3,2,1,0:T(8,128)S(1)}, f32[2,22,16,128]{3,2,1,0:T(8,128)S(1)}) custom-call(s32[4]{0:T(128)S(1)} %dynamic_slice.3.kept, f32[3072,128]{1,0:T(8,128)S(1)} %bitcast.35, f32[3072,128]{1,0:T(8,128)S(1)} %bitcast.33, f32[3072,128]{1,0:T(8,128)S(1)} %bitcast.37), custom_call_target="tpu_custom_call" | custom-call | tf_op jit(solution)/shard_map/prep/pallas_call | solution.py:228
  55.5 0.1 collective-permute-start.4
  55.6 6.4 %collective-permute-start.5 = (f32[2,22,16,128]{3,2,1,0:T(8,128)S(1)}, f32[2,22,16,128]{3,2,1,0:T(8,128)S(1)}, u32[]{:S(2)}, u32[]{:S(2)}) collective-permute-start(f32[2,22,16,128]{3,2,1,0:T(8,128)S(1)} %get-tuple-element.32), channel_id=1, source_target_pairs={{1,0},{2,1},{3,2},{4,3},{5,4},{6,5},{7,6},{8,7},{9,8},{10,9},{11,1... | collective-permute-start | bytes 1081352 | tf_op jit(solution)/shard_map/ppermute | solution.py:237
  61.9 1.2 %prep.2 = (f32[2,3,16,16,128]{4,3,2,1,0:T(8,128)S(1)}, f32[2,22,16,128]{3,2,1,0:T(8,128)S(1)}, f32[2,22,16,128]{3,2,1,0:T(8,128)S(1)}) custom-call(s32[4]{0:T(128)S(1)} %dynamic_slice.3.kept, f32[3072,128]{1,0:T(8,128)S(1)} %bitcast.36, f32[3072,128]{1,0:T(8,128)S(1)} %bitcast.34, f32[3072,128]{1,0:T(8,128)S(1)} %bitcast.38), custom_call_target="tpu_custom_call" | custom-call | tf_op jit(solution)/shard_map/prep/pallas_call | solution.py:228
  63.1 0.1 collective-permute-start.2
  63.2 5.1 %collective-permute-start.3 = (f32[2,22,16,128]{3,2,1,0:T(8,128)S(1)}, f32[2,22,16,128]{3,2,1,0:T(8,128)S(1)}, u32[]{:S(2)}, u32[]{:S(2)}) collective-permute-start(f32[2,22,16,128]{3,2,1,0:T(8,128)S(1)} %get-tuple-element.26), channel_id=1, source_target_pairs={{1,0},{2,1},{3,2},{4,3},{5,4},{6,5},{7,6},{8,7},{9,8},{10,9},{11,1... | collective-permute-start | bytes 1081352 | tf_op jit(solution)/shard_map/ppermute | solution.py:237
  68.3 0.9 %collective-permute-done.4.above = f32[2,22,16,128]{3,2,1,0:T(8,128)S(1)} collective-permute-done((f32[2,22,16,128]{3,2,1,0:T(8,128)S(1)}, f32[2,22,16,128]{3,2,1,0:T(8,128)S(1)}, u32[]{:S(2)}, u32[]{:S(2)}) %collective-permute-start.4) | collective-permute-done | bytes 360480 | tf_op jit(solution)/shard_map/ppermute | solution.py:236
  69.2 0.0 collective-permute-done.5.below
  69.2 6.9 %steps.2.rest_0_ = f32[4,3,256,128]{3,2,1,0:T(8,128)} custom-call(f32[2,3,16,16,128]{4,3,2,1,0:T(8,128)S(1)} %get-tuple-element.30.fields, f32[2,22,16,128]{3,2,1,0:T(8,128)S(1)} %collective-permute-done.4.above, f32[2,22,16,128]{3,2,1,0:T(8,128)S(1)} %collective-permute-done.5.below, f32[3,16,16,128]{3,2,1,0:T(8,128)S(1)} %get-tuple-element.27.coef, ...), custom_call_target="tpu_custom_call" | custom-call | tf_op jit(solution)/shard_map/steps/pallas_call | solution.py:243
  76.2 1.1 %collective-permute-done.2.above = f32[2,22,16,128]{3,2,1,0:T(8,128)S(1)} collective-permute-done((f32[2,22,16,128]{3,2,1,0:T(8,128)S(1)}, f32[2,22,16,128]{3,2,1,0:T(8,128)S(1)}, u32[]{:S(2)}, u32[]{:S(2)}) %collective-permute-start.2) | collective-permute-done | bytes 360480 | tf_op jit(solution)/shard_map/ppermute | solution.py:236
  77.3 0.0 collective-permute-done.3.below
  77.3 6.9 %steps.3 = f32[4,3,256,128]{3,2,1,0:T(8,128)} custom-call(f32[2,3,16,16,128]{4,3,2,1,0:T(8,128)S(1)} %get-tuple-element.24.fields, f32[2,22,16,128]{3,2,1,0:T(8,128)S(1)} %collective-permute-done.2.above, f32[2,22,16,128]{3,2,1,0:T(8,128)S(1)} %collective-permute-done.3.below, ...), custom_call_target="tpu_custom_call", output_to_operand_aliasing={{}: (6, {})} | custom-call | tf_op jit(solution)/shard_map/steps/pallas_call | solution.py:243
  (14 shorter events, 0.0 us)
Async XLA Ops:
  0.0 1.4 %copy-start = (f32[4,3,16,2048]{3,2,1,0:T(8,128)S(1)}, f32[4,3,16,2048]{3,2,1,0:T(8,128)}, u32[]{:S(2)}) copy-start(f32[4,3,16,2048]{3,2,1,0:T(8,128)} %param.7) | copy-start | bytes 4718596
  1.4 0.7 copy-start.6
  2.1 8.8 %copy-start.3 = (f32[16,2048]{1,0:T(8,128)S(1)}, f32[16,2048]{1,0:T(8,128)}, u32[]{:S(2)}) copy-start(f32[16,2048]{1,0:T(8,128)} %param.9) | copy-start | bytes 393220
  2.1 8.8 %copy-start.4 = (f32[16,2048]{1,0:T(8,128)S(1)}, f32[16,2048]{1,0:T(8,128)}, u32[]{:S(2)}) copy-start(f32[16,2048]{1,0:T(8,128)} %param.10) | copy-start | bytes 393220
  2.1 8.8 %copy-start.5 = (f32[16,2048]{1,0:T(8,128)S(1)}, f32[16,2048]{1,0:T(8,128)}, u32[]{:S(2)}) copy-start(f32[16,2048]{1,0:T(8,128)} %param.11) | copy-start | bytes 393220
  4.0 15.1 %copy-start.7 = (s32[64]{0:T(128)S(1)}, s32[64]{0:T(128)}, u32[]{:S(2)}) copy-start(s32[64]{0:T(128)} %anc.1) | copy-start | bytes 772
  4.1 23.7 %all-to-all-start = ((f32[16,2,3,2,8,128]{5,4,3,2,1,0:T(8,128)}), f32[16,2,3,2,8,128]{5,4,3,2,1,0:T(8,128)S(1)}, u32[]{:S(2)}, u32[]{:S(2)}) async-start(f32[16,2,3,2,8,128]{5,4,3,2,1,0:T(8,128)} %pack.1), calls=%async_computation | async-start | bytes 1572864 | tf_op jit(solution)/shard_map/all_to_all | solution.py:186
  11.0 16.7 %collective-permute-start = (f32[3,8,16,128]{3,2,1,0:T(8,128)S(1)}, f32[3,8,16,128]{3,2,1,0:T(8,128)S(1)}, u32[]{:S(2)}, u32[]{:S(2)}) collective-permute-start(f32[3,8,16,128]{3,2,1,0:T(8,128)S(1)} %get-tuple-element.19), channel_id=1, source_target_pairs={{0,1},{1,2},{2,3},{3,4},{4,5},{5,6},{6,7},{7,8},{8,9},{9,10},{10,1... | collective-permute-start | bytes 589832 | tf_op jit(solution)/shard_map/ppermute | solution.py:207
  12.8 14.9 %collective-permute-start.1 = (f32[3,8,16,128]{3,2,1,0:T(8,128)S(1)}, f32[3,8,16,128]{3,2,1,0:T(8,128)S(1)}, u32[]{:S(2)}, u32[]{:S(2)}) collective-permute-start(f32[3,8,16,128]{3,2,1,0:T(8,128)S(1)} %get-tuple-element.20), channel_id=1, source_target_pairs={{1,0},{2,1},{3,2},{4,3},{5,4},{6,5},{7,6},{8,7},{9,8},{10,9},{11,1... | collective-permute-start | bytes 589832 | tf_op jit(solution)/shard_map/ppermute | solution.py:208
  28.4 25.9 %copy-start.1 = (f32[4,3,16,2048]{3,2,1,0:T(8,128)S(1)}, f32[4,3,16,2048]{3,2,1,0:T(8,128)}, u32[]{:S(2)}) copy-start(f32[4,3,16,2048]{3,2,1,0:T(8,128)} %param.7) | copy-start | bytes 4718596
  28.4 25.9 %copy-start.2 = (f32[4,3,16,2048]{3,2,1,0:T(8,128)S(1)}, f32[4,3,16,2048]{3,2,1,0:T(8,128)}, u32[]{:S(2)}) copy-start(f32[4,3,16,2048]{3,2,1,0:T(8,128)} %param.8) | copy-start | bytes 4718596
  55.5 13.8 %collective-permute-start.4 = (f32[2,22,16,128]{3,2,1,0:T(8,128)S(1)}, f32[2,22,16,128]{3,2,1,0:T(8,128)S(1)}, u32[]{:S(2)}, u32[]{:S(2)}) collective-permute-start(f32[2,22,16,128]{3,2,1,0:T(8,128)S(1)} %get-tuple-element.31), channel_id=1, source_target_pairs={{0,1},{1,2},{2,3},{3,4},{4,5},{5,6},{6,7},{7,8},{8,9},{9,10},{10,1... | collective-permute-start | bytes 1081352 | tf_op jit(solution)/shard_map/ppermute | solution.py:236
  55.6 13.7 %collective-permute-start.5 = (f32[2,22,16,128]{3,2,1,0:T(8,128)S(1)}, f32[2,22,16,128]{3,2,1,0:T(8,128)S(1)}, u32[]{:S(2)}, u32[]{:S(2)}) collective-permute-start(f32[2,22,16,128]{3,2,1,0:T(8,128)S(1)} %get-tuple-element.32), channel_id=1, source_target_pairs={{1,0},{2,1},{3,2},{4,3},{5,4},{6,5},{7,6},{8,7},{9,8},{10,9},{11,1... | collective-permute-start | bytes 1081352 | tf_op jit(solution)/shard_map/ppermute | solution.py:237
  63.1 14.2 %collective-permute-start.2 = (f32[2,22,16,128]{3,2,1,0:T(8,128)S(1)}, f32[2,22,16,128]{3,2,1,0:T(8,128)S(1)}, u32[]{:S(2)}, u32[]{:S(2)}) collective-permute-start(f32[2,22,16,128]{3,2,1,0:T(8,128)S(1)} %get-tuple-element.25), channel_id=1, source_target_pairs={{0,1},{1,2},{2,3},{3,4},{4,5},{5,6},{6,7},{7,8},{8,9},{9,10},{10,1... | collective-permute-start | bytes 1081352 | tf_op jit(solution)/shard_map/ppermute | solution.py:236
  63.2 14.1 %collective-permute-start.3 = (f32[2,22,16,128]{3,2,1,0:T(8,128)S(1)}, f32[2,22,16,128]{3,2,1,0:T(8,128)S(1)}, u32[]{:S(2)}, u32[]{:S(2)}) collective-permute-start(f32[2,22,16,128]{3,2,1,0:T(8,128)S(1)} %get-tuple-element.26), channel_id=1, source_target_pairs={{1,0},{2,1},{3,2},{4,3},{5,4},{6,5},{7,6},{8,7},{9,8},{10,9},{11,1... | collective-permute-start | bytes 1081352 | tf_op jit(solution)/shard_map/ppermute | solution.py:237

commit v3 on v2

--- a/solution.py
+++ b/solution.py
@@ -16,6 +16,9 @@
 RIM = (7, 7, 8)
 RIMS = sum(RIM)
 FROM = (0, 7, 14)
+COEF_RIM = (8, 6, 6)
+COEF_FROM = (0, 8, 14)
+COEF_RIMS = sum(COEF_RIM)
 CHUNKS = ((0, 2), (2, 4))
 
 VM = pl.BlockSpec(memory_space=pltpu.VMEM)
@@ -24,7 +27,7 @@
 PARAMS = pltpu.CompilerParams(vmem_limit_bytes=24 << 20)
 
 
-def pack_kernel(members, anc, state, out, sem):
+def pack_kernel(members, anc, state, out):
     me = lax.axis_index("dom")
     bits = jnp.int32(0)
     for j in range(anc.shape[0]):
@@ -37,17 +40,10 @@
     second = jnp.int32(members - 1)
     for k in reversed(range(members)):
         second = jnp.where(((bits >> k) & 1 == 1) & (k != first), k, second)
-    copies = []
     for q, p in enumerate((first, second)):
         for f in range(state.shape[1]):
             for t in range(state.shape[2]):
-                copies.append(
-                    pltpu.make_async_copy(state.at[p, f, t], out.at[:, q, f, t], sem.at[len(copies)])
-                )
-    for c in copies:
-        c.start()
-    for c in copies:
-        c.wait()
+                out[:, q, f, t] = state[p, f, t]
 
 
 def coef_kernel(depth, coriolis, drag, own, top, bottom):
@@ -57,10 +53,10 @@
         values = ((0.5 * DT) * depth[at, :], DT * coriolis[at, :], 1.0 / (1.0 + DT * drag[at, :]))
         for n, value in enumerate(values):
             own[n, r] = value
-            if r < DEEP:
-                top[n, r] = value
-            if r >= rows - DEEP:
-                bottom[n, r - (rows - DEEP)] = value
+            if r < COEF_RIM[n]:
+                top[COEF_FROM[n] + r] = value
+            if r >= rows - COEF_RIM[n]:
+                bottom[COEF_FROM[n] + r - (rows - COEF_RIM[n])] = value
 
 
 def pick_kernel(members, low, high, table, got, out):
@@ -88,8 +84,8 @@
                     bottom[k - low, FROM[f] + r - (rows - RIM[f])] = value
 
 
-def step_kernel(low, high, fields, above, below, coef, coef_above, coef_below, *rest):
-    out, eta, u, v = rest[-4:]
+def step_kernel(size, fields, above, below, coef, coef_rims, *rest):
+    out, *held = rest[-4:]
     kinds, rows, tiles = fields.shape[1:4]
     lane = lax.broadcasted_iota(jnp.int32, (tiles, LANES), 1)
     tile = lax.broadcasted_iota(jnp.int32, (tiles, LANES), 0)
@@ -98,64 +94,52 @@
     wall_last = lane_last & (tile == tiles - 1)
     half = 0.5 * DT
 
-    def difference(x, before, after):
-        x_before = pltpu.roll(jnp.where(lane_last, pltpu.roll(x, 1, 0), x), 1, 1)
-        x_after = pltpu.roll(jnp.where(lane_first, pltpu.roll(x, tiles - 1, 0), x), LANES - 1, 1)
-        return jnp.where(wall_last, after, x_after) - jnp.where(wall_first, before, x_before)
+    def difference(x, edge):
+        before = pltpu.roll(jnp.where(lane_last, pltpu.roll(x, 1, 0), x), 1, 1)
+        after = pltpu.roll(jnp.where(lane_first, pltpu.roll(x, tiles - 1, 0), x), LANES - 1, 1)
+        return jnp.where(wall_last, edge, after) - jnp.where(wall_first, edge, before)
 
     def const(n, r):
         if r < 0:
-            return coef_above[n, r + DEEP]
+            return coef_rims[0, COEF_FROM[n] + r + COEF_RIM[n]]
         if r >= rows:
-            return coef_below[n, r - rows]
+            return coef_rims[1, COEF_FROM[n] + r - rows]
         return coef[n, r]
 
     def particle(k, carry):
-        def start(f, r):
+        def get(n, f, r):
+            if n:
+                return held[f][n - 1, r + DEEP]
             if r < 0:
                 return above[k, FROM[f] + r + RIM[f]]
             if r >= rows:
                 return below[k, FROM[f] + r - rows]
             return fields[k, f, r]
 
-        held = (eta, u, v)
-
-        def store(n, f, r, value):
-            if n + 1 < STEPS:
-                held[f][r + DEEP] = value
-            else:
-                out[k, f, pl.ds(r // SUB * tiles * SUB + r % SUB, tiles, stride=SUB), :] = value
+        def put(n, f, r, value):
+            if n < STEPS or f == 0:
+                held[f][n - 1, r + DEEP] = value
+            if n == STEPS and 0 <= r < rows:
+                at = pl.ds(r // SUB * tiles * SUB + r % SUB, tiles, stride=SUB)
+                out[k, f, at, :] = value
 
         for n in range(STEPS):
             left = STEPS - 1 - n
-            get = start if n == 0 else (lambda f, r: held[f][r + DEEP])
-            low_e, high_e = -(2 * left + 1), rows + 2 * left + 1
-            low_v, high_v = -2 * left, rows + 2 * left
-            low_u, high_u = (-(2 * left - 1), rows + 2 * left - 1) if left else (0, rows)
-            zero = jnp.zeros((tiles, LANES), jnp.float32)
-
-            def flux(r):
-                return const(0, r) * get(2, r)
-
-            flux_b, flux_m = flux(low_e - 1), flux(low_e)
-            eta_b = eta_m = None
-            for r in range(low_e, high_e):
-                flux_a = flux(r + 1)
-                across = difference(const(0, r) * get(1, r), zero, zero)
-                eta_a = get(0, r) - (across + (flux_a - flux_b))
-                flux_b, flux_m = flux_m, flux_a
+            low_u, high_u = (1 - 2 * left, rows + 2 * left - 1) if left else (0, rows)
+            for r in range(-(2 * left + 1), rows + 2 * left + 1):
+                across = difference(const(0, r) * get(n, 1, r), 0.0)
+                along = const(0, r + 1) * get(n, 2, r + 1) - const(0, r - 1) * get(n, 2, r - 1)
+                put(n + 1, 0, r, get(n, 0, r) - (across + along))
+            for r in range(-2 * left, rows + 2 * left):
+                uu, vv, c, s = get(n, 1, r), get(n, 2, r), const(1, r), const(2, r)
                 if low_u <= r < high_u:
-                    store(n, 0, r, eta_a)
-                m = r - 1
-                if low_v <= m < high_v:
-                    uu, vv, c, s = get(1, m), get(2, m), const(1, m), const(2, m)
-                    if low_u <= m < high_u:
-                        store(n, 1, m, s * (uu + c * vv - half * difference(eta_m, eta_m, eta_m)))
-                    store(n, 2, m, s * (vv - c * uu - half * (eta_a - eta_b)))
-                eta_b, eta_m = eta_m, eta_a
+                    here = get(n + 1, 0, r)
+                    put(n + 1, 1, r, s * (uu + c * vv - half * difference(here, here)))
+                along = get(n + 1, 0, r + 1) - get(n + 1, 0, r - 1)
+                put(n + 1, 2, r, s * (vv - c * uu - half * along))
         return carry
 
-    lax.fori_loop(0, high - low, particle, 0)
+    lax.fori_loop(0, size, particle, 0)
 
 
 def local(ancestor, state, jitter, depth, coriolis, drag):
@@ -176,16 +160,12 @@
 
     packed = pl.pallas_call(
         functools.partial(pack_kernel, members),
-        in_specs=[SM, HB],
-        out_specs=HB,
+        in_specs=[SM, VM],
+        out_specs=VM,
         out_shape=jax.ShapeDtypeStruct((tiles, CAP, kinds, bands, SUB, LANES), f32),
-        scratch_shapes=[pltpu.SemaphoreType.DMA((CAP * kinds * bands,))],
         compiler_params=PARAMS,
         name="pack",
     )(ancestor, state_t)
-    pieces = lax.all_to_all(packed, "dom", 0, 0, tiled=True)
-    pieces = pieces.reshape(blocks * CAP, kinds * rows, LANES)
-
     slot = jnp.arange(ancestor.shape[0], dtype=jnp.int32)
     moved = ancestor != slot
     donor = jnp.any((ancestor[:, None] == slot[None, :]) & moved[:, None], axis=0)
@@ -195,7 +175,7 @@
     table = jnp.sum(jnp.where(ancestor[:, None] == slot[None, :], place[None, :], 0), axis=1)
     kept = lax.dynamic_slice_in_dim(jnp.where(moved, 0, 1).astype(jnp.int32), me * members, members)
 
-    rim = jax.ShapeDtypeStruct((3, DEEP, tiles, LANES), f32)
+    rim = jax.ShapeDtypeStruct((COEF_RIMS, tiles, LANES), f32)
     coef, coef_top, coef_bottom = pl.pallas_call(
         coef_kernel,
         in_specs=[VM] * 3,
@@ -204,11 +184,20 @@
         compiler_params=PARAMS,
         name="coef",
     )(*(tiled(x).reshape(rows * tiles, LANES) for x in (depth, coriolis, drag)))
-    coef_above = lax.ppermute(coef_bottom, "space", down)
-    coef_below = lax.ppermute(coef_top, "space", up)
-    pieces, coef_above, coef_below, table, kept = lax.optimization_barrier(
-        (pieces, coef_above, coef_below, table, kept)
+    packed, coef_top, coef_bottom = lax.optimization_barrier((packed, coef_top, coef_bottom))
+    pieces = lax.all_to_all(packed, "dom", 0, 0, tiled=True)
+    pieces = pieces.reshape(blocks * CAP, kinds * rows, LANES)
+
+    odd = me % 2
+    part = COEF_RIMS // 2
+    coef_above = lax.ppermute(lax.dynamic_slice_in_dim(coef_bottom, odd * part, part), "space", down)
+    coef_below = lax.ppermute(lax.dynamic_slice_in_dim(coef_top, odd * part, part), "space", up)
+    mine = jnp.stack([coef_above, coef_below])
+    other = lax.ppermute(mine, "dom", [(i, i ^ 1) for i in range(blocks)])
+    coef_rims = jnp.where(
+        odd == 0, jnp.concatenate([mine, other], 1), jnp.concatenate([other, mine], 1)
     )
+    pieces, coef_rims, table, kept = lax.optimization_barrier((pieces, coef_rims, table, kept))
 
     chosen = pl.pallas_call(
         functools.partial(pick_kernel, members, 0, members),
@@ -241,16 +230,16 @@
         size = high - low
         done = pl.BlockSpec((size, kinds, rows * tiles, LANES), lambda i, at=low // size: (at, 0, 0, 0))
         out = pl.pallas_call(
-            functools.partial(step_kernel, low, high),
+            functools.partial(step_kernel, size),
             grid=(1,),
-            in_specs=[VM] * 6 + ([] if out is None else [HB]),
+            in_specs=[VM] * 5 + ([] if out is None else [HB]),
             out_specs=done,
             out_shape=jax.ShapeDtypeStruct((members, kinds, rows * tiles, LANES), f32),
-            scratch_shapes=[pltpu.VMEM((rows + 2 * DEEP, tiles, LANES), f32)] * 3,
-            input_output_aliases={} if out is None else {6: 0},
+            scratch_shapes=[pltpu.VMEM((STEPS, rows + 2 * DEEP, tiles, LANES), f32)] * 3,
+            input_output_aliases={} if out is None else {5: 0},
             compiler_params=PARAMS,
             name="steps",
-        )(fields, above, below, coef, coef_above, coef_below, *([] if out is None else [out]))
+        )(fields, above, below, coef, coef_rims, *([] if out is None else [out]))
     out = out.reshape(members, kinds, bands, tiles, SUB, LANES)
     return jnp.swapaxes(out, -3, -2).reshape(state.shape)
 

time: 84.5 us -> 80.4 us (0.951)
  Pallas kernels: 19 us -> 10.6 us
  waiting for transfers between devices: 10.2 us -> 14.4 us
    pallas_call x3, Pallas kernels: 15.8 us -> 7.46 us  [the longest x2 5.5 us: local(): pl.pallas_call(functools.partial(step_kernel, size), grid=(1,), in_specs=...]
    ppermute x2, waiting for transfers between devices: 2.08 us -> 6.26 us  [local(): above = lax.ppermute(bottom, 'space', down)]
    ppermute x2 -> x3, starting transfers between devices: 8.1 us -> 9.65 us  [the longest x1 7.99 us: local(): lax.ppermute(lax.dynamic_slice_in_dim(coef_top, odd * part, part), 'space...]
    ppermute x2, starting transfers between devices: 11.4 us -> 10.1 us  [local(): below = lax.ppermute(top, 'space', up)]
    ppermute x2 -> x3, waiting for transfers between devices: 8.08 us -> 8.13 us  [the longest x1 5.9 us: local(): lax.ppermute(lax.dynamic_slice_in_dim(coef_bottom, odd * part, part), 'sp...]
  transfers between devices with their start and end apart: 7 -> 8, of which waited for: 3 -> 5; matrix products, arithmetic and copies ran while one was open for 1% -> 1% of each run, Pallas kernels for 10% -> 5%
where the time goes in v3:
time: 80.4 us; the launch traced here: 80.1 us
  starting transfers between devices  26.8 us (33%)
  blocking collectives  25.6 us (32%)
  waiting for transfers between devices  14.4 us (18%)
  Pallas kernels  10.6 us (13%)
  local copies, waits for them, and re-layouts  2.18 us (3%)
    all_to_all x1, blocking collectives, local(): routed = lax.all_to_all(chosen, 'dom', 0, 0, tiled=True).reshape(-1, LANES)  25.6 us
    ppermute x2, starting transfers between devices, local(): below = lax.ppermute(top, 'space', up)  10.1 us
    ppermute x1, starting transfers between devices, local(): lax.ppermute(lax.dynamic_slice_in_dim(coef_top, odd * part, part), 'space...  7.99 us
    all_to_all x1, starting transfers between devices, local(): pieces = lax.all_to_all(packed, 'dom', 0, 0, tiled=True)  6.84 us
    ppermute x2, waiting for transfers between devices, local(): above = lax.ppermute(bottom, 'space', down)  6.26 us
    ppermute x1, waiting for transfers between devices, local(): lax.ppermute(lax.dynamic_slice_in_dim(coef_bottom, odd * part, part), 'sp...  5.9 us
    pallas_call x2, Pallas kernels, local(): pl.pallas_call(functools.partial(step_kernel, size), grid=(1,), in_specs=...  5.5 us
    pallas_call x2, Pallas kernels, local(): pl.pallas_call(functools.partial(prep_kernel, members, low, high), in_spe...  2.41 us
  transfers between devices with their start and end apart: 8, of which 5 were waited for; matrix products, arithmetic and copies ran while one was open for 1% of the time, Pallas kernels for 5%

profile of v3, /device:TPU:1, one launch (start us, length us, event | category | flops | bytes accessed | tf_op | source)
XLA Modules:
  0.0 80.1 jit_solution(13251099615853518682)
XLA Ops:
  0.0 1.4 %copy-done = f32[4,3,16,2048]{3,2,1,0:T(8,128)S(1)} copy-done((f32[4,3,16,2048]{3,2,1,0:T(8,128)S(1)}, f32[4,3,16,2048]{3,2,1,0:T(8,128)}, u32[]{:S(2)}) %copy-start) | copy-done | bytes 1572888
  1.4 0.7 copy-done.6
  2.1 2.0 %pack.1 = f32[16,2,3,2,8,128]{5,4,3,2,1,0:T(8,128)} custom-call(s32[64]{0:T(128)S(1)} %copy-done.6, f32[4,3,2,16,8,128]{5,4,3,2,1,0:T(8,128)S(1)} %bitcast.34), custom_call_target="tpu_custom_call" | custom-call | tf_op jit(solution)/shard_map/pack/pallas_call | solution.py:161
  4.0 0.1 coef.1
  4.2 6.8 %all-to-all-start = ((f32[16,2,3,2,8,128]{5,4,3,2,1,0:T(8,128)}), f32[16,2,3,2,8,128]{5,4,3,2,1,0:T(8,128)S(1)}, u32[]{:S(2)}, u32[]{:S(2)}) async-start(f32[16,2,3,2,8,128]{5,4,3,2,1,0:T(8,128)} %pack.1), calls=%async_computation | async-start | bytes 1572864 | tf_op jit(solution)/shard_map/all_to_all | solution.py:188
  11.0 8.0 %collective-permute-start.1 = (f32[10,16,128]{2,1,0:T(8,128)S(1)}, f32[10,16,128]{2,1,0:T(8,128)S(1)}, u32[]{:S(2)}, u32[]{:S(2)}) collective-permute-start(f32[10,16,128]{2,1,0:T(8,128)S(1)} %constant_dynamic-slice_fusion), channel_id=1, source_target_pairs={{1,0},{2,1},{3,2},{4,3},{5,4},{6,5},{7,6},{8,7},{9,8},{10,9},{11,1... | collective-permute-start | bytes 245768 | tf_op jit(solution)/shard_map/ppermute | solution.py:194
  19.0 0.0 collective-permute-start
  19.0 0.1 fusion.1
  19.1 0.1 fusion.4
  19.2 1.5 %collective-permute-done.1 = f32[10,16,128]{2,1,0:T(8,128)S(1)} collective-permute-done((f32[10,16,128]{2,1,0:T(8,128)S(1)}, f32[10,16,128]{2,1,0:T(8,128)S(1)}, u32[]{:S(2)}, u32[]{:S(2)}) %collective-permute-start.1) | collective-permute-done | bytes 81952 | tf_op jit(solution)/shard_map/ppermute | solution.py:194
  20.7 5.9 %collective-permute-done = f32[10,16,128]{2,1,0:T(8,128)S(1)} collective-permute-done((f32[10,16,128]{2,1,0:T(8,128)S(1)}, f32[10,16,128]{2,1,0:T(8,128)S(1)}, u32[]{:S(2)}, u32[]{:S(2)}) %collective-permute-start) | collective-permute-done | bytes 81952 | tf_op jit(solution)/shard_map/ppermute | solution.py:193
  26.6 1.7 %collective-permute-start.2 = (f32[2,10,16,128]{3,2,1,0:T(8,128)S(1)}, f32[2,10,16,128]{3,2,1,0:T(8,128)S(1)}, u32[]{:S(2)}, u32[]{:S(2)}) collective-permute-start(f32[2,10,16,128]{3,2,1,0:T(8,128)S(1)} %pad_maximum_fusion), channel_id=1, source_target_pairs={{0,16},{16,0},{32,48},{48,32},{64,80},{80,64},{96,112},{112,96},{1... | collective-permute-start | bytes 491528 | tf_op jit(solution)/shard_map/ppermute | solution.py:196
  28.3 0.1 dynamic_slice.11.kept
  28.4 0.2 select_reduce_fusion.table
  28.5 0.8 collective-permute-done.2
  29.3 0.0 all-to-all-done
  29.3 0.6 pick.1
  30.0 0.0 copy-start.1
  30.0 0.0 copy-start.2
  30.0 25.6 %all_to_all.10 = f32[16,4,48,128]{3,2,1,0:T(8,128)S(1)} all-to-all(f32[16,4,48,128]{3,2,1,0:T(8,128)S(1)} %pick.1), channel_id=1, replica_groups=mesh['dom'=16,'space'=16] {'dom'}, dimensions={0} | all-to-all | bytes 3145728 | tf_op jit(solution)/shard_map/all_to_all | solution.py:210
  55.6 1.2 %prep.3 = (f32[2,3,16,16,128]{4,3,2,1,0:T(8,128)S(1)}, f32[2,22,16,128]{3,2,1,0:T(8,128)S(1)}, f32[2,22,16,128]{3,2,1,0:T(8,128)S(1)}) custom-call(s32[4]{0:T(128)S(1)} %dynamic_slice.11.kept, f32[3072,128]{1,0:T(8,128)S(1)} %bitcast.37, f32[3072,128]{1,0:T(8,128)S(1)} %bitcast.35, f32[3072,128]{1,0:T(8,128)S(1)} %bitcast.39), custom_call_target="tpu_custom_call" | custom-call | tf_op jit(solution)/shard_map/prep/pallas_call | solution.py:217
  56.8 0.1 collective-permute-start.5
  56.9 5.1 %collective-permute-start.6 = (f32[2,22,16,128]{3,2,1,0:T(8,128)S(1)}, f32[2,22,16,128]{3,2,1,0:T(8,128)S(1)}, u32[]{:S(2)}, u32[]{:S(2)}) collective-permute-start(f32[2,22,16,128]{3,2,1,0:T(8,128)S(1)} %get-tuple-element.36), channel_id=1, source_target_pairs={{1,0},{2,1},{3,2},{4,3},{5,4},{6,5},{7,6},{8,7},{9,8},{10,9},{11,1... | collective-permute-start | bytes 1081352 | tf_op jit(solution)/shard_map/ppermute | solution.py:226
  62.0 1.2 %prep.2 = (f32[2,3,16,16,128]{4,3,2,1,0:T(8,128)S(1)}, f32[2,22,16,128]{3,2,1,0:T(8,128)S(1)}, f32[2,22,16,128]{3,2,1,0:T(8,128)S(1)}) custom-call(s32[4]{0:T(128)S(1)} %dynamic_slice.11.kept, f32[3072,128]{1,0:T(8,128)S(1)} %bitcast.38, f32[3072,128]{1,0:T(8,128)S(1)} %bitcast.36, f32[3072,128]{1,0:T(8,128)S(1)} %bitcast.40), custom_call_target="tpu_custom_call" | custom-call | tf_op jit(solution)/shard_map/prep/pallas_call | solution.py:217
  63.2 0.1 collective-permute-start.3
  63.3 5.1 %collective-permute-start.4 = (f32[2,22,16,128]{3,2,1,0:T(8,128)S(1)}, f32[2,22,16,128]{3,2,1,0:T(8,128)S(1)}, u32[]{:S(2)}, u32[]{:S(2)}) collective-permute-start(f32[2,22,16,128]{3,2,1,0:T(8,128)S(1)} %get-tuple-element.31), channel_id=1, source_target_pairs={{1,0},{2,1},{3,2},{4,3},{5,4},{6,5},{7,6},{8,7},{9,8},{10,9},{11,1... | collective-permute-start | bytes 1081352 | tf_op jit(solution)/shard_map/ppermute | solution.py:226
  68.3 0.7 collective-permute-done.5.above
  69.1 0.0 collective-permute-done.6.below
  69.1 2.8 %steps.2.rest_0_ = f32[4,3,256,128]{3,2,1,0:T(8,128)} custom-call(f32[2,3,16,16,128]{4,3,2,1,0:T(8,128)S(1)} %get-tuple-element.34.fields, f32[2,22,16,128]{3,2,1,0:T(8,128)S(1)} %collective-permute-done.5.above, f32[2,22,16,128]{3,2,1,0:T(8,128)S(1)} %collective-permute-done.6.below, f32[3,16,16,128]{3,2,1,0:T(8,128)S(1)} %get-tuple-element.32.coef, ...), custom_call_target="tpu_custom_call" | custom-call | tf_op jit(solution)/shard_map/steps/pallas_call | solution.py:232
  71.9 5.5 %collective-permute-done.3.above = f32[2,22,16,128]{3,2,1,0:T(8,128)S(1)} collective-permute-done((f32[2,22,16,128]{3,2,1,0:T(8,128)S(1)}, f32[2,22,16,128]{3,2,1,0:T(8,128)S(1)}, u32[]{:S(2)}, u32[]{:S(2)}) %collective-permute-start.3) | collective-permute-done | bytes 360480 | tf_op jit(solution)/shard_map/ppermute | solution.py:225
  77.4 0.0 collective-permute-done.4.below
  77.4 2.7 %steps.3 = f32[4,3,256,128]{3,2,1,0:T(8,128)} custom-call(f32[2,3,16,16,128]{4,3,2,1,0:T(8,128)S(1)} %get-tuple-element.29.fields, f32[2,22,16,128]{3,2,1,0:T(8,128)S(1)} %collective-permute-done.3.above, f32[2,22,16,128]{3,2,1,0:T(8,128)S(1)} %collective-permute-done.4.below, ...), custom_call_target="tpu_custom_call", output_to_operand_aliasing={{}: (5, {})} | custom-call | tf_op jit(solution)/shard_map/steps/pallas_call | solution.py:232
  (19 shorter events, 0.1 us)
Async XLA Ops:
  0.0 1.4 %copy-start = (f32[4,3,16,2048]{3,2,1,0:T(8,128)S(1)}, f32[4,3,16,2048]{3,2,1,0:T(8,128)}, u32[]{:S(2)}) copy-start(f32[4,3,16,2048]{3,2,1,0:T(8,128)} %param.7) | copy-start | bytes 4718596
  1.4 0.7 copy-start.6
  2.1 2.0 %copy-start.3 = (f32[16,2048]{1,0:T(8,128)S(1)}, f32[16,2048]{1,0:T(8,128)}, u32[]{:S(2)}) copy-start(f32[16,2048]{1,0:T(8,128)} %param.9) | copy-start | bytes 393220
  2.1 2.0 %copy-start.4 = (f32[16,2048]{1,0:T(8,128)S(1)}, f32[16,2048]{1,0:T(8,128)}, u32[]{:S(2)}) copy-start(f32[16,2048]{1,0:T(8,128)} %param.10) | copy-start | bytes 393220
  2.1 2.0 %copy-start.5 = (f32[16,2048]{1,0:T(8,128)S(1)}, f32[16,2048]{1,0:T(8,128)}, u32[]{:S(2)}) copy-start(f32[16,2048]{1,0:T(8,128)} %param.11) | copy-start | bytes 393220
  4.0 15.0 %copy-start.7 = (s32[64]{0:T(128)S(1)}, s32[64]{0:T(128)}, u32[]{:S(2)}) copy-start(s32[64]{0:T(128)} %anc.1) | copy-start | bytes 772
  4.2 25.2 %all-to-all-start = ((f32[16,2,3,2,8,128]{5,4,3,2,1,0:T(8,128)}), f32[16,2,3,2,8,128]{5,4,3,2,1,0:T(8,128)S(1)}, u32[]{:S(2)}, u32[]{:S(2)}) async-start(f32[16,2,3,2,8,128]{5,4,3,2,1,0:T(8,128)} %pack.1), calls=%async_computation | async-start | bytes 1572864 | tf_op jit(solution)/shard_map/all_to_all | solution.py:188
  11.0 9.7 %collective-permute-start.1 = (f32[10,16,128]{2,1,0:T(8,128)S(1)}, f32[10,16,128]{2,1,0:T(8,128)S(1)}, u32[]{:S(2)}, u32[]{:S(2)}) collective-permute-start(f32[10,16,128]{2,1,0:T(8,128)S(1)} %constant_dynamic-slice_fusion), channel_id=1, source_target_pairs={{1,0},{2,1},{3,2},{4,3},{5,4},{6,5},{7,6},{8,7},{9,8},{10,9},{11,1... | collective-permute-start | bytes 245768 | tf_op jit(solution)/shard_map/ppermute | solution.py:194
  19.0 7.6 %collective-permute-start = (f32[10,16,128]{2,1,0:T(8,128)S(1)}, f32[10,16,128]{2,1,0:T(8,128)S(1)}, u32[]{:S(2)}, u32[]{:S(2)}) collective-permute-start(f32[10,16,128]{2,1,0:T(8,128)S(1)} %constant_dynamic-slice_fusion.1), channel_id=1, source_target_pairs={{0,1},{1,2},{2,3},{3,4},{4,5},{5,6},{6,7},{7,8},{8,9},{9,10},{10,1... | collective-permute-start | bytes 245768 | tf_op jit(solution)/shard_map/ppermute | solution.py:193
  26.6 2.7 %collective-permute-start.2 = (f32[2,10,16,128]{3,2,1,0:T(8,128)S(1)}, f32[2,10,16,128]{3,2,1,0:T(8,128)S(1)}, u32[]{:S(2)}, u32[]{:S(2)}) collective-permute-start(f32[2,10,16,128]{3,2,1,0:T(8,128)S(1)} %pad_maximum_fusion), channel_id=1, source_target_pairs={{0,16},{16,0},{32,48},{48,32},{64,80},{80,64},{96,112},{112,96},{1... | collective-permute-start | bytes 491528 | tf_op jit(solution)/shard_map/ppermute | solution.py:196
  30.0 25.6 %copy-start.1 = (f32[4,3,16,2048]{3,2,1,0:T(8,128)S(1)}, f32[4,3,16,2048]{3,2,1,0:T(8,128)}, u32[]{:S(2)}) copy-start(f32[4,3,16,2048]{3,2,1,0:T(8,128)} %param.7) | copy-start | bytes 4718596
  30.0 25.6 %copy-start.2 = (f32[4,3,16,2048]{3,2,1,0:T(8,128)S(1)}, f32[4,3,16,2048]{3,2,1,0:T(8,128)}, u32[]{:S(2)}) copy-start(f32[4,3,16,2048]{3,2,1,0:T(8,128)} %param.8) | copy-start | bytes 4718596
  56.8 12.3 %collective-permute-start.5 = (f32[2,22,16,128]{3,2,1,0:T(8,128)S(1)}, f32[2,22,16,128]{3,2,1,0:T(8,128)S(1)}, u32[]{:S(2)}, u32[]{:S(2)}) collective-permute-start(f32[2,22,16,128]{3,2,1,0:T(8,128)S(1)} %get-tuple-element.35), channel_id=1, source_target_pairs={{0,1},{1,2},{2,3},{3,4},{4,5},{5,6},{6,7},{7,8},{8,9},{9,10},{10,1... | collective-permute-start | bytes 1081352 | tf_op jit(solution)/shard_map/ppermute | solution.py:225
  56.9 12.2 %collective-permute-start.6 = (f32[2,22,16,128]{3,2,1,0:T(8,128)S(1)}, f32[2,22,16,128]{3,2,1,0:T(8,128)S(1)}, u32[]{:S(2)}, u32[]{:S(2)}) collective-permute-start(f32[2,22,16,128]{3,2,1,0:T(8,128)S(1)} %get-tuple-element.36), channel_id=1, source_target_pairs={{1,0},{2,1},{3,2},{4,3},{5,4},{6,5},{7,6},{8,7},{9,8},{10,9},{11,1... | collective-permute-start | bytes 1081352 | tf_op jit(solution)/shard_map/ppermute | solution.py:226
  63.2 14.2 %collective-permute-start.3 = (f32[2,22,16,128]{3,2,1,0:T(8,128)S(1)}, f32[2,22,16,128]{3,2,1,0:T(8,128)S(1)}, u32[]{:S(2)}, u32[]{:S(2)}) collective-permute-start(f32[2,22,16,128]{3,2,1,0:T(8,128)S(1)} %get-tuple-element.30), channel_id=1, source_target_pairs={{0,1},{1,2},{2,3},{3,4},{4,5},{5,6},{6,7},{7,8},{8,9},{9,10},{10,1... | collective-permute-start | bytes 1081352 | tf_op jit(solution)/shard_map/ppermute | solution.py:225
  63.3 14.1 %collective-permute-start.4 = (f32[2,22,16,128]{3,2,1,0:T(8,128)S(1)}, f32[2,22,16,128]{3,2,1,0:T(8,128)S(1)}, u32[]{:S(2)}, u32[]{:S(2)}) collective-permute-start(f32[2,22,16,128]{3,2,1,0:T(8,128)S(1)} %get-tuple-element.31), channel_id=1, source_target_pairs={{1,0},{2,1},{3,2},{4,3},{5,4},{6,5},{7,6},{8,7},{9,8},{10,9},{11,1... | collective-permute-start | bytes 1081352 | tf_op jit(solution)/shard_map/ppermute | solution.py:226

commit v4 on v3

--- a/solution.py
+++ b/solution.py
@@ -188,16 +188,10 @@
     pieces = lax.all_to_all(packed, "dom", 0, 0, tiled=True)
     pieces = pieces.reshape(blocks * CAP, kinds * rows, LANES)
 
-    odd = me % 2
-    part = COEF_RIMS // 2
-    coef_above = lax.ppermute(lax.dynamic_slice_in_dim(coef_bottom, odd * part, part), "space", down)
-    coef_below = lax.ppermute(lax.dynamic_slice_in_dim(coef_top, odd * part, part), "space", up)
-    mine = jnp.stack([coef_above, coef_below])
-    other = lax.ppermute(mine, "dom", [(i, i ^ 1) for i in range(blocks)])
-    coef_rims = jnp.where(
-        odd == 0, jnp.concatenate([mine, other], 1), jnp.concatenate([other, mine], 1)
+    coef_rims = jnp.stack(
+        [lax.ppermute(coef_bottom, "space", down), lax.ppermute(coef_top, "space", up)]
     )
-    pieces, coef_rims, table, kept = lax.optimization_barrier((pieces, coef_rims, table, kept))
+    pieces, table, kept = lax.optimization_barrier((pieces, table, kept))
 
     chosen = pl.pallas_call(
         functools.partial(pick_kernel, members, 0, members),
@@ -208,6 +202,7 @@
         name="pick",
     )(table, pieces)
     routed = lax.all_to_all(chosen, "dom", 0, 0, tiled=True).reshape(-1, LANES)
+    routed, coef_rims = lax.optimization_barrier((routed, coef_rims))
 
     out = None
     chunks = []

time: 80.4 us -> 84 us (1.045)
  blocking collectives: 25.6 us -> 0 us
  waiting for transfers between devices: 14.4 us -> 34.2 us
  starting transfers between devices: 26.8 us -> 32.6 us
  local copies, waits for them, and re-layouts: 2.18 us -> 5.45 us
    all_to_all x1 -> x0, blocking collectives: 25.6 us -> none  [local(): routed = lax.all_to_all(chosen, 'dom', 0, 0, tiled=True).reshape(-1, LANES)]
    all_to_all x1, waiting for transfers between devices: 0.01 us -> 12.1 us  [local(): pieces = lax.all_to_all(packed, 'dom', 0, 0, tiled=True)]
    all_to_all x0 -> x1, waiting for transfers between devices: none -> 8.43 us  [local(): routed = lax.all_to_all(chosen, 'dom', 0, 0, tiled=True).reshape(-1, LANES)]
    all_to_all x0 -> x1, starting transfers between devices: none -> 4.74 us  [local(): routed = lax.all_to_all(chosen, 'dom', 0, 0, tiled=True).reshape(-1, LANES)]
    unnamed x16 -> x22, local copies, waits for them, and re-layouts: 2.09 us -> 5.37 us
    ppermute x2, starting transfers between devices: 10.1 us -> 12.9 us  [local(): below = lax.ppermute(top, 'space', up)]
    ppermute x3 -> x2, starting transfers between devices: 9.65 us -> 8 us  [the longest x1 6.36 us: local(): lax.ppermute(coef_top, 'space', up)]
    ppermute x3 -> x2, waiting for transfers between devices: 8.13 us -> 6.6 us  [the longest x1 6.6 us: local(): lax.ppermute(coef_bottom, 'space', down)]
where the time goes in v4:
time: 84 us; the launch traced here: 83.7 us
  waiting for transfers between devices  34.2 us (41%)
  starting transfers between devices  32.6 us (39%)
  Pallas kernels  10.8 us (13%)
  local copies, waits for them, and re-layouts  5.45 us (6%)
    ppermute x2, starting transfers between devices, local(): below = lax.ppermute(top, 'space', up)  12.9 us
    all_to_all x1, waiting for transfers between devices, local(): pieces = lax.all_to_all(packed, 'dom', 0, 0, tiled=True)  12.1 us
    all_to_all x1, waiting for transfers between devices, local(): routed = lax.all_to_all(chosen, 'dom', 0, 0, tiled=True).reshape(-1, LANES)  8.43 us
    ppermute x2, waiting for transfers between devices, local(): above = lax.ppermute(bottom, 'space', down)  7.07 us
    all_to_all x1, starting transfers between devices, local(): pieces = lax.all_to_all(packed, 'dom', 0, 0, tiled=True)  6.83 us
    ppermute x1, waiting for transfers between devices, local(): lax.ppermute(coef_bottom, 'space', down)  6.6 us
    ppermute x1, starting transfers between devices, local(): lax.ppermute(coef_top, 'space', up)  6.36 us
    pallas_call x2, Pallas kernels, local(): pl.pallas_call(functools.partial(step_kernel, size), grid=(1,), in_specs=...  5.72 us
  transfers between devices with their start and end apart: 8, of which 5 were waited for; matrix products, arithmetic and copies ran while one was open for 1% of the time, Pallas kernels for 5%

profile of v4, /device:TPU:1, one launch (start us, length us, event | category | flops | bytes accessed | tf_op | source)
XLA Modules:
  0.0 83.7 jit_solution(3044084830274947217)
XLA Ops:
  0.0 1.4 %copy-done = f32[4,3,16,2048]{3,2,1,0:T(8,128)S(1)} copy-done((f32[4,3,16,2048]{3,2,1,0:T(8,128)S(1)}, f32[4,3,16,2048]{3,2,1,0:T(8,128)}, u32[]{:S(2)}) %copy-start) | copy-done | bytes 1572888
  1.4 0.7 copy-done.9
  2.1 2.0 %pack.1 = f32[16,2,3,2,8,128]{5,4,3,2,1,0:T(8,128)} custom-call(s32[64]{0:T(128)S(1)} %copy-done.9, f32[4,3,2,16,8,128]{5,4,3,2,1,0:T(8,128)S(1)} %bitcast.34), custom_call_target="tpu_custom_call" | custom-call | tf_op jit(solution)/shard_map/pack/pallas_call | solution.py:161
  4.0 0.1 coef.1
  4.2 0.7 copy-done.4
  4.9 6.8 %all-to-all-start = ((f32[16,2,3,2,8,128]{5,4,3,2,1,0:T(8,128)}), f32[16,2,3,2,8,128]{5,4,3,2,1,0:T(8,128)S(1)}, u32[]{:S(2)}, u32[]{:S(2)}) async-start(f32[16,2,3,2,8,128]{5,4,3,2,1,0:T(8,128)} %pack.1), calls=%async_computation | async-start | bytes 1572864 | tf_op jit(solution)/shard_map/all_to_all | solution.py:188
  11.8 0.1 dynamic_slice.3.kept
  11.8 0.1 fusion.1
  11.9 0.1 fusion.4
  12.1 0.2 select_reduce_fusion.table
  12.2 12.1 %all-to-all-done = f32[16,2,3,2,8,128]{5,4,3,2,1,0:T(8,128)S(1)} async-done(((f32[16,2,3,2,8,128]{5,4,3,2,1,0:T(8,128)}), f32[16,2,3,2,8,128]{5,4,3,2,1,0:T(8,128)S(1)}, u32[]{:S(2)}, u32[]{:S(2)}) %all-to-all-start) | async-done | bytes 786464 | tf_op jit(solution)/shard_map/all_to_all | solution.py:188
  24.4 0.6 pick.1
  25.0 0.0 copy-start.3
  25.0 1.1 %copy-done.3 = f32[16,4,48,128]{3,2,1,0:T(8,128)} copy-done((f32[16,4,48,128]{3,2,1,0:T(8,128)}, f32[16,4,48,128]{3,2,1,0:T(8,128)S(1)}, u32[]{:S(2)}) %copy-start.3) | copy-done | bytes 1572888
  26.2 4.7 %all-to-all-start.1 = ((f32[16,4,48,128]{3,2,1,0:T(8,128)}), f32[16,4,48,128]{3,2,1,0:T(8,128)S(1)}, u32[]{:S(2)}, u32[]{:S(2)}) async-start(f32[16,4,48,128]{3,2,1,0:T(8,128)} %copy-done.3), calls=%async_computation.1 | async-start | bytes 3145728 | tf_op jit(solution)/shard_map/all_to_all | solution.py:204
  30.9 1.6 %collective-permute-start = (f32[20,16,128]{2,1,0:T(8,128)S(1)}, f32[20,16,128]{2,1,0:T(8,128)S(1)}, u32[]{:S(2)}, u32[]{:S(2)}) collective-permute-start(f32[20,16,128]{2,1,0:T(8,128)S(1)} %get-tuple-element.28), channel_id=1, source_target_pairs={{0,1},{1,2},{2,3},{3,4},{4,5},{5,6},{6,7},{7,8},{8,9},{9,10},{10,1... | collective-permute-start | bytes 491528 | tf_op jit(solution)/shard_map/ppermute | solution.py:192
  32.6 6.4 %collective-permute-start.1 = (f32[20,16,128]{2,1,0:T(8,128)S(1)}, f32[20,16,128]{2,1,0:T(8,128)S(1)}, u32[]{:S(2)}, u32[]{:S(2)}) collective-permute-start(f32[20,16,128]{2,1,0:T(8,128)S(1)} %get-tuple-element.29), channel_id=1, source_target_pairs={{1,0},{2,1},{3,2},{4,3},{5,4},{6,5},{7,6},{8,7},{9,8},{10,9},{11,1... | collective-permute-start | bytes 491528 | tf_op jit(solution)/shard_map/ppermute | solution.py:192
  38.9 6.6 %collective-permute-done = f32[20,16,128]{2,1,0:T(8,128)S(1)} collective-permute-done((f32[20,16,128]{2,1,0:T(8,128)S(1)}, f32[20,16,128]{2,1,0:T(8,128)S(1)}, u32[]{:S(2)}, u32[]{:S(2)}) %collective-permute-start) | collective-permute-done | bytes 163872 | tf_op jit(solution)/shard_map/ppermute | solution.py:192
  45.6 8.4 %all-to-all-done.1 = f32[16,4,48,128]{3,2,1,0:T(8,128)S(1)} async-done(((f32[16,4,48,128]{3,2,1,0:T(8,128)}), f32[16,4,48,128]{3,2,1,0:T(8,128)S(1)}, u32[]{:S(2)}, u32[]{:S(2)}) %all-to-all-start.1) | async-done | bytes 1572896 | tf_op jit(solution)/shard_map/all_to_all | solution.py:204
  54.0 1.4 %copy-done.2 = f32[4,3,16,2048]{3,2,1,0:T(8,128)S(1)} copy-done((f32[4,3,16,2048]{3,2,1,0:T(8,128)S(1)}, f32[4,3,16,2048]{3,2,1,0:T(8,128)}, u32[]{:S(2)}) %copy-start.2) | copy-done | bytes 1572888
  55.4 1.2 %prep.3 = (f32[2,3,16,16,128]{4,3,2,1,0:T(8,128)S(1)}, f32[2,22,16,128]{3,2,1,0:T(8,128)S(1)}, f32[2,22,16,128]{3,2,1,0:T(8,128)S(1)}) custom-call(s32[4]{0:T(128)S(1)} %dynamic_slice.3.kept, f32[3072,128]{1,0:T(8,128)S(1)} %bitcast.37, f32[3072,128]{1,0:T(8,128)S(1)} %bitcast.35, f32[3072,128]{1,0:T(8,128)S(1)} %bitcast.39), custom_call_target="tpu_custom_call" | custom-call | tf_op jit(solution)/shard_map/prep/pallas_call | solution.py:212
  56.6 0.1 collective-permute-start.4
  56.7 7.8 %collective-permute-start.5 = (f32[2,22,16,128]{3,2,1,0:T(8,128)S(1)}, f32[2,22,16,128]{3,2,1,0:T(8,128)S(1)}, u32[]{:S(2)}, u32[]{:S(2)}) collective-permute-start(f32[2,22,16,128]{3,2,1,0:T(8,128)S(1)} %get-tuple-element.38), channel_id=1, source_target_pairs={{1,0},{2,1},{3,2},{4,3},{5,4},{6,5},{7,6},{8,7},{9,8},{10,9},{11,1... | collective-permute-start | bytes 1081352 | tf_op jit(solution)/shard_map/ppermute | solution.py:221
  64.5 1.2 %prep.2 = (f32[2,3,16,16,128]{4,3,2,1,0:T(8,128)S(1)}, f32[2,22,16,128]{3,2,1,0:T(8,128)S(1)}, f32[2,22,16,128]{3,2,1,0:T(8,128)S(1)}) custom-call(s32[4]{0:T(128)S(1)} %dynamic_slice.3.kept, f32[3072,128]{1,0:T(8,128)S(1)} %bitcast.38, f32[3072,128]{1,0:T(8,128)S(1)} %bitcast.36, f32[3072,128]{1,0:T(8,128)S(1)} %bitcast.40), custom_call_target="tpu_custom_call" | custom-call | tf_op jit(solution)/shard_map/prep/pallas_call | solution.py:212
  65.8 0.1 collective-permute-start.2
  65.8 5.1 %collective-permute-start.3 = (f32[2,22,16,128]{3,2,1,0:T(8,128)S(1)}, f32[2,22,16,128]{3,2,1,0:T(8,128)S(1)}, u32[]{:S(2)}, u32[]{:S(2)}) collective-permute-start(f32[2,22,16,128]{3,2,1,0:T(8,128)S(1)} %get-tuple-element.33), channel_id=1, source_target_pairs={{1,0},{2,1},{3,2},{4,3},{5,4},{6,5},{7,6},{8,7},{9,8},{10,9},{11,1... | collective-permute-start | bytes 1081352 | tf_op jit(solution)/shard_map/ppermute | solution.py:221
  70.9 2.2 %collective-permute-done.4.above = f32[2,22,16,128]{3,2,1,0:T(8,128)S(1)} collective-permute-done((f32[2,22,16,128]{3,2,1,0:T(8,128)S(1)}, f32[2,22,16,128]{3,2,1,0:T(8,128)S(1)}, u32[]{:S(2)}, u32[]{:S(2)}) %collective-permute-start.4) | collective-permute-done | bytes 360480 | tf_op jit(solution)/shard_map/ppermute | solution.py:220
  73.1 0.0 collective-permute-done.5.below
  73.1 2.9 %steps.2.rest_0_ = f32[4,3,256,128]{3,2,1,0:T(8,128)} custom-call(f32[2,3,16,16,128]{4,3,2,1,0:T(8,128)S(1)} %get-tuple-element.36.fields, f32[2,22,16,128]{3,2,1,0:T(8,128)S(1)} %collective-permute-done.4.above, f32[2,22,16,128]{3,2,1,0:T(8,128)S(1)} %collective-permute-done.5.below, f32[3,16,16,128]{3,2,1,0:T(8,128)S(1)} %copy-done.5, ...), custom_call_target="tpu_custom_call" | custom-call | tf_op jit(solution)/shard_map/steps/pallas_call | solution.py:227
  76.0 4.9 %collective-permute-done.2.above = f32[2,22,16,128]{3,2,1,0:T(8,128)S(1)} collective-permute-done((f32[2,22,16,128]{3,2,1,0:T(8,128)S(1)}, f32[2,22,16,128]{3,2,1,0:T(8,128)S(1)}, u32[]{:S(2)}, u32[]{:S(2)}) %collective-permute-start.2) | collective-permute-done | bytes 360480 | tf_op jit(solution)/shard_map/ppermute | solution.py:220
  80.9 0.0 collective-permute-done.3.below
  80.9 2.9 %steps.3 = f32[4,3,256,128]{3,2,1,0:T(8,128)} custom-call(f32[2,3,16,16,128]{4,3,2,1,0:T(8,128)S(1)} %get-tuple-element.31.fields, f32[2,22,16,128]{3,2,1,0:T(8,128)S(1)} %collective-permute-done.2.above, f32[2,22,16,128]{3,2,1,0:T(8,128)S(1)} %collective-permute-done.3.below, f32[3,16,16,128]{3,2,1,0:T(8,128)S(1)} %copy-done.5, ...), custom_call_target="tpu_custom_call", output_to_operand_aliasing={{}: (5, {})} | custom-call | tf_op jit(solution)/shard_map/steps/pallas_call | solution.py:227
  (22 shorter events, 0.1 us)
Async XLA Ops:
  0.0 1.4 %copy-start = (f32[4,3,16,2048]{3,2,1,0:T(8,128)S(1)}, f32[4,3,16,2048]{3,2,1,0:T(8,128)}, u32[]{:S(2)}) copy-start(f32[4,3,16,2048]{3,2,1,0:T(8,128)} %param.7) | copy-start | bytes 4718596
  1.4 0.7 copy-start.9
  2.1 2.0 %copy-start.6 = (f32[16,2048]{1,0:T(8,128)S(1)}, f32[16,2048]{1,0:T(8,128)}, u32[]{:S(2)}) copy-start(f32[16,2048]{1,0:T(8,128)} %param.9) | copy-start | bytes 393220
  2.1 2.0 %copy-start.7 = (f32[16,2048]{1,0:T(8,128)S(1)}, f32[16,2048]{1,0:T(8,128)}, u32[]{:S(2)}) copy-start(f32[16,2048]{1,0:T(8,128)} %param.10) | copy-start | bytes 393220
  2.1 2.0 %copy-start.8 = (f32[16,2048]{1,0:T(8,128)S(1)}, f32[16,2048]{1,0:T(8,128)}, u32[]{:S(2)}) copy-start(f32[16,2048]{1,0:T(8,128)} %param.11) | copy-start | bytes 393220
  4.0 7.7 %copy-start.10 = (s32[64]{0:T(128)S(1)}, s32[64]{0:T(128)}, u32[]{:S(2)}) copy-start(s32[64]{0:T(128)} %anc.1) | copy-start | bytes 772
  4.2 0.7 copy-start.4
  4.9 19.5 %all-to-all-start = ((f32[16,2,3,2,8,128]{5,4,3,2,1,0:T(8,128)}), f32[16,2,3,2,8,128]{5,4,3,2,1,0:T(8,128)S(1)}, u32[]{:S(2)}, u32[]{:S(2)}) async-start(f32[16,2,3,2,8,128]{5,4,3,2,1,0:T(8,128)} %pack.1), calls=%async_computation | async-start | bytes 1572864 | tf_op jit(solution)/shard_map/all_to_all | solution.py:188
  25.0 1.1 %copy-start.3 = (f32[16,4,48,128]{3,2,1,0:T(8,128)}, f32[16,4,48,128]{3,2,1,0:T(8,128)S(1)}, u32[]{:S(2)}) copy-start(f32[16,4,48,128]{3,2,1,0:T(8,128)S(1)} %pick.1) | copy-start | bytes 4718596
  26.2 27.8 %copy-start.1 = (f32[4,3,16,2048]{3,2,1,0:T(8,128)S(1)}, f32[4,3,16,2048]{3,2,1,0:T(8,128)}, u32[]{:S(2)}) copy-start(f32[4,3,16,2048]{3,2,1,0:T(8,128)} %param.7) | copy-start | bytes 4718596
  26.2 27.8 %all-to-all-start.1 = ((f32[16,4,48,128]{3,2,1,0:T(8,128)}), f32[16,4,48,128]{3,2,1,0:T(8,128)S(1)}, u32[]{:S(2)}, u32[]{:S(2)}) async-start(f32[16,4,48,128]{3,2,1,0:T(8,128)} %copy-done.3), calls=%async_computation.1 | async-start | bytes 3145728 | tf_op jit(solution)/shard_map/all_to_all | solution.py:204
  30.9 14.6 %collective-permute-start = (f32[20,16,128]{2,1,0:T(8,128)S(1)}, f32[20,16,128]{2,1,0:T(8,128)S(1)}, u32[]{:S(2)}, u32[]{:S(2)}) collective-permute-start(f32[20,16,128]{2,1,0:T(8,128)S(1)} %get-tuple-element.28), channel_id=1, source_target_pairs={{0,1},{1,2},{2,3},{3,4},{4,5},{5,6},{6,7},{7,8},{8,9},{9,10},{10,1... | collective-permute-start | bytes 491528 | tf_op jit(solution)/shard_map/ppermute | solution.py:192
  32.6 13.0 %collective-permute-start.1 = (f32[20,16,128]{2,1,0:T(8,128)S(1)}, f32[20,16,128]{2,1,0:T(8,128)S(1)}, u32[]{:S(2)}, u32[]{:S(2)}) collective-permute-start(f32[20,16,128]{2,1,0:T(8,128)S(1)} %get-tuple-element.29), channel_id=1, source_target_pairs={{1,0},{2,1},{3,2},{4,3},{5,4},{6,5},{7,6},{8,7},{9,8},{10,9},{11,1... | collective-permute-start | bytes 491528 | tf_op jit(solution)/shard_map/ppermute | solution.py:192
  54.0 1.4 %copy-start.2 = (f32[4,3,16,2048]{3,2,1,0:T(8,128)S(1)}, f32[4,3,16,2048]{3,2,1,0:T(8,128)}, u32[]{:S(2)}) copy-start(f32[4,3,16,2048]{3,2,1,0:T(8,128)} %param.8) | copy-start | bytes 4718596
  56.6 16.5 %collective-permute-start.4 = (f32[2,22,16,128]{3,2,1,0:T(8,128)S(1)}, f32[2,22,16,128]{3,2,1,0:T(8,128)S(1)}, u32[]{:S(2)}, u32[]{:S(2)}) collective-permute-start(f32[2,22,16,128]{3,2,1,0:T(8,128)S(1)} %get-tuple-element.37), channel_id=1, source_target_pairs={{0,1},{1,2},{2,3},{3,4},{4,5},{5,6},{6,7},{7,8},{8,9},{9,10},{10,1... | collective-permute-start | bytes 1081352 | tf_op jit(solution)/shard_map/ppermute | solution.py:220
  56.7 16.4 %copy-start.5 = (f32[3,16,16,128]{3,2,1,0:T(8,128)S(1)}, f32[3,16,16,128]{3,2,1,0:T(8,128)}, u32[]{:S(2)}) copy-start(f32[3,16,16,128]{3,2,1,0:T(8,128)} %copy-done.4) | copy-start | bytes 1179652
  56.7 16.4 %collective-permute-start.5 = (f32[2,22,16,128]{3,2,1,0:T(8,128)S(1)}, f32[2,22,16,128]{3,2,1,0:T(8,128)S(1)}, u32[]{:S(2)}, u32[]{:S(2)}) collective-permute-start(f32[2,22,16,128]{3,2,1,0:T(8,128)S(1)} %get-tuple-element.38), channel_id=1, source_target_pairs={{1,0},{2,1},{3,2},{4,3},{5,4},{6,5},{7,6},{8,7},{9,8},{10,9},{11,1... | collective-permute-start | bytes 1081352 | tf_op jit(solution)/shard_map/ppermute | solution.py:221
  65.8 15.1 %collective-permute-start.2 = (f32[2,22,16,128]{3,2,1,0:T(8,128)S(1)}, f32[2,22,16,128]{3,2,1,0:T(8,128)S(1)}, u32[]{:S(2)}, u32[]{:S(2)}) collective-permute-start(f32[2,22,16,128]{3,2,1,0:T(8,128)S(1)} %get-tuple-element.32), channel_id=1, source_target_pairs={{0,1},{1,2},{2,3},{3,4},{4,5},{5,6},{6,7},{7,8},{8,9},{9,10},{10,1... | collective-permute-start | bytes 1081352 | tf_op jit(solution)/shard_map/ppermute | solution.py:220
  65.8 15.0 %collective-permute-start.3 = (f32[2,22,16,128]{3,2,1,0:T(8,128)S(1)}, f32[2,22,16,128]{3,2,1,0:T(8,128)S(1)}, u32[]{:S(2)}, u32[]{:S(2)}) collective-permute-start(f32[2,22,16,128]{3,2,1,0:T(8,128)S(1)} %get-tuple-element.33), channel_id=1, source_target_pairs={{1,0},{2,1},{3,2},{4,3},{5,4},{6,5},{7,6},{8,7},{9,8},{10,9},{11,1... | collective-permute-start | bytes 1081352 | tf_op jit(solution)/shard_map/ppermute | solution.py:221

commit v5 on v4

--- a/solution.py
+++ b/solution.py
@@ -16,9 +16,6 @@
 RIM = (7, 7, 8)
 RIMS = sum(RIM)
 FROM = (0, 7, 14)
-COEF_RIM = (8, 6, 6)
-COEF_FROM = (0, 8, 14)
-COEF_RIMS = sum(COEF_RIM)
 CHUNKS = ((0, 2), (2, 4))
 
 VM = pl.BlockSpec(memory_space=pltpu.VMEM)
@@ -46,17 +43,18 @@
                 out[:, q, f, t] = state[p, f, t]
 
 
-def coef_kernel(depth, coriolis, drag, own, top, bottom):
-    rows, tiles = own.shape[1:3]
-    for r in range(rows):
-        at = pl.ds(r // SUB * tiles * SUB + r % SUB, tiles, stride=SUB)
-        values = ((0.5 * DT) * depth[at, :], DT * coriolis[at, :], 1.0 / (1.0 + DT * drag[at, :]))
-        for n, value in enumerate(values):
-            own[n, r] = value
-            if r < COEF_RIM[n]:
-                top[COEF_FROM[n] + r] = value
-            if r >= rows - COEF_RIM[n]:
-                bottom[COEF_FROM[n] + r - (rows - COEF_RIM[n])] = value
+def coef_kernel(depth, coriolis, drag, above, below, out):
+    tiles = out.shape[2]
+    bands = depth.shape[0] // (tiles * SUB)
+    for r in range(out.shape[1]):
+        band, row = r // SUB - 1, r % SUB
+        values = []
+        for n, own in enumerate((depth, coriolis, drag)):
+            ref, at = (above, n) if band < 0 else (below, n) if band == bands else (own, band)
+            values.append(ref[pl.ds(at * tiles * SUB + row, tiles, stride=SUB), :])
+        out[0, r] = (0.5 * DT) * values[0]
+        out[1, r] = DT * values[1]
+        out[2, r] = 1.0 / (1.0 + DT * values[2])
 
 
 def pick_kernel(members, low, high, table, got, out):
@@ -84,7 +82,7 @@
                     bottom[k - low, FROM[f] + r - (rows - RIM[f])] = value
 
 
-def step_kernel(size, fields, above, below, coef, coef_rims, *rest):
+def step_kernel(size, fields, above, below, coef, *rest):
     out, *held = rest[-4:]
     kinds, rows, tiles = fields.shape[1:4]
     lane = lax.broadcasted_iota(jnp.int32, (tiles, LANES), 1)
@@ -100,11 +98,7 @@
         return jnp.where(wall_last, edge, after) - jnp.where(wall_first, edge, before)
 
     def const(n, r):
-        if r < 0:
-            return coef_rims[0, COEF_FROM[n] + r + COEF_RIM[n]]
-        if r >= rows:
-            return coef_rims[1, COEF_FROM[n] + r - rows]
-        return coef[n, r]
+        return coef[n, r + DEEP]
 
     def particle(k, carry):
         def get(n, f, r):
@@ -153,7 +147,7 @@
     f32 = jnp.float32
 
     def tiled(x):
-        x = x.reshape(x.shape[:-2] + (bands, SUB, tiles, LANES))
+        x = x.reshape(x.shape[:-2] + (x.shape[-2] // SUB, SUB, tiles, LANES))
         return jnp.swapaxes(x, -3, -2)
 
     state_t, jitter_t = tiled(state), tiled(jitter)
@@ -166,6 +160,9 @@
         compiler_params=PARAMS,
         name="pack",
     )(ancestor, state_t)
+    pieces = lax.all_to_all(packed, "dom", 0, 0, tiled=True)
+    pieces = pieces.reshape(blocks * CAP, kinds * rows, LANES)
+
     slot = jnp.arange(ancestor.shape[0], dtype=jnp.int32)
     moved = ancestor != slot
     donor = jnp.any((ancestor[:, None] == slot[None, :]) & moved[:, None], axis=0)
@@ -175,23 +172,21 @@
     table = jnp.sum(jnp.where(ancestor[:, None] == slot[None, :], place[None, :], 0), axis=1)
     kept = lax.dynamic_slice_in_dim(jnp.where(moved, 0, 1).astype(jnp.int32), me * members, members)
 
-    rim = jax.ShapeDtypeStruct((COEF_RIMS, tiles, LANES), f32)
-    coef, coef_top, coef_bottom = pl.pallas_call(
+    raw = (depth, coriolis, drag)
+    rim_above = lax.ppermute(jnp.stack([x[rows - DEEP :] for x in raw]), "space", down)
+    rim_below = lax.ppermute(jnp.stack([x[:DEEP] for x in raw]), "space", up)
+    coef = pl.pallas_call(
         coef_kernel,
-        in_specs=[VM] * 3,
-        out_specs=(VM, VM, VM),
-        out_shape=(jax.ShapeDtypeStruct((3, rows, tiles, LANES), f32), rim, rim),
+        in_specs=[VM] * 5,
+        out_specs=VM,
+        out_shape=jax.ShapeDtypeStruct((3, rows + 2 * DEEP, tiles, LANES), f32),
         compiler_params=PARAMS,
         name="coef",
-    )(*(tiled(x).reshape(rows * tiles, LANES) for x in (depth, coriolis, drag)))
-    packed, coef_top, coef_bottom = lax.optimization_barrier((packed, coef_top, coef_bottom))
-    pieces = lax.all_to_all(packed, "dom", 0, 0, tiled=True)
-    pieces = pieces.reshape(blocks * CAP, kinds * rows, LANES)
-
-    coef_rims = jnp.stack(
-        [lax.ppermute(coef_bottom, "space", down), lax.ppermute(coef_top, "space", up)]
+    )(
+        *(tiled(x).reshape(rows * tiles, LANES) for x in raw),
+        *(tiled(x).reshape(3 * DEEP * tiles, LANES) for x in (rim_above, rim_below)),
     )
-    pieces, table, kept = lax.optimization_barrier((pieces, table, kept))
+    pieces, coef, table, kept = lax.optimization_barrier((pieces, coef, table, kept))
 
     chosen = pl.pallas_call(
         functools.partial(pick_kernel, members, 0, members),
@@ -202,7 +197,6 @@
         name="pick",
     )(table, pieces)
     routed = lax.all_to_all(chosen, "dom", 0, 0, tiled=True).reshape(-1, LANES)
-    routed, coef_rims = lax.optimization_barrier((routed, coef_rims))
 
     out = None
     chunks = []
@@ -227,14 +221,14 @@
         out = pl.pallas_call(
             functools.partial(step_kernel, size),
             grid=(1,),
-            in_specs=[VM] * 5 + ([] if out is None else [HB]),
+            in_specs=[VM] * 4 + ([] if out is None else [HB]),
             out_specs=done,
             out_shape=jax.ShapeDtypeStruct((members, kinds, rows * tiles, LANES), f32),
             scratch_shapes=[pltpu.VMEM((STEPS, rows + 2 * DEEP, tiles, LANES), f32)] * 3,
-            input_output_aliases={} if out is None else {5: 0},
+            input_output_aliases={} if out is None else {4: 0},
             compiler_params=PARAMS,
             name="steps",
-        )(fields, above, below, coef, coef_rims, *([] if out is None else [out]))
+        )(fields, above, below, coef, *([] if out is None else [out]))
     out = out.reshape(members, kinds, bands, tiles, SUB, LANES)
     return jnp.swapaxes(out, -3, -2).reshape(state.shape)
 

time: 84 us -> 82 us (0.976)
  blocking collectives: 0 us -> 24.6 us
  waiting for transfers between devices: 34.2 us -> 15 us
  starting transfers between devices: 32.6 us -> 24.8 us
    all_to_all x0 -> x1, blocking collectives: none -> 24.6 us  [local(): routed = lax.all_to_all(chosen, 'dom', 0, 0, tiled=True).reshape(-1, LANES)]
    all_to_all x1 -> x0, waiting for transfers between devices: 8.43 us -> none  [local(): routed = lax.all_to_all(chosen, 'dom', 0, 0, tiled=True).reshape(-1, LANES)]
    ppermute x2, waiting for transfers between devices: 6.6 us -> 0.01 us  [the longest x1 0.01 us: local(): lax.ppermute(jnp.stack([x[rows - DEEP:] for x in raw]), 'space', down)]
    all_to_all x1 -> x0, starting transfers between devices: 4.74 us -> none  [local(): routed = lax.all_to_all(chosen, 'dom', 0, 0, tiled=True).reshape(-1, LANES)]
    all_to_all x1, waiting for transfers between devices: 12.1 us -> 8.74 us  [local(): pieces = lax.all_to_all(packed, 'dom', 0, 0, tiled=True)]
    ppermute x2, starting transfers between devices: 12.9 us -> 10.1 us  [local(): below = lax.ppermute(top, 'space', up)]
    unnamed x22 -> x20, local copies, waits for them, and re-layouts: 5.37 us -> 3.23 us
    another operation x0 -> x2, local copies, waits for them, and re-layouts: none -> 1.96 us  [local(): rim_below = lax.ppermute(jnp.stack([x[:DEEP] for x in raw]), 'space', up)]
  transfers between devices with their start and end apart: 8 -> 7, of which waited for: 5 -> 3; matrix products, arithmetic and copies ran while one was open for 1% -> 1% of each run, Pallas kernels for 5% -> 7%
where the time goes in v5:
time: 82 us; the launch traced here: 81.6 us
  starting transfers between devices  24.8 us (30%)
  blocking collectives  24.6 us (30%)
  waiting for transfers between devices  15 us (18%)
  Pallas kernels  10.7 us (13%)
  local copies, waits for them, and re-layouts  5.26 us (6%)
  other arithmetic  1.1 us (1%)
    all_to_all x1, blocking collectives, local(): routed = lax.all_to_all(chosen, 'dom', 0, 0, tiled=True).reshape(-1, LANES)  24.6 us
    ppermute x2, starting transfers between devices, local(): below = lax.ppermute(top, 'space', up)  10.1 us
    all_to_all x1, waiting for transfers between devices, local(): pieces = lax.all_to_all(packed, 'dom', 0, 0, tiled=True)  8.74 us
    ppermute x1, starting transfers between devices, local(): rim_below = lax.ppermute(jnp.stack([x[:DEEP] for x in raw]), 'space', up)  6.58 us
    ppermute x2, waiting for transfers between devices, local(): above = lax.ppermute(bottom, 'space', down)  6.26 us
    pallas_call x2, Pallas kernels, local(): pl.pallas_call(functools.partial(step_kernel, size), grid=(1,), in_specs=...  5.5 us
    all_to_all x1, starting transfers between devices, local(): pieces = lax.all_to_all(packed, 'dom', 0, 0, tiled=True)  5.38 us
    unnamed x20, local copies, waits for them, and re-layouts  3.23 us
  transfers between devices with their start and end apart: 7, of which 3 were waited for; matrix products, arithmetic and copies ran while one was open for 1% of the time, Pallas kernels for 7%

profile of v5, /device:TPU:1, one launch (start us, length us, event | category | flops | bytes accessed | tf_op | source)
XLA Modules:
  0.0 81.6 jit_solution(341145821315680545)
XLA Ops:
  0.0 1.0 %slice_bitcast_fusion.2 = (f32[1,8,2048]{2,1,0:T(8,128)S(1)}, f32[1,8,2048]{2,1,0:T(8,128)S(1)}) fusion(f32[16,2048]{1,0:T(8,128)} %param.9), kind=kLoop, calls=%fused_computation.4 | loop fusion | bytes 262144 | tf_op jit(solution)/shard_map/stack | solution.py:177
  1.0 1.0 %slice_bitcast_fusion = (f32[1,8,2048]{2,1,0:T(8,128)S(1)}, f32[1,8,2048]{2,1,0:T(8,128)S(1)}, f32[1,8,2048]{2,1,0:T(8,128)S(1)}, f32[1,8,2048]{2,1,0:T(8,128)S(1)}) fusion(f32[16,2048]{1,0:T(8,128)} %param.11, f32[16,2048]{1,0:T(8,128)} %param.10), kind=kLoop, calls=%fused_computation.2 | loop fusion | bytes 524288 | tf_op jit(solution)/shard_map/stack | solution.py:177
  2.0 2.5 %collective-permute-start = (f32[3,8,2048]{2,1,0:T(8,128)S(1)}, f32[3,8,2048]{2,1,0:T(8,128)S(1)}, u32[]{:S(2)}, u32[]{:S(2)}) collective-permute-start(f32[3,8,2048]{2,1,0:T(8,128)S(1)} %pad_maximum_fusion), channel_id=1, source_target_pairs={{0,1},{1,2},{2,3},{3,4},{4,5},{5,6},{6,7},{7,8},{8,9},{9,10},{10,1... | collective-permute-start | bytes 589832 | tf_op jit(solution)/shard_map/ppermute | solution.py:176
  4.5 0.7 pad_maximum_fusion.1
  5.2 6.6 %collective-permute-start.1 = (f32[3,8,2048]{2,1,0:T(8,128)}, f32[3,8,2048]{2,1,0:T(8,128)S(1)}, u32[]{:S(2)}, u32[]{:S(2)}) collective-permute-start(f32[3,8,2048]{2,1,0:T(8,128)} %pad_maximum_fusion.1), channel_id=1, source_target_pairs={{1,0},{2,1},{3,2},{4,3},{5,4},{6,5},{7,6},{8,7},{9,8},{10,9},{11,1... | collective-permute-start | bytes 589832 | tf_op jit(solution)/shard_map/ppermute | solution.py:177
  11.8 0.0 copy-start.4
  11.8 2.0 %pack.1 = f32[16,2,3,2,8,128]{5,4,3,2,1,0:T(8,128)} custom-call(s32[64]{0:T(128)S(1)} %copy-done.9, f32[4,3,2,16,8,128]{5,4,3,2,1,0:T(8,128)S(1)} %bitcast.54), custom_call_target="tpu_custom_call" | custom-call | tf_op jit(solution)/shard_map/pack/pallas_call | solution.py:155
  13.8 5.4 %all-to-all-start = ((f32[16,2,3,2,8,128]{5,4,3,2,1,0:T(8,128)}), f32[16,2,3,2,8,128]{5,4,3,2,1,0:T(8,128)S(1)}, u32[]{:S(2)}, u32[]{:S(2)}) async-start(f32[16,2,3,2,8,128]{5,4,3,2,1,0:T(8,128)} %pack.1), calls=%async_computation | async-start | bytes 1572864 | tf_op jit(solution)/shard_map/all_to_all | solution.py:163
  19.2 0.1 fusion.1
  19.3 0.1 fusion.4
  19.4 0.1 dynamic_slice.3.kept
  19.5 0.2 select_reduce_fusion.table
  19.7 0.0 collective-permute-done
  19.7 0.7 copy-done.5
  20.4 0.7 copy-done.7
  21.1 0.9 %copy-done.6 = f32[3,8,2048]{2,1,0:T(8,128)S(1)} copy-done((f32[3,8,2048]{2,1,0:T(8,128)S(1)}, f32[3,8,2048]{2,1,0:T(8,128)}, u32[]{:S(2)}) %copy-start.6) | copy-done | bytes 196632
  22.0 0.9 %copy-done.8 = f32[3,8,2048]{2,1,0:T(8,128)S(1)} copy-done((f32[3,8,2048]{2,1,0:T(8,128)S(1)}, f32[3,8,2048]{2,1,0:T(8,128)}, u32[]{:S(2)}) %copy-start.8) | copy-done | bytes 196632
  22.9 0.2 coef.1
  23.1 8.7 %all-to-all-done = f32[16,2,3,2,8,128]{5,4,3,2,1,0:T(8,128)S(1)} async-done(((f32[16,2,3,2,8,128]{5,4,3,2,1,0:T(8,128)}), f32[16,2,3,2,8,128]{5,4,3,2,1,0:T(8,128)S(1)}, u32[]{:S(2)}, u32[]{:S(2)}) %all-to-all-start) | async-done | bytes 786464 | tf_op jit(solution)/shard_map/all_to_all | solution.py:163
  31.8 0.6 pick.1
  32.5 0.0 copy-start.1
  32.5 24.6 %all_to_all.10 = f32[16,4,48,128]{3,2,1,0:T(8,128)S(1)} all-to-all(f32[16,4,48,128]{3,2,1,0:T(8,128)S(1)} %pick.1), channel_id=1, replica_groups=mesh['dom'=16,'space'=16] {'dom'}, dimensions={0} | all-to-all | bytes 3145728 | tf_op jit(solution)/shard_map/all_to_all | solution.py:199
  57.1 1.2 %prep.3 = (f32[2,3,16,16,128]{4,3,2,1,0:T(8,128)S(1)}, f32[2,22,16,128]{3,2,1,0:T(8,128)S(1)}, f32[2,22,16,128]{3,2,1,0:T(8,128)S(1)}) custom-call(s32[4]{0:T(128)S(1)} %dynamic_slice.3.kept, f32[3072,128]{1,0:T(8,128)S(1)} %bitcast.57, f32[3072,128]{1,0:T(8,128)S(1)} %bitcast.55, f32[3072,128]{1,0:T(8,128)S(1)} %bitcast.59), custom_call_target="tpu_custom_call" | custom-call | tf_op jit(solution)/shard_map/prep/pallas_call | solution.py:206
  58.3 0.1 collective-permute-start.4
  58.4 5.1 %collective-permute-start.5 = (f32[2,22,16,128]{3,2,1,0:T(8,128)S(1)}, f32[2,22,16,128]{3,2,1,0:T(8,128)S(1)}, u32[]{:S(2)}, u32[]{:S(2)}) collective-permute-start(f32[2,22,16,128]{3,2,1,0:T(8,128)S(1)} %get-tuple-element.24), channel_id=1, source_target_pairs={{1,0},{2,1},{3,2},{4,3},{5,4},{6,5},{7,6},{8,7},{9,8},{10,9},{11,1... | collective-permute-start | bytes 1081352 | tf_op jit(solution)/shard_map/ppermute | solution.py:215
  63.5 1.2 %prep.2 = (f32[2,3,16,16,128]{4,3,2,1,0:T(8,128)S(1)}, f32[2,22,16,128]{3,2,1,0:T(8,128)S(1)}, f32[2,22,16,128]{3,2,1,0:T(8,128)S(1)}) custom-call(s32[4]{0:T(128)S(1)} %dynamic_slice.3.kept, f32[3072,128]{1,0:T(8,128)S(1)} %bitcast.58, f32[3072,128]{1,0:T(8,128)S(1)} %bitcast.56, f32[3072,128]{1,0:T(8,128)S(1)} %bitcast.60), custom_call_target="tpu_custom_call" | custom-call | tf_op jit(solution)/shard_map/prep/pallas_call | solution.py:206
  64.7 0.1 collective-permute-start.2
  64.8 5.1 %collective-permute-start.3 = (f32[2,22,16,128]{3,2,1,0:T(8,128)S(1)}, f32[2,22,16,128]{3,2,1,0:T(8,128)S(1)}, u32[]{:S(2)}, u32[]{:S(2)}) collective-permute-start(f32[2,22,16,128]{3,2,1,0:T(8,128)S(1)} %get-tuple-element.20), channel_id=1, source_target_pairs={{1,0},{2,1},{3,2},{4,3},{5,4},{6,5},{7,6},{8,7},{9,8},{10,9},{11,1... | collective-permute-start | bytes 1081352 | tf_op jit(solution)/shard_map/ppermute | solution.py:215
  69.9 0.7 collective-permute-done.4.above
  70.6 2.8 %steps.2.rest_0_ = f32[4,3,256,128]{3,2,1,0:T(8,128)} custom-call(f32[2,3,16,16,128]{4,3,2,1,0:T(8,128)S(1)} %get-tuple-element.22.fields, f32[2,22,16,128]{3,2,1,0:T(8,128)S(1)} %collective-permute-done.4.above, f32[2,22,16,128]{3,2,1,0:T(8,128)S(1)} %collective-permute-done.5.below, f32[3,32,16,128]{3,2,1,0:T(8,128)S(1)} %coef.1), custom_call_target="tpu_custom_call" | custom-call | tf_op jit(solution)/shard_map/steps/pallas_call | solution.py:221
  73.4 5.5 %collective-permute-done.2.above = f32[2,22,16,128]{3,2,1,0:T(8,128)S(1)} collective-permute-done((f32[2,22,16,128]{3,2,1,0:T(8,128)S(1)}, f32[2,22,16,128]{3,2,1,0:T(8,128)S(1)}, u32[]{:S(2)}, u32[]{:S(2)}) %collective-permute-start.2) | collective-permute-done | bytes 360480 | tf_op jit(solution)/shard_map/ppermute | solution.py:214
  78.9 2.7 %steps.3 = f32[4,3,256,128]{3,2,1,0:T(8,128)} custom-call(f32[2,3,16,16,128]{4,3,2,1,0:T(8,128)S(1)} %get-tuple-element.18.fields, f32[2,22,16,128]{3,2,1,0:T(8,128)S(1)} %collective-permute-done.2.above, f32[2,22,16,128]{3,2,1,0:T(8,128)S(1)} %collective-permute-done.3.below, f32[3,32,16,128]{3,2,1,0:T(8,128)S(1)} %coef.1, ...), custom_call_target="tpu_custom_call", output_to_operand_aliasing={{}: (4, {})} | custom-call | tf_op jit(solution)/shard_map/steps/pallas_call | solution.py:221
  (22 shorter events, 0.1 us)
Async XLA Ops:
  0.0 11.8 %copy-start.9 = (s32[64]{0:T(128)S(1)}, s32[64]{0:T(128)}, u32[]{:S(2)}) copy-start(s32[64]{0:T(128)} %anc.1) | copy-start | bytes 772
  0.0 11.8 %copy-start = (f32[4,3,16,2048]{3,2,1,0:T(8,128)S(1)}, f32[4,3,16,2048]{3,2,1,0:T(8,128)}, u32[]{:S(2)}) copy-start(f32[4,3,16,2048]{3,2,1,0:T(8,128)} %param.7) | copy-start | bytes 4718596
  2.0 17.7 %collective-permute-start = (f32[3,8,2048]{2,1,0:T(8,128)S(1)}, f32[3,8,2048]{2,1,0:T(8,128)S(1)}, u32[]{:S(2)}, u32[]{:S(2)}) collective-permute-start(f32[3,8,2048]{2,1,0:T(8,128)S(1)} %pad_maximum_fusion), channel_id=1, source_target_pairs={{0,1},{1,2},{2,3},{3,4},{4,5},{5,6},{6,7},{7,8},{8,9},{9,10},{10,1... | collective-permute-start | bytes 589832 | tf_op jit(solution)/shard_map/ppermute | solution.py:176
  5.2 15.1 %collective-permute-start.1 = (f32[3,8,2048]{2,1,0:T(8,128)}, f32[3,8,2048]{2,1,0:T(8,128)S(1)}, u32[]{:S(2)}, u32[]{:S(2)}) collective-permute-start(f32[3,8,2048]{2,1,0:T(8,128)} %pad_maximum_fusion.1), channel_id=1, source_target_pairs={{1,0},{2,1},{3,2},{4,3},{5,4},{6,5},{7,6},{8,7},{9,8},{10,9},{11,1... | collective-permute-start | bytes 589832 | tf_op jit(solution)/shard_map/ppermute | solution.py:177
  11.8 9.2 %copy-start.2 = (f32[16,2048]{1,0:T(8,128)S(1)}, f32[16,2048]{1,0:T(8,128)}, u32[]{:S(2)}) copy-start(f32[16,2048]{1,0:T(8,128)} %param.9) | copy-start | bytes 393220
  11.8 9.2 %copy-start.3 = (f32[16,2048]{1,0:T(8,128)S(1)}, f32[16,2048]{1,0:T(8,128)}, u32[]{:S(2)}) copy-start(f32[16,2048]{1,0:T(8,128)} %param.10) | copy-start | bytes 393220
  11.8 9.2 %copy-start.4 = (f32[16,2048]{1,0:T(8,128)S(1)}, f32[16,2048]{1,0:T(8,128)}, u32[]{:S(2)}) copy-start(f32[16,2048]{1,0:T(8,128)} %param.11) | copy-start | bytes 393220
  13.8 18.0 %all-to-all-start = ((f32[16,2,3,2,8,128]{5,4,3,2,1,0:T(8,128)}), f32[16,2,3,2,8,128]{5,4,3,2,1,0:T(8,128)S(1)}, u32[]{:S(2)}, u32[]{:S(2)}) async-start(f32[16,2,3,2,8,128]{5,4,3,2,1,0:T(8,128)} %pack.1), calls=%async_computation | async-start | bytes 1572864 | tf_op jit(solution)/shard_map/all_to_all | solution.py:163
  19.7 0.7 copy-start.5
  20.4 0.7 copy-start.7
  21.1 0.9 %copy-start.6 = (f32[3,8,2048]{2,1,0:T(8,128)S(1)}, f32[3,8,2048]{2,1,0:T(8,128)}, u32[]{:S(2)}) copy-start(f32[3,8,2048]{2,1,0:T(8,128)} %copy-done.5) | copy-start | bytes 589828
  22.0 0.9 %copy-start.8 = (f32[3,8,2048]{2,1,0:T(8,128)S(1)}, f32[3,8,2048]{2,1,0:T(8,128)}, u32[]{:S(2)}) copy-start(f32[3,8,2048]{2,1,0:T(8,128)} %copy-done.7) | copy-start | bytes 589828
  32.5 24.6 %copy-start.1 = (f32[4,3,16,2048]{3,2,1,0:T(8,128)S(1)}, f32[4,3,16,2048]{3,2,1,0:T(8,128)}, u32[]{:S(2)}) copy-start(f32[4,3,16,2048]{3,2,1,0:T(8,128)} %param.8) | copy-start | bytes 4718596
  58.3 12.2 %collective-permute-start.4 = (f32[2,22,16,128]{3,2,1,0:T(8,128)S(1)}, f32[2,22,16,128]{3,2,1,0:T(8,128)S(1)}, u32[]{:S(2)}, u32[]{:S(2)}) collective-permute-start(f32[2,22,16,128]{3,2,1,0:T(8,128)S(1)} %get-tuple-element.23), channel_id=1, source_target_pairs={{0,1},{1,2},{2,3},{3,4},{4,5},{5,6},{6,7},{7,8},{8,9},{9,10},{10,1... | collective-permute-start | bytes 1081352 | tf_op jit(solution)/shard_map/ppermute | solution.py:214
  58.4 12.2 %collective-permute-start.5 = (f32[2,22,16,128]{3,2,1,0:T(8,128)S(1)}, f32[2,22,16,128]{3,2,1,0:T(8,128)S(1)}, u32[]{:S(2)}, u32[]{:S(2)}) collective-permute-start(f32[2,22,16,128]{3,2,1,0:T(8,128)S(1)} %get-tuple-element.24), channel_id=1, source_target_pairs={{1,0},{2,1},{3,2},{4,3},{5,4},{6,5},{7,6},{8,7},{9,8},{10,9},{11,1... | collective-permute-start | bytes 1081352 | tf_op jit(solution)/shard_map/ppermute | solution.py:215
  64.7 14.2 %collective-permute-start.2 = (f32[2,22,16,128]{3,2,1,0:T(8,128)S(1)}, f32[2,22,16,128]{3,2,1,0:T(8,128)S(1)}, u32[]{:S(2)}, u32[]{:S(2)}) collective-permute-start(f32[2,22,16,128]{3,2,1,0:T(8,128)S(1)} %get-tuple-element.19), channel_id=1, source_target_pairs={{0,1},{1,2},{2,3},{3,4},{4,5},{5,6},{6,7},{7,8},{8,9},{9,10},{10,1... | collective-permute-start | bytes 1081352 | tf_op jit(solution)/shard_map/ppermute | solution.py:214
  64.8 14.1 %collective-permute-start.3 = (f32[2,22,16,128]{3,2,1,0:T(8,128)S(1)}, f32[2,22,16,128]{3,2,1,0:T(8,128)S(1)}, u32[]{:S(2)}, u32[]{:S(2)}) collective-permute-start(f32[2,22,16,128]{3,2,1,0:T(8,128)S(1)} %get-tuple-element.20), channel_id=1, source_target_pairs={{1,0},{2,1},{3,2},{4,3},{5,4},{6,5},{7,6},{8,7},{9,8},{10,9},{11,1... | collective-permute-start | bytes 1081352 | tf_op jit(solution)/shard_map/ppermute | solution.py:215

commit v6 on v5

--- a/solution.py
+++ b/solution.py
@@ -24,7 +24,7 @@
 PARAMS = pltpu.CompilerParams(vmem_limit_bytes=24 << 20)
 
 
-def pack_kernel(members, anc, state, out):
+def pack_kernel(members, anc, state, out, sem):
     me = lax.axis_index("dom")
     bits = jnp.int32(0)
     for j in range(anc.shape[0]):
@@ -37,21 +37,45 @@
     second = jnp.int32(members - 1)
     for k in reversed(range(members)):
         second = jnp.where(((bits >> k) & 1 == 1) & (k != first), k, second)
+    copies = []
     for q, p in enumerate((first, second)):
         for f in range(state.shape[1]):
             for t in range(state.shape[2]):
-                out[:, q, f, t] = state[p, f, t]
-
-
-def coef_kernel(depth, coriolis, drag, above, below, out):
+                copies.append(
+                    pltpu.make_async_copy(state.at[p, f, t], out.at[:, q, f, t], sem.at[len(copies)])
+                )
+    for c in copies:
+        c.start()
+    for c in copies:
+        c.wait()
+
+
+def rim_kernel(depth, coriolis, drag, first, second, sem):
+    toward = 1 - lax.axis_index("space") % 2
+    last = depth.shape[0] - 1
+    copies = []
+    for n, ref in enumerate((depth, coriolis, drag)):
+        for out, at in ((first, toward * last), (second, (1 - toward) * last)):
+            copies.append(pltpu.make_async_copy(ref.at[at], out.at[n], sem.at[len(copies)]))
+    for c in copies:
+        c.start()
+    for c in copies:
+        c.wait()
+
+
+def coef_kernel(depth, coriolis, drag, first, second, out):
     tiles = out.shape[2]
     bands = depth.shape[0] // (tiles * SUB)
+    odd = lax.axis_index("space") % 2 == 1
     for r in range(out.shape[1]):
         band, row = r // SUB - 1, r % SUB
         values = []
         for n, own in enumerate((depth, coriolis, drag)):
-            ref, at = (above, n) if band < 0 else (below, n) if band == bands else (own, band)
-            values.append(ref[pl.ds(at * tiles * SUB + row, tiles, stride=SUB), :])
+            if 0 <= band < bands:
+                values.append(own[pl.ds(band * tiles * SUB + row, tiles, stride=SUB), :])
+            else:
+                at = pl.ds(n * tiles * SUB + row, tiles, stride=SUB)
+                values.append(jnp.where(odd == (band < 0), first[at, :], second[at, :]))
         out[0, r] = (0.5 * DT) * values[0]
         out[1, r] = DT * values[1]
         out[2, r] = 1.0 / (1.0 + DT * values[2])
@@ -64,25 +88,28 @@
             out[d, k - low] = got[at]
 
 
-def prep_kernel(members, low, high, kept, routed, state, jitter, fields, top, bottom):
+def prep_kernel(members, low, high, kept, routed, state, jitter, fields, first, second):
     kinds, rows, tiles = fields.shape[1:4]
     slab = kinds * rows
+    odd = lax.axis_index("space") % 2 == 1
     for k in range(low, high):
         mine = kept[k] == 1
         for f in range(kinds):
+            values = []
             for r in range(rows):
                 far = pl.ds(k * slab + f * rows + r, tiles, stride=members * slab)
                 t = (k * kinds + f) * (rows // SUB) + r // SUB
                 near = pl.ds(t * tiles * SUB + r % SUB, tiles, stride=SUB)
                 value = jnp.where(mine, state[near, :], routed[far, :]) + jitter[near, :]
                 fields[k - low, f, r] = value
-                if r < RIM[f]:
-                    top[k - low, FROM[f] + r] = value
-                if r >= rows - RIM[f]:
-                    bottom[k - low, FROM[f] + r - (rows - RIM[f])] = value
-
-
-def step_kernel(size, fields, above, below, coef, *rest):
+                values.append(value)
+            for r in range(RIM[f]):
+                top, bottom = values[r], values[rows - RIM[f] + r]
+                first[k - low, FROM[f] + r] = jnp.where(odd, top, bottom)
+                second[k - low, FROM[f] + r] = jnp.where(odd, bottom, top)
+
+
+def step_kernel(size, fields, first, second, coef, *rest):
     out, *held = rest[-4:]
     kinds, rows, tiles = fields.shape[1:4]
     lane = lax.broadcasted_iota(jnp.int32, (tiles, LANES), 1)
@@ -91,6 +118,7 @@
     wall_first = lane_first & (tile == 0)
     wall_last = lane_last & (tile == tiles - 1)
     half = 0.5 * DT
+    odd = lax.axis_index("space") % 2 == 1
 
     def difference(x, edge):
         before = pltpu.roll(jnp.where(lane_last, pltpu.roll(x, 1, 0), x), 1, 1)
@@ -104,11 +132,10 @@
         def get(n, f, r):
             if n:
                 return held[f][n - 1, r + DEEP]
-            if r < 0:
-                return above[k, FROM[f] + r + RIM[f]]
-            if r >= rows:
-                return below[k, FROM[f] + r - rows]
-            return fields[k, f, r]
+            if 0 <= r < rows:
+                return fields[k, f, r]
+            at = FROM[f] + (r + RIM[f] if r < 0 else r - rows)
+            return jnp.where(odd == (r < 0), first[k, at], second[k, at])
 
         def put(n, f, r, value):
             if n < STEPS or f == 0:
@@ -141,8 +168,8 @@
     tiles, bands = width // LANES, rows // SUB
     blocks = lax.axis_size("dom")
     count = lax.axis_size("space")
-    down = [(i, (i + 1) % count) for i in range(count)]
-    up = [((i + 1) % count, i) for i in range(count)]
+    swap_first = [(i, i ^ 1) for i in range(count)]
+    swap_second = [(i, (i + 2 * (i % 2) - 1) % count) for i in range(count)]
     me = lax.axis_index("dom")
     f32 = jnp.float32
 
@@ -154,12 +181,13 @@
 
     packed = pl.pallas_call(
         functools.partial(pack_kernel, members),
-        in_specs=[SM, VM],
-        out_specs=VM,
+        in_specs=[SM, HB],
+        out_specs=HB,
         out_shape=jax.ShapeDtypeStruct((tiles, CAP, kinds, bands, SUB, LANES), f32),
+        scratch_shapes=[pltpu.SemaphoreType.DMA((CAP * kinds * bands,))],
         compiler_params=PARAMS,
         name="pack",
-    )(ancestor, state_t)
+    )(ancestor, pltpu.with_memory_space_constraint(state_t, pltpu.HBM))
     pieces = lax.all_to_all(packed, "dom", 0, 0, tiled=True)
     pieces = pieces.reshape(blocks * CAP, kinds * rows, LANES)
 
@@ -173,8 +201,17 @@
     kept = lax.dynamic_slice_in_dim(jnp.where(moved, 0, 1).astype(jnp.int32), me * members, members)
 
     raw = (depth, coriolis, drag)
-    rim_above = lax.ppermute(jnp.stack([x[rows - DEEP :] for x in raw]), "space", down)
-    rim_below = lax.ppermute(jnp.stack([x[:DEEP] for x in raw]), "space", up)
+    rim = jax.ShapeDtypeStruct((3, tiles, SUB, LANES), f32)
+    rims = pl.pallas_call(
+        rim_kernel,
+        in_specs=[HB] * 3,
+        out_specs=(VM, VM),
+        out_shape=(rim, rim),
+        scratch_shapes=[pltpu.SemaphoreType.DMA((6,))],
+        compiler_params=PARAMS,
+        name="rims",
+    )(*(pltpu.with_memory_space_constraint(tiled(x), pltpu.HBM) for x in raw))
+    rims = (lax.ppermute(rims[0], "space", swap_first), lax.ppermute(rims[1], "space", swap_second))
     coef = pl.pallas_call(
         coef_kernel,
         in_specs=[VM] * 5,
@@ -184,7 +221,7 @@
         name="coef",
     )(
         *(tiled(x).reshape(rows * tiles, LANES) for x in raw),
-        *(tiled(x).reshape(3 * DEEP * tiles, LANES) for x in (rim_above, rim_below)),
+        *(x.reshape(3 * tiles * SUB, LANES) for x in rims),
     )
     pieces, coef, table, kept = lax.optimization_barrier((pieces, coef, table, kept))
 
@@ -203,7 +240,7 @@
     for low, high in CHUNKS:
         size = high - low
         rim = jax.ShapeDtypeStruct((size, RIMS, tiles, LANES), f32)
-        fields, top, bottom = pl.pallas_call(
+        fields, first, second = pl.pallas_call(
             functools.partial(prep_kernel, members, low, high),
             in_specs=[SM, VM, VM, VM],
             out_specs=(VM, VM, VM),
@@ -211,11 +248,11 @@
             compiler_params=PARAMS,
             name="prep",
         )(kept, routed, state_t.reshape(-1, LANES), jitter_t.reshape(-1, LANES))
-        above = lax.ppermute(bottom, "space", down)
-        below = lax.ppermute(top, "space", up)
-        chunks.append((fields, above, below))
-
-    for (low, high), (fields, above, below) in zip(CHUNKS, chunks):
+        first = lax.ppermute(first, "space", swap_first)
+        second = lax.ppermute(second, "space", swap_second)
+        chunks.append((fields, first, second))
+
+    for (low, high), (fields, first, second) in zip(CHUNKS, chunks):
         size = high - low
         done = pl.BlockSpec((size, kinds, rows * tiles, LANES), lambda i, at=low // size: (at, 0, 0, 0))
         out = pl.pallas_call(
@@ -228,7 +265,7 @@
             input_output_aliases={} if out is None else {4: 0},
             compiler_params=PARAMS,
             name="steps",
-        )(fields, above, below, coef, *([] if out is None else [out]))
+        )(fields, first, second, coef, *([] if out is None else [out]))
     out = out.reshape(members, kinds, bands, tiles, SUB, LANES)
     return jnp.swapaxes(out, -3, -2).reshape(state.shape)
 

time: 82 us -> 106 us (1.29)
  Pallas kernels: 10.7 us -> 36.1 us
  waiting for transfers between devices: 15 us -> 22.4 us
  local copies, waits for them, and re-layouts: 5.26 us -> 0.76 us
  starting transfers between devices: 24.8 us -> 21 us
    pallas_call x1 -> x2, Pallas kernels: 1.96 us -> 27.1 us  [the longest x1 26 us: local(): pl.pallas_call(functools.partial(pack_kernel, members), in_specs=[SM, HB]...]
    ppermute x6, waiting for transfers between devices: 6.27 us -> 10.5 us  [the longest x2 7.43 us: local(): second = lax.ppermute(second, 'space', swap_second)]
    ppermute x6, starting transfers between devices: 19.4 us -> 15.3 us  [the longest x1 7.3 us: local(): lax.ppermute(rims[1], 'space', swap_second)]
    all_to_all x1, waiting for transfers between devices: 8.74 us -> 11.8 us  [local(): pieces = lax.all_to_all(packed, 'dom', 0, 0, tiled=True)]
    unnamed x20 -> x14, local copies, waits for them, and re-layouts: 3.23 us -> 0.68 us
    another operation x2 -> x0, local copies, waits for them, and re-layouts: 1.96 us -> none  [local(): rim_below = lax.ppermute(jnp.stack([x[:DEEP] for x in raw]), 'space', up)]
  transfers between devices with their start and end apart: 7 -> 7, of which waited for: 3 -> 5; matrix products, arithmetic and copies ran while one was open for 1% -> 0% of each run, Pallas kernels for 7% -> 29%
where the time goes in v6:
time: 106 us; the launch traced here: 105 us
  Pallas kernels  36.1 us (34%)
  blocking collectives  24.8 us (23%)
  waiting for transfers between devices  22.4 us (21%)
  starting transfers between devices  21 us (20%)
    pallas_call x1, Pallas kernels, local(): pl.pallas_call(functools.partial(pack_kernel, members), in_specs=[SM, HB]...  26 us
    all_to_all x1, blocking collectives, local(): routed = lax.all_to_all(chosen, 'dom', 0, 0, tiled=True).reshape(-1, LANES)  24.8 us
    all_to_all x1, waiting for transfers between devices, local(): pieces = lax.all_to_all(packed, 'dom', 0, 0, tiled=True)  11.8 us
    ppermute x2, waiting for transfers between devices, local(): second = lax.ppermute(second, 'space', swap_second)  7.43 us
    ppermute x1, starting transfers between devices, local(): lax.ppermute(rims[1], 'space', swap_second)  7.3 us
    all_to_all x1, starting transfers between devices, local(): pieces = lax.all_to_all(packed, 'dom', 0, 0, tiled=True)  5.67 us
    pallas_call x2, Pallas kernels, local(): pl.pallas_call(functools.partial(step_kernel, size), grid=(1,), in_specs=...  5.65 us
    ppermute x2, starting transfers between devices, local(): second = lax.ppermute(second, 'space', swap_second)  5.25 us
  transfers between devices with their start and end apart: 7, of which 5 were waited for; matrix products, arithmetic and copies ran while one was open for 0% of the time, Pallas kernels for 29%

profile of v6, /device:TPU:1, one launch (start us, length us, event | category | flops | bytes accessed | tf_op | source)
XLA Modules:
  0.0 105.5 jit_solution(15095940072278285307)
XLA Ops:
  0.0 1.0 rims.1
  1.1 2.6 %collective-permute-start = (f32[3,16,8,128]{3,2,1,0:T(8,128)S(1)}, f32[3,16,8,128]{3,2,1,0:T(8,128)S(1)}, u32[]{:S(2)}, u32[]{:S(2)}) collective-permute-start(f32[3,16,8,128]{3,2,1,0:T(8,128)S(1)} %get-tuple-element.17), channel_id=1, source_target_pairs={{0,1},{1,0},{2,3},{3,2},{4,5},{5,4},{6,7},{7,6},{8,9},{9,8},{10,11... | collective-permute-start | bytes 589832 | tf_op jit(solution)/shard_map/ppermute | solution.py:214
  3.6 7.3 %collective-permute-start.1 = (f32[3,16,8,128]{3,2,1,0:T(8,128)S(1)}, f32[3,16,8,128]{3,2,1,0:T(8,128)S(1)}, u32[]{:S(2)}, u32[]{:S(2)}) collective-permute-start(f32[3,16,8,128]{3,2,1,0:T(8,128)S(1)} %get-tuple-element.18), channel_id=1, source_target_pairs={{0,15},{1,2},{2,1},{3,4},{4,3},{5,6},{6,5},{7,8},{8,7},{9,10},{10,... | collective-permute-start | bytes 589832 | tf_op jit(solution)/shard_map/ppermute | solution.py:214
  10.9 0.7 copy-done.5
  11.6 26.0 %pack.1 = f32[16,2,3,2,8,128]{5,4,3,2,1,0:T(8,128)} custom-call(s32[64]{0:T(128)S(1)} %copy-done.5, f32[4,3,2,16,8,128]{5,4,3,2,1,0:T(8,128)} %bitcast.34), custom_call_target="tpu_custom_call" | custom-call | tf_op jit(solution)/shard_map/pack/pallas_call | solution.py:182
  37.6 5.7 %all-to-all-start = ((f32[16,2,3,2,8,128]{5,4,3,2,1,0:T(8,128)}), f32[16,2,3,2,8,128]{5,4,3,2,1,0:T(8,128)S(1)}, u32[]{:S(2)}, u32[]{:S(2)}) async-start(f32[16,2,3,2,8,128]{5,4,3,2,1,0:T(8,128)} %pack.1), calls=%async_computation | async-start | bytes 1572864 | tf_op jit(solution)/shard_map/all_to_all | solution.py:191
  43.3 0.0 copy-done.6
  43.3 0.1 fusion.1
  43.4 0.1 fusion.4
  43.5 0.1 dynamic_slice.3.kept
  43.6 0.2 select_reduce_fusion.table
  43.8 0.0 collective-permute-done
  43.8 0.0 collective-permute-done.1
  43.8 0.2 coef.1
  44.1 11.8 %all-to-all-done = f32[16,2,3,2,8,128]{5,4,3,2,1,0:T(8,128)S(1)} async-done(((f32[16,2,3,2,8,128]{5,4,3,2,1,0:T(8,128)}), f32[16,2,3,2,8,128]{5,4,3,2,1,0:T(8,128)S(1)}, u32[]{:S(2)}, u32[]{:S(2)}) %all-to-all-start) | async-done | bytes 786464 | tf_op jit(solution)/shard_map/all_to_all | solution.py:191
  55.9 0.6 pick.1
  56.6 0.0 copy-start
  56.6 0.0 copy-start.1
  56.6 24.8 %all_to_all.10 = f32[16,4,48,128]{3,2,1,0:T(8,128)S(1)} all-to-all(f32[16,4,48,128]{3,2,1,0:T(8,128)S(1)} %pick.1), channel_id=1, replica_groups=mesh['dom'=16,'space'=16] {'dom'}, dimensions={0} | all-to-all | bytes 3145728 | tf_op jit(solution)/shard_map/all_to_all | solution.py:236
  81.4 0.0 copy-done.1
  81.4 1.2 %prep.3 = (f32[2,3,16,16,128]{4,3,2,1,0:T(8,128)S(1)}, f32[2,22,16,128]{3,2,1,0:T(8,128)S(1)}, f32[2,22,16,128]{3,2,1,0:T(8,128)S(1)}) custom-call(s32[4]{0:T(128)S(1)} %dynamic_slice.3.kept, f32[3072,128]{1,0:T(8,128)S(1)} %bitcast.37, f32[3072,128]{1,0:T(8,128)S(1)} %bitcast.35, f32[3072,128]{1,0:T(8,128)S(1)} %bitcast.39), custom_call_target="tpu_custom_call" | custom-call | tf_op jit(solution)/shard_map/prep/pallas_call | solution.py:243
  82.6 0.1 collective-permute-start.4
  82.7 2.0 %collective-permute-start.5 = (f32[2,22,16,128]{3,2,1,0:T(8,128)S(1)}, f32[2,22,16,128]{3,2,1,0:T(8,128)S(1)}, u32[]{:S(2)}, u32[]{:S(2)}) collective-permute-start(f32[2,22,16,128]{3,2,1,0:T(8,128)S(1)} %get-tuple-element.28), channel_id=1, source_target_pairs={{0,15},{1,2},{2,1},{3,4},{4,3},{5,6},{6,5},{7,8},{8,7},{9,10},{10,... | collective-permute-start | bytes 1081352 | tf_op jit(solution)/shard_map/ppermute | solution.py:252
  84.8 1.2 %prep.2 = (f32[2,3,16,16,128]{4,3,2,1,0:T(8,128)S(1)}, f32[2,22,16,128]{3,2,1,0:T(8,128)S(1)}, f32[2,22,16,128]{3,2,1,0:T(8,128)S(1)}) custom-call(s32[4]{0:T(128)S(1)} %dynamic_slice.3.kept, f32[3072,128]{1,0:T(8,128)S(1)} %bitcast.38, f32[3072,128]{1,0:T(8,128)S(1)} %bitcast.36, f32[3072,128]{1,0:T(8,128)S(1)} %bitcast.40), custom_call_target="tpu_custom_call" | custom-call | tf_op jit(solution)/shard_map/prep/pallas_call | solution.py:243
  86.0 0.1 collective-permute-start.2
  86.1 3.2 %collective-permute-start.3 = (f32[2,22,16,128]{3,2,1,0:T(8,128)S(1)}, f32[2,22,16,128]{3,2,1,0:T(8,128)S(1)}, u32[]{:S(2)}, u32[]{:S(2)}) collective-permute-start(f32[2,22,16,128]{3,2,1,0:T(8,128)S(1)} %get-tuple-element.24), channel_id=1, source_target_pairs={{0,15},{1,2},{2,1},{3,4},{4,3},{5,6},{6,5},{7,8},{8,7},{9,10},{10,... | collective-permute-start | bytes 1081352 | tf_op jit(solution)/shard_map/ppermute | solution.py:252
  89.3 2.0 %collective-permute-done.4.first = f32[2,22,16,128]{3,2,1,0:T(8,128)S(1)} collective-permute-done((f32[2,22,16,128]{3,2,1,0:T(8,128)S(1)}, f32[2,22,16,128]{3,2,1,0:T(8,128)S(1)}, u32[]{:S(2)}, u32[]{:S(2)}) %collective-permute-start.4) | collective-permute-done | bytes 360480 | tf_op jit(solution)/shard_map/ppermute | solution.py:251
  91.3 3.7 %collective-permute-done.5.second = f32[2,22,16,128]{3,2,1,0:T(8,128)S(1)} collective-permute-done((f32[2,22,16,128]{3,2,1,0:T(8,128)S(1)}, f32[2,22,16,128]{3,2,1,0:T(8,128)S(1)}, u32[]{:S(2)}, u32[]{:S(2)}) %collective-permute-start.5) | collective-permute-done | bytes 360480 | tf_op jit(solution)/shard_map/ppermute | solution.py:252
  95.0 2.8 %steps.2.rest_0_ = f32[4,3,256,128]{3,2,1,0:T(8,128)} custom-call(f32[2,3,16,16,128]{4,3,2,1,0:T(8,128)S(1)} %get-tuple-element.26.fields, f32[2,22,16,128]{3,2,1,0:T(8,128)S(1)} %collective-permute-done.4.first, f32[2,22,16,128]{3,2,1,0:T(8,128)S(1)} %collective-permute-done.5.second, f32[3,32,16,128]{3,2,1,0:T(8,128)S(1)} %coef.1), custom_call_target="tpu_custom_call" | custom-call | tf_op jit(solution)/shard_map/steps/pallas_call | solution.py:258
  97.8 1.2 %collective-permute-done.2.first = f32[2,22,16,128]{3,2,1,0:T(8,128)S(1)} collective-permute-done((f32[2,22,16,128]{3,2,1,0:T(8,128)S(1)}, f32[2,22,16,128]{3,2,1,0:T(8,128)S(1)}, u32[]{:S(2)}, u32[]{:S(2)}) %collective-permute-start.2) | collective-permute-done | bytes 360480 | tf_op jit(solution)/shard_map/ppermute | solution.py:251
  99.0 3.7 %collective-permute-done.3.second = f32[2,22,16,128]{3,2,1,0:T(8,128)S(1)} collective-permute-done((f32[2,22,16,128]{3,2,1,0:T(8,128)S(1)}, f32[2,22,16,128]{3,2,1,0:T(8,128)S(1)}, u32[]{:S(2)}, u32[]{:S(2)}) %collective-permute-start.3) | collective-permute-done | bytes 360480 | tf_op jit(solution)/shard_map/ppermute | solution.py:252
  102.7 2.8 %steps.3 = f32[4,3,256,128]{3,2,1,0:T(8,128)} custom-call(f32[2,3,16,16,128]{4,3,2,1,0:T(8,128)S(1)} %get-tuple-element.22.fields, f32[2,22,16,128]{3,2,1,0:T(8,128)S(1)} %collective-permute-done.2.first, f32[2,22,16,128]{3,2,1,0:T(8,128)S(1)} %collective-permute-done.3.second, f32[3,32,16,128]{3,2,1,0:T(8,128)S(1)} %coef.1, ...), custom_call_target="tpu_custom_call", output_to_operand_aliasing={{}: (4, {})} | custom-call | tf_op jit(solution)/shard_map/steps/pallas_call | solution.py:258
  (13 shorter events, 0.0 us)
Async XLA Ops:
  1.1 42.7 %collective-permute-start = (f32[3,16,8,128]{3,2,1,0:T(8,128)S(1)}, f32[3,16,8,128]{3,2,1,0:T(8,128)S(1)}, u32[]{:S(2)}, u32[]{:S(2)}) collective-permute-start(f32[3,16,8,128]{3,2,1,0:T(8,128)S(1)} %get-tuple-element.17), channel_id=1, source_target_pairs={{0,1},{1,0},{2,3},{3,2},{4,5},{5,4},{6,7},{7,6},{8,9},{9,8},{10,11... | collective-permute-start | bytes 589832 | tf_op jit(solution)/shard_map/ppermute | solution.py:214
  3.6 40.2 %collective-permute-start.1 = (f32[3,16,8,128]{3,2,1,0:T(8,128)S(1)}, f32[3,16,8,128]{3,2,1,0:T(8,128)S(1)}, u32[]{:S(2)}, u32[]{:S(2)}) collective-permute-start(f32[3,16,8,128]{3,2,1,0:T(8,128)S(1)} %get-tuple-element.18), channel_id=1, source_target_pairs={{0,15},{1,2},{2,1},{3,4},{4,3},{5,6},{6,5},{7,8},{8,7},{9,10},{10,... | collective-permute-start | bytes 589832 | tf_op jit(solution)/shard_map/ppermute | solution.py:214
  10.9 0.7 copy-start.5
  11.6 31.7 %copy-start.6 = (s32[64]{0:T(128)S(1)}, s32[64]{0:T(128)}, u32[]{:S(2)}) copy-start(s32[64]{0:T(128)} %anc.1) | copy-start | bytes 772
  11.6 32.2 %copy-start.2 = (f32[16,2048]{1,0:T(8,128)S(1)}, f32[16,2048]{1,0:T(8,128)}, u32[]{:S(2)}) copy-start(f32[16,2048]{1,0:T(8,128)} %param.9) | copy-start | bytes 393220
  11.6 32.3 %copy-start.3 = (f32[16,2048]{1,0:T(8,128)S(1)}, f32[16,2048]{1,0:T(8,128)}, u32[]{:S(2)}) copy-start(f32[16,2048]{1,0:T(8,128)} %param.10) | copy-start | bytes 393220
  11.6 32.3 %copy-start.4 = (f32[16,2048]{1,0:T(8,128)S(1)}, f32[16,2048]{1,0:T(8,128)}, u32[]{:S(2)}) copy-start(f32[16,2048]{1,0:T(8,128)} %param.11) | copy-start | bytes 393220
  37.6 18.3 %all-to-all-start = ((f32[16,2,3,2,8,128]{5,4,3,2,1,0:T(8,128)}), f32[16,2,3,2,8,128]{5,4,3,2,1,0:T(8,128)S(1)}, u32[]{:S(2)}, u32[]{:S(2)}) async-start(f32[16,2,3,2,8,128]{5,4,3,2,1,0:T(8,128)} %pack.1), calls=%async_computation | async-start | bytes 1572864 | tf_op jit(solution)/shard_map/all_to_all | solution.py:191
  56.6 24.8 %copy-start = (f32[4,3,16,2048]{3,2,1,0:T(8,128)S(1)}, f32[4,3,16,2048]{3,2,1,0:T(8,128)}, u32[]{:S(2)}) copy-start(f32[4,3,16,2048]{3,2,1,0:T(8,128)} %param.7) | copy-start | bytes 4718596
  56.6 24.8 %copy-start.1 = (f32[4,3,16,2048]{3,2,1,0:T(8,128)S(1)}, f32[4,3,16,2048]{3,2,1,0:T(8,128)}, u32[]{:S(2)}) copy-start(f32[4,3,16,2048]{3,2,1,0:T(8,128)} %param.8) | copy-start | bytes 4718596
  82.6 8.6 %collective-permute-start.4 = (f32[2,22,16,128]{3,2,1,0:T(8,128)S(1)}, f32[2,22,16,128]{3,2,1,0:T(8,128)S(1)}, u32[]{:S(2)}, u32[]{:S(2)}) collective-permute-start(f32[2,22,16,128]{3,2,1,0:T(8,128)S(1)} %get-tuple-element.27), channel_id=1, source_target_pairs={{0,1},{1,0},{2,3},{3,2},{4,5},{5,4},{6,7},{7,6},{8,9},{9,8},{10,11... | collective-permute-start | bytes 1081352 | tf_op jit(solution)/shard_map/ppermute | solution.py:251
  82.7 12.3 %collective-permute-start.5 = (f32[2,22,16,128]{3,2,1,0:T(8,128)S(1)}, f32[2,22,16,128]{3,2,1,0:T(8,128)S(1)}, u32[]{:S(2)}, u32[]{:S(2)}) collective-permute-start(f32[2,22,16,128]{3,2,1,0:T(8,128)S(1)} %get-tuple-element.28), channel_id=1, source_target_pairs={{0,15},{1,2},{2,1},{3,4},{4,3},{5,6},{6,5},{7,8},{8,7},{9,10},{10,... | collective-permute-start | bytes 1081352 | tf_op jit(solution)/shard_map/ppermute | solution.py:252
  86.0 13.0 %collective-permute-start.2 = (f32[2,22,16,128]{3,2,1,0:T(8,128)S(1)}, f32[2,22,16,128]{3,2,1,0:T(8,128)S(1)}, u32[]{:S(2)}, u32[]{:S(2)}) collective-permute-start(f32[2,22,16,128]{3,2,1,0:T(8,128)S(1)} %get-tuple-element.23), channel_id=1, source_target_pairs={{0,1},{1,0},{2,3},{3,2},{4,5},{5,4},{6,7},{7,6},{8,9},{9,8},{10,11... | collective-permute-start | bytes 1081352 | tf_op jit(solution)/shard_map/ppermute | solution.py:251
  86.1 16.6 %collective-permute-start.3 = (f32[2,22,16,128]{3,2,1,0:T(8,128)S(1)}, f32[2,22,16,128]{3,2,1,0:T(8,128)S(1)}, u32[]{:S(2)}, u32[]{:S(2)}) collective-permute-start(f32[2,22,16,128]{3,2,1,0:T(8,128)S(1)} %get-tuple-element.24), channel_id=1, source_target_pairs={{0,15},{1,2},{2,1},{3,4},{4,3},{5,6},{6,5},{7,8},{8,7},{9,10},{10,... | collective-permute-start | bytes 1081352 | tf_op jit(solution)/shard_map/ppermute | solution.py:252

commit v7 on v6

--- a/solution.py
+++ b/solution.py
@@ -16,7 +16,7 @@
 RIM = (7, 7, 8)
 RIMS = sum(RIM)
 FROM = (0, 7, 14)
-CHUNKS = ((0, 2), (2, 4))
+CHUNKS = {2: (1, 1), 3: (2, 1), 4: (2, 2)}
 
 VM = pl.BlockSpec(memory_space=pltpu.VMEM)
 SM = pl.BlockSpec(memory_space=pltpu.SMEM)
@@ -81,37 +81,45 @@
         out[2, r] = 1.0 / (1.0 + DT * values[2])
 
 
-def pick_kernel(members, low, high, table, got, out):
+def pick_kernel(members, table, got, out):
+    size = out.shape[1]
     for d in range(out.shape[0]):
-        for k in range(low, high):
-            at = table[d * members + k]
-            out[d, k - low] = got[at]
-
-
-def prep_kernel(members, low, high, kept, routed, state, jitter, fields, first, second):
-    kinds, rows, tiles = fields.shape[1:4]
+        for k in range(size):
+            out[d, k] = got[table[(d + 1) * members - size + k]]
+
+
+def prep_kernel(low, order, gone, state, jitter, *rest):
+    *routed, fields, first, second = rest
+    size, kinds, rows, tiles = fields.shape[:4]
     slab = kinds * rows
     odd = lax.axis_index("space") % 2 == 1
-    for k in range(low, high):
-        mine = kept[k] == 1
+    for k in range(size):
+        slot = order[low + k]
+        if routed:
+            ref, = routed
+            late = ref.shape[0] // (tiles * slab)
+            at = low + k - (order.shape[0] - late)
+            mine = gone[low + k] == 0
         for f in range(kinds):
             values = []
             for r in range(rows):
-                far = pl.ds(k * slab + f * rows + r, tiles, stride=members * slab)
-                t = (k * kinds + f) * (rows // SUB) + r // SUB
-                near = pl.ds(t * tiles * SUB + r % SUB, tiles, stride=SUB)
-                value = jnp.where(mine, state[near, :], routed[far, :]) + jitter[near, :]
-                fields[k - low, f, r] = value
+                near = pl.ds((f * (rows // SUB) + r // SUB) * tiles * SUB + r % SUB, tiles, stride=SUB)
+                value = state[slot, near, :]
+                if routed:
+                    far = ref[pl.ds(at * slab + f * rows + r, tiles, stride=late * slab), :]
+                    value = jnp.where(mine, value, far)
+                value = value + jitter[slot, near, :]
+                fields[k, f, r] = value
                 values.append(value)
             for r in range(RIM[f]):
                 top, bottom = values[r], values[rows - RIM[f] + r]
-                first[k - low, FROM[f] + r] = jnp.where(odd, top, bottom)
-                second[k - low, FROM[f] + r] = jnp.where(odd, bottom, top)
-
-
-def step_kernel(size, fields, first, second, coef, *rest):
-    out, *held = rest[-4:]
-    kinds, rows, tiles = fields.shape[1:4]
+                first[k, FROM[f] + r] = jnp.where(odd, top, bottom)
+                second[k, FROM[f] + r] = jnp.where(odd, bottom, top)
+
+
+def step_kernel(low, order, fields, first, second, coef, *rest):
+    whole, out, sem, *held = rest[-6:]
+    size, kinds, rows, tiles = fields.shape[:4]
     lane = lax.broadcasted_iota(jnp.int32, (tiles, LANES), 1)
     tile = lax.broadcasted_iota(jnp.int32, (tiles, LANES), 0)
     lane_first, lane_last = lane == 0, lane == LANES - 1
@@ -158,9 +166,15 @@
                     put(n + 1, 1, r, s * (uu + c * vv - half * difference(here, here)))
                 along = get(n + 1, 0, r + 1) - get(n + 1, 0, r - 1)
                 put(n + 1, 2, r, s * (vv - c * uu - half * along))
+        copy_out(k).start()
         return carry
 
+    def copy_out(k):
+        return pltpu.make_async_copy(out.at[k], whole.at[order[low + k]], sem.at[k])
+
     lax.fori_loop(0, size, particle, 0)
+    for k in range(size):
+        copy_out(k).wait()
 
 
 def local(ancestor, state, jitter, depth, coriolis, drag):
@@ -182,7 +196,7 @@
     packed = pl.pallas_call(
         functools.partial(pack_kernel, members),
         in_specs=[SM, HB],
-        out_specs=HB,
+        out_specs=VM,
         out_shape=jax.ShapeDtypeStruct((tiles, CAP, kinds, bands, SUB, LANES), f32),
         scratch_shapes=[pltpu.SemaphoreType.DMA((CAP * kinds * bands,))],
         compiler_params=PARAMS,
@@ -193,12 +207,21 @@
 
     slot = jnp.arange(ancestor.shape[0], dtype=jnp.int32)
     moved = ancestor != slot
+    same = slot[:, None] // members == slot[None, :] // members
     donor = jnp.any((ancestor[:, None] == slot[None, :]) & moved[:, None], axis=0)
-    same = (slot[:, None] // members == slot[None, :] // members) & (slot[:, None] < slot[None, :])
-    rank = jnp.any(same & donor[:, None], axis=0).astype(jnp.int32)
+    rank = jnp.any(same & (slot[:, None] < slot[None, :]) & donor[:, None], axis=0).astype(jnp.int32)
     place = slot // members * CAP + rank
-    table = jnp.sum(jnp.where(ancestor[:, None] == slot[None, :], place[None, :], 0), axis=1)
-    kept = lax.dynamic_slice_in_dim(jnp.where(moved, 0, 1).astype(jnp.int32), me * members, members)
+    source = jnp.sum(jnp.where(ancestor[:, None] == slot[None, :], place[None, :], 0), axis=1)
+
+    rated = slot + jnp.where(moved, ancestor.shape[0], 0)
+    turn = jnp.sum((same & (rated[:, None] < rated[None, :])).astype(jnp.int32), axis=0)
+    seat = slot // members * members + turn
+    hit = seat[None, :] == slot[:, None]
+    table = jnp.sum(jnp.where(hit, source[None, :], 0), axis=1)
+    pair = jnp.sum(jnp.where(hit, slot[None, :] % members + members * moved[None, :], 0), axis=1)
+    pair = lax.dynamic_slice_in_dim(pair, me * members, members)
+    order, gone = pair % members, pair // members
+    most = jnp.max(jnp.sum((same & moved[:, None]).astype(jnp.int32), axis=0))
 
     raw = (depth, coriolis, drag)
     rim = jax.ShapeDtypeStruct((3, tiles, SUB, LANES), f32)
@@ -223,49 +246,66 @@
         *(tiled(x).reshape(rows * tiles, LANES) for x in raw),
         *(x.reshape(3 * tiles * SUB, LANES) for x in rims),
     )
-    pieces, coef, table, kept = lax.optimization_barrier((pieces, coef, table, kept))
-
-    chosen = pl.pallas_call(
-        functools.partial(pick_kernel, members, 0, members),
-        in_specs=[SM, VM],
-        out_specs=VM,
-        out_shape=jax.ShapeDtypeStruct((blocks, members, kinds * rows, LANES), f32),
-        compiler_params=PARAMS,
-        name="pick",
-    )(table, pieces)
-    routed = lax.all_to_all(chosen, "dom", 0, 0, tiled=True).reshape(-1, LANES)
-
-    out = None
-    chunks = []
-    for low, high in CHUNKS:
-        size = high - low
+    sides = (members, kinds * rows * tiles, LANES)
+    state_t, jitter_t = state_t.reshape(sides), jitter_t.reshape(sides)
+
+    def prepared(low, size, order, gone, routed):
         rim = jax.ShapeDtypeStruct((size, RIMS, tiles, LANES), f32)
         fields, first, second = pl.pallas_call(
-            functools.partial(prep_kernel, members, low, high),
-            in_specs=[SM, VM, VM, VM],
+            functools.partial(prep_kernel, low),
+            in_specs=[SM, SM] + [VM] * (2 + len(routed)),
             out_specs=(VM, VM, VM),
             out_shape=(jax.ShapeDtypeStruct((size, kinds, rows, tiles, LANES), f32), rim, rim),
             compiler_params=PARAMS,
             name="prep",
-        )(kept, routed, state_t.reshape(-1, LANES), jitter_t.reshape(-1, LANES))
+        )(order, gone, state_t, jitter_t, *routed)
         first = lax.ppermute(first, "space", swap_first)
         second = lax.ppermute(second, "space", swap_second)
-        chunks.append((fields, first, second))
-
-    for (low, high), (fields, first, second) in zip(CHUNKS, chunks):
-        size = high - low
-        done = pl.BlockSpec((size, kinds, rows * tiles, LANES), lambda i, at=low // size: (at, 0, 0, 0))
-        out = pl.pallas_call(
-            functools.partial(step_kernel, size),
-            grid=(1,),
-            in_specs=[VM] * 4 + ([] if out is None else [HB]),
-            out_specs=done,
+        return fields, first, second
+
+    def stepped(low, size, order, parts, coef, out):
+        return pl.pallas_call(
+            functools.partial(step_kernel, low),
+            in_specs=[SM] + [VM] * 4 + [HB] * len(out),
+            out_specs=HB,
             out_shape=jax.ShapeDtypeStruct((members, kinds, rows * tiles, LANES), f32),
-            scratch_shapes=[pltpu.VMEM((STEPS, rows + 2 * DEEP, tiles, LANES), f32)] * 3,
-            input_output_aliases={} if out is None else {4: 0},
+            scratch_shapes=[
+                pltpu.VMEM((size, kinds, rows * tiles, LANES), f32),
+                pltpu.SemaphoreType.DMA((size,)),
+            ]
+            + [pltpu.VMEM((STEPS, rows + 2 * DEEP, tiles, LANES), f32)] * 3,
+            input_output_aliases={5: 0} if out else {},
             compiler_params=PARAMS,
             name="steps",
-        )(fields, first, second, coef, *([] if out is None else [out]))
+        )(order, *parts, coef, *out)
+
+    def rest(late, pieces, coef, table, order, gone):
+        early = members - late
+        chosen = pl.pallas_call(
+            functools.partial(pick_kernel, members),
+            in_specs=[SM, VM],
+            out_specs=VM,
+            out_shape=jax.ShapeDtypeStruct((blocks, late, kinds * rows, LANES), f32),
+            compiler_params=PARAMS,
+            name="pick",
+        )(table, pieces)
+        routed = lax.all_to_all(chosen, "dom", 0, 0, tiled=True).reshape(-1, LANES)
+        out = []
+        if early:
+            parts = prepared(0, early, order, gone, ())
+            out = [stepped(0, early, order, parts, coef, out)]
+        chunks = []
+        for size in CHUNKS[late]:
+            chunks.append((early, size, prepared(early, size, order, gone, (routed,))))
+            early += size
+        for low, size, parts in chunks:
+            out = [stepped(low, size, order, parts, coef, out)]
+        return out[0]
+
+    args = lax.optimization_barrier((pieces, coef, table, order, gone))
+    sizes = sorted(CHUNKS)
+    which = jnp.clip(most - sizes[0], 0, len(sizes) - 1)
+    out = lax.switch(which, [functools.partial(rest, size) for size in sizes], *args)
     out = out.reshape(members, kinds, bands, tiles, SUB, LANES)
     return jnp.swapaxes(out, -3, -2).reshape(state.shape)
 

time: 106 us -> 84.4 us (0.80)
  Pallas kernels: 36.1 us -> 14.7 us
  waiting for transfers between devices: 22.4 us -> 19.5 us
    pallas_call x1, Pallas kernels: 26 us -> 3.13 us  [local(): pl.pallas_call(functools.partial(pack_kernel, members), in_specs=[SM, HB]...]
    all_to_all x1, waiting for transfers between devices: 11.8 us -> 9.26 us  [local(): pieces = lax.all_to_all(packed, 'dom', 0, 0, tiled=True)]
  transfers between devices with their start and end apart: 7 -> 7, of which waited for: 5 -> 5; matrix products, arithmetic and copies ran while one was open for 0% -> 2% of each run, Pallas kernels for 29% -> 10%
where the time goes in v7:
time: 84.4 us; the launch traced here: 83.4 us
  blocking collectives  24.8 us (29%)
  starting transfers between devices  21 us (25%)
  waiting for transfers between devices  19.5 us (23%)
  Pallas kernels  14.7 us (17%)
  other arithmetic  1.44 us (2%)
  between operations  1 us (1%)
    all_to_all x1, blocking collectives, rest(): routed = lax.all_to_all(chosen, 'dom', 0, 0, tiled=True).reshape(-1, LANES)  24.8 us
    all_to_all x1, waiting for transfers between devices, local(): pieces = lax.all_to_all(packed, 'dom', 0, 0, tiled=True)  9.26 us
    ppermute x2, waiting for transfers between devices, prepared(): second = lax.ppermute(second, 'space', swap_second)  7.45 us
    ppermute x1, starting transfers between devices, local(): lax.ppermute(rims[1], 'space', swap_second)  7.3 us
    pallas_call x2, Pallas kernels, stepped(): pl.pallas_call(functools.partial(step_kernel, low), in_specs=[SM] + [VM]...  6.32 us
    all_to_all x1, starting transfers between devices, local(): pieces = lax.all_to_all(packed, 'dom', 0, 0, tiled=True)  5.67 us
    ppermute x2, starting transfers between devices, prepared(): second = lax.ppermute(second, 'space', swap_second)  5.25 us
    pallas_call x1, Pallas kernels, local(): pl.pallas_call(functools.partial(pack_kernel, members), in_specs=[SM, HB]...  3.13 us
  transfers between devices with their start and end apart: 7, of which 5 were waited for; matrix products, arithmetic and copies ran while one was open for 2% of the time, Pallas kernels for 10%

profile of v7, /device:TPU:1, one launch (start us, length us, event | category | flops | bytes accessed | tf_op | source)
XLA Modules:
  0.0 83.4 jit_solution(9506602436234442715)
XLA Ops:
  0.0 1.0 %rims.1 = (f32[3,16,8,128]{3,2,1,0:T(8,128)S(1)}, f32[3,16,8,128]{3,2,1,0:T(8,128)S(1)}) custom-call(f32[2,16,8,128]{3,2,1,0:T(8,128)} %bitcast.42, f32[2,16,8,128]{3,2,1,0:T(8,128)} %bitcast.44, f32[2,16,8,128]{3,2,1,0:T(8,128)} %bitcast.46), custom_call_target="tpu_custom_call" | custom-call | tf_op jit(solution)/shard_map/rims/pallas_call | solution.py:228
  1.1 2.6 %collective-permute-start.16 = (f32[3,16,8,128]{3,2,1,0:T(8,128)S(1)}, f32[3,16,8,128]{3,2,1,0:T(8,128)S(1)}, u32[]{:S(2)}, u32[]{:S(2)}) collective-permute-start(f32[3,16,8,128]{3,2,1,0:T(8,128)S(1)} %get-tuple-element.103), channel_id=1, source_target_pairs={{0,1},{1,0},{2,3},{3,2},{4,5},{5,4},{6,7},{7,6},{8,9},{9,8},{10,11... | collective-permute-start | bytes 589832 | tf_op jit(solution)/shard_map/ppermute | solution.py:237
  3.6 7.3 %collective-permute-start.17 = (f32[3,16,8,128]{3,2,1,0:T(8,128)S(1)}, f32[3,16,8,128]{3,2,1,0:T(8,128)S(1)}, u32[]{:S(2)}, u32[]{:S(2)}) collective-permute-start(f32[3,16,8,128]{3,2,1,0:T(8,128)S(1)} %get-tuple-element.104), channel_id=1, source_target_pairs={{0,15},{1,2},{2,1},{3,4},{4,3},{5,6},{6,5},{7,8},{8,7},{9,10},{10,... | collective-permute-start | bytes 589832 | tf_op jit(solution)/shard_map/ppermute | solution.py:237
  10.9 0.7 copy-done.3
  11.6 3.1 %pack.1 = f32[16,2,3,2,8,128]{5,4,3,2,1,0:T(8,128)} custom-call(s32[64]{0:T(128)S(1)} %copy-done.3, f32[4,3,2,16,8,128]{5,4,3,2,1,0:T(8,128)} %bitcast.50), custom_call_target="tpu_custom_call" | custom-call | tf_op jit(solution)/shard_map/pack/pallas_call | solution.py:196
  14.7 5.7 %all-to-all-start.3 = ((f32[16,2,3,2,8,128]{5,4,3,2,1,0:T(8,128)}), f32[16,2,3,2,8,128]{5,4,3,2,1,0:T(8,128)S(1)}, u32[]{:S(2)}, u32[]{:S(2)}) async-start(f32[16,2,3,2,8,128]{5,4,3,2,1,0:T(8,128)} %pack.1), calls=%async_computation.3 | async-start | bytes 1572864 | tf_op jit(solution)/shard_map/all_to_all | solution.py:205
  20.4 0.1 fusion.1
  20.5 0.1 fusion.3
  20.6 0.1 convert_reduce_fusion
  20.8 0.7 reduce_max.9
  22.2 0.2 select_reduce_fusion.2
  22.4 0.1 select_reduce_fusion
  22.5 0.1 and_select_fusion
  22.6 1.1 %coef.1 = f32[3,32,16,128]{3,2,1,0:T(8,128)} custom-call(f32[256,128]{1,0:T(8,128)S(1)} %bitcast.43, f32[256,128]{1,0:T(8,128)S(1)} %bitcast.45, f32[256,128]{1,0:T(8,128)S(1)} %bitcast.47, f32[384,128]{1,0:T(8,128)S(1)} %bitcast.48, f32[384,128]{1,0:T(8,128)S(1)} %bitcast.49), custom_call_target="tpu_custom_call" | custom-call | tf_op jit(solution)/shard_map/coef/pallas_call | solution.py:238
  23.8 9.3 %all-to-all-done.3 = f32[16,2,3,2,8,128]{5,4,3,2,1,0:T(8,128)S(1)} async-done(((f32[16,2,3,2,8,128]{5,4,3,2,1,0:T(8,128)}), f32[16,2,3,2,8,128]{5,4,3,2,1,0:T(8,128)S(1)}, u32[]{:S(2)}, u32[]{:S(2)}) %all-to-all-start.3) | async-done | bytes 786464 | tf_op jit(solution)/shard_map/all_to_all | solution.py:205
  33.0 50.1 %conditional.1 = (f32[4,3,256,128]{3,2,1,0:T(8,128)}) conditional(s32[]{:T(128)} %clamp.3, (s32[64]{0:T(128)S(1)}, f32[32,48,128]{2,1,0:T(8,128)S(1)}, s32[4]{0:T(128)S(1)}, s32[4]{0:T(128)S(1)}, f32[4,768,128]{2,1,0:T(8,128)}, /*index=5*/f32[4,768,128]{2,1,0:T(8,128)}, f32[3,32,16,128]{3,2,1,0:T(8,128)}) %tuple.30, ...), branch_computations={%region_8.9_spmd, %region_9.10_spmd, %region_10.11_spmd} | conditional | bytes 25035116 | solution.py:308
  33.0 0.6 pick.5
  33.7 0.0 copy-start.7
  33.7 0.0 copy-start.10
  33.7 24.8 %all_to_all.17 = f32[16,4,48,128]{3,2,1,0:T(8,128)S(1)} all-to-all(f32[16,4,48,128]{3,2,1,0:T(8,128)S(1)} %pick.5), channel_id=1, replica_groups=mesh['dom'=16,'space'=16] {'dom'}, dimensions={0} | all-to-all | bytes 3145728 | tf_op jit(solution)/shard_map/cond/branch_2_fun/all_to_all | solution.py:292
  58.5 1.2 %prep.15 = (f32[2,3,16,16,128]{4,3,2,1,0:T(8,128)S(1)}, f32[2,22,16,128]{3,2,1,0:T(8,128)S(1)}, f32[2,22,16,128]{3,2,1,0:T(8,128)S(1)}) custom-call(s32[4]{0:T(128)S(1)} %get-tuple-element.83.order, s32[4]{0:T(128)S(1)} %get-tuple-element.84.gone, f32[4,768,128]{2,1,0:T(8,128)S(1)} %copy-done.7, f32[4,768,128]{2,1,0:T(8,128)S(1)} %copy-done.10, ...), custom_call_target="tpu_custom_call" | custom-call | tf_op jit(solution)/shard_map/cond/branch_2_fun/prep/pallas_call | solution.py:254
  59.7 0.1 collective-permute-start.14
  59.8 2.0 %collective-permute-start.15 = (f32[2,22,16,128]{3,2,1,0:T(8,128)S(1)}, f32[2,22,16,128]{3,2,1,0:T(8,128)S(1)}, u32[]{:S(2)}, u32[]{:S(2)}) collective-permute-start(f32[2,22,16,128]{3,2,1,0:T(8,128)S(1)} %get-tuple-element.95), channel_id=1, source_target_pairs={{0,15},{1,2},{2,1},{3,4},{4,3},{5,6},{6,5},{7,8},{8,7},{9,10},{10,... | collective-permute-start | bytes 1081352 | tf_op jit(solution)/shard_map/cond/branch_2_fun/ppermute | solution.py:263
  61.9 1.2 %prep.14 = (f32[2,3,16,16,128]{4,3,2,1,0:T(8,128)S(1)}, f32[2,22,16,128]{3,2,1,0:T(8,128)S(1)}, f32[2,22,16,128]{3,2,1,0:T(8,128)S(1)}) custom-call(s32[4]{0:T(128)S(1)} %get-tuple-element.83.order, s32[4]{0:T(128)S(1)} %get-tuple-element.84.gone, f32[4,768,128]{2,1,0:T(8,128)S(1)} %copy-done.7, f32[4,768,128]{2,1,0:T(8,128)S(1)} %copy-done.10, ...), custom_call_target="tpu_custom_call" | custom-call | tf_op jit(solution)/shard_map/cond/branch_2_fun/prep/pallas_call | solution.py:254
  63.1 0.1 collective-permute-start.12
  63.2 3.2 %collective-permute-start.13 = (f32[2,22,16,128]{3,2,1,0:T(8,128)S(1)}, f32[2,22,16,128]{3,2,1,0:T(8,128)S(1)}, u32[]{:S(2)}, u32[]{:S(2)}) collective-permute-start(f32[2,22,16,128]{3,2,1,0:T(8,128)S(1)} %get-tuple-element.91), channel_id=1, source_target_pairs={{0,15},{1,2},{2,1},{3,4},{4,3},{5,6},{6,5},{7,8},{8,7},{9,10},{10,... | collective-permute-start | bytes 1081352 | tf_op jit(solution)/shard_map/cond/branch_2_fun/ppermute | solution.py:263
  66.4 1.9 %collective-permute-done.14.first = f32[2,22,16,128]{3,2,1,0:T(8,128)S(1)} collective-permute-done((f32[2,22,16,128]{3,2,1,0:T(8,128)S(1)}, f32[2,22,16,128]{3,2,1,0:T(8,128)S(1)}, u32[]{:S(2)}, u32[]{:S(2)}) %collective-permute-start.14) | collective-permute-done | bytes 360480 | tf_op jit(solution)/shard_map/cond/branch_2_fun/ppermute | solution.py:262
  68.4 3.7 %collective-permute-done.15.second = f32[2,22,16,128]{3,2,1,0:T(8,128)S(1)} collective-permute-done((f32[2,22,16,128]{3,2,1,0:T(8,128)S(1)}, f32[2,22,16,128]{3,2,1,0:T(8,128)S(1)}, u32[]{:S(2)}, u32[]{:S(2)}) %collective-permute-start.15) | collective-permute-done | bytes 360480 | tf_op jit(solution)/shard_map/cond/branch_2_fun/ppermute | solution.py:263
  72.1 3.2 %steps.14.rest_0_ = f32[4,3,256,128]{3,2,1,0:T(8,128)} custom-call(s32[4]{0:T(128)S(1)} %get-tuple-element.83.order, f32[2,3,16,16,128]{4,3,2,1,0:T(8,128)S(1)} %get-tuple-element.93.fields, f32[2,22,16,128]{3,2,1,0:T(8,128)S(1)} %collective-permute-done.14.first, f32[2,22,16,128]{3,2,1,0:T(8,128)S(1)} %collective-permute-done.15.second, ...), custom_call_target="tpu_custom_call" | custom-call | tf_op jit(solution)/shard_map/cond/branch_2_fun/steps/pallas_call | solution.py:267
  75.3 0.8 collective-permute-done.12.first
  76.1 3.7 %collective-permute-done.13.second = f32[2,22,16,128]{3,2,1,0:T(8,128)S(1)} collective-permute-done((f32[2,22,16,128]{3,2,1,0:T(8,128)S(1)}, f32[2,22,16,128]{3,2,1,0:T(8,128)S(1)}, u32[]{:S(2)}, u32[]{:S(2)}) %collective-permute-start.13) | collective-permute-done | bytes 360480 | tf_op jit(solution)/shard_map/cond/branch_2_fun/ppermute | solution.py:263
  79.8 3.2 %steps.15 = f32[4,3,256,128]{3,2,1,0:T(8,128)} custom-call(s32[4]{0:T(128)S(1)} %get-tuple-element.83.order, f32[2,3,16,16,128]{4,3,2,1,0:T(8,128)S(1)} %get-tuple-element.89.fields, f32[2,22,16,128]{3,2,1,0:T(8,128)S(1)} %collective-permute-done.12.first, f32[2,22,16,128]{3,2,1,0:T(8,128)S(1)} %collective-permute-done.13.second, ...), custom_call_target="tpu_custom_call", output_to_operand_aliasing={{}: (5, {})} | custom-call | tf_op jit(solution)/shard_map/cond/branch_2_fun/steps/pallas_call | solution.py:267
  (21 shorter events, 0.1 us)
Async XLA Ops:
  1.1 21.5 %collective-permute-start.16 = (f32[3,16,8,128]{3,2,1,0:T(8,128)S(1)}, f32[3,16,8,128]{3,2,1,0:T(8,128)S(1)}, u32[]{:S(2)}, u32[]{:S(2)}) collective-permute-start(f32[3,16,8,128]{3,2,1,0:T(8,128)S(1)} %get-tuple-element.103), channel_id=1, source_target_pairs={{0,1},{1,0},{2,3},{3,2},{4,5},{5,4},{6,7},{7,6},{8,9},{9,8},{10,11... | collective-permute-start | bytes 589832 | tf_op jit(solution)/shard_map/ppermute | solution.py:237
  3.6 19.0 %collective-permute-start.17 = (f32[3,16,8,128]{3,2,1,0:T(8,128)S(1)}, f32[3,16,8,128]{3,2,1,0:T(8,128)S(1)}, u32[]{:S(2)}, u32[]{:S(2)}) collective-permute-start(f32[3,16,8,128]{3,2,1,0:T(8,128)S(1)} %get-tuple-element.104), channel_id=1, source_target_pairs={{0,15},{1,2},{2,1},{3,4},{4,3},{5,6},{6,5},{7,8},{8,7},{9,10},{10,... | collective-permute-start | bytes 589832 | tf_op jit(solution)/shard_map/ppermute | solution.py:237
  10.9 0.7 copy-start.3
  11.6 8.8 %copy-start.4 = (s32[64]{0:T(128)S(1)}, s32[64]{0:T(128)}, u32[]{:S(2)}) copy-start(s32[64]{0:T(128)} %anc.1) | copy-start | bytes 772
  11.6 11.0 %copy-start = (f32[16,2048]{1,0:T(8,128)S(1)}, f32[16,2048]{1,0:T(8,128)}, u32[]{:S(2)}) copy-start(f32[16,2048]{1,0:T(8,128)} %param.12) | copy-start | bytes 393220
  11.6 11.0 %copy-start.1 = (f32[16,2048]{1,0:T(8,128)S(1)}, f32[16,2048]{1,0:T(8,128)}, u32[]{:S(2)}) copy-start(f32[16,2048]{1,0:T(8,128)} %param.13) | copy-start | bytes 393220
  11.6 11.1 %copy-start.2 = (f32[16,2048]{1,0:T(8,128)S(1)}, f32[16,2048]{1,0:T(8,128)}, u32[]{:S(2)}) copy-start(f32[16,2048]{1,0:T(8,128)} %param.14) | copy-start | bytes 393220
  14.7 18.3 %all-to-all-start.3 = ((f32[16,2,3,2,8,128]{5,4,3,2,1,0:T(8,128)}), f32[16,2,3,2,8,128]{5,4,3,2,1,0:T(8,128)S(1)}, u32[]{:S(2)}, u32[]{:S(2)}) async-start(f32[16,2,3,2,8,128]{5,4,3,2,1,0:T(8,128)} %pack.1), calls=%async_computation.3 | async-start | bytes 1572864 | tf_op jit(solution)/shard_map/all_to_all | solution.py:205
  33.7 24.8 %copy-start.7 = (f32[4,768,128]{2,1,0:T(8,128)S(1)}, f32[4,768,128]{2,1,0:T(8,128)}, u32[]{:S(2)}) copy-start(f32[4,768,128]{2,1,0:T(8,128)} %get-tuple-element.85.state) | copy-start | bytes 4718596 | tf_op jit(solution)/shard_map/cond
  33.7 24.8 %copy-start.10 = (f32[4,768,128]{2,1,0:T(8,128)S(1)}, f32[4,768,128]{2,1,0:T(8,128)}, u32[]{:S(2)}) copy-start(f32[4,768,128]{2,1,0:T(8,128)} %get-tuple-element.86.jitter) | copy-start | bytes 4718596 | tf_op jit(solution)/shard_map/cond
  59.7 8.6 %collective-permute-start.14 = (f32[2,22,16,128]{3,2,1,0:T(8,128)S(1)}, f32[2,22,16,128]{3,2,1,0:T(8,128)S(1)}, u32[]{:S(2)}, u32[]{:S(2)}) collective-permute-start(f32[2,22,16,128]{3,2,1,0:T(8,128)S(1)} %get-tuple-element.94), channel_id=1, source_target_pairs={{0,1},{1,0},{2,3},{3,2},{4,5},{5,4},{6,7},{7,6},{8,9},{9,8},{10,11... | collective-permute-start | bytes 1081352 | tf_op jit(solution)/shard_map/cond/branch_2_fun/ppermute | solution.py:262
  59.8 12.3 %copy-start.13 = (f32[3,32,16,128]{3,2,1,0:T(8,128)S(1)}, f32[3,32,16,128]{3,2,1,0:T(8,128)}, u32[]{:S(2)}) copy-start(f32[3,32,16,128]{3,2,1,0:T(8,128)} %get-tuple-element.92.coef) | copy-start | bytes 2359300 | tf_op jit(solution)/shard_map/cond
  59.8 12.3 %collective-permute-start.15 = (f32[2,22,16,128]{3,2,1,0:T(8,128)S(1)}, f32[2,22,16,128]{3,2,1,0:T(8,128)S(1)}, u32[]{:S(2)}, u32[]{:S(2)}) collective-permute-start(f32[2,22,16,128]{3,2,1,0:T(8,128)S(1)} %get-tuple-element.95), channel_id=1, source_target_pairs={{0,15},{1,2},{2,1},{3,4},{4,3},{5,6},{6,5},{7,8},{8,7},{9,10},{10,... | collective-permute-start | bytes 1081352 | tf_op jit(solution)/shard_map/cond/branch_2_fun/ppermute | solution.py:263
  63.1 13.0 %collective-permute-start.12 = (f32[2,22,16,128]{3,2,1,0:T(8,128)S(1)}, f32[2,22,16,128]{3,2,1,0:T(8,128)S(1)}, u32[]{:S(2)}, u32[]{:S(2)}) collective-permute-start(f32[2,22,16,128]{3,2,1,0:T(8,128)S(1)} %get-tuple-element.90), channel_id=1, source_target_pairs={{0,1},{1,0},{2,3},{3,2},{4,5},{5,4},{6,7},{7,6},{8,9},{9,8},{10,11... | collective-permute-start | bytes 1081352 | tf_op jit(solution)/shard_map/cond/branch_2_fun/ppermute | solution.py:262
  63.2 16.6 %collective-permute-start.13 = (f32[2,22,16,128]{3,2,1,0:T(8,128)S(1)}, f32[2,22,16,128]{3,2,1,0:T(8,128)S(1)}, u32[]{:S(2)}, u32[]{:S(2)}) collective-permute-start(f32[2,22,16,128]{3,2,1,0:T(8,128)S(1)} %get-tuple-element.91), channel_id=1, source_target_pairs={{0,15},{1,2},{2,1},{3,4},{4,3},{5,6},{6,5},{7,8},{8,7},{9,10},{10,... | collective-permute-start | bytes 1081352 | tf_op jit(solution)/shard_map/cond/branch_2_fun/ppermute | solution.py:263
